TPU v7x, 256 devices: a whole 4x4x8 slice. The times are simulated.
256 devices in a mesh: depth: 16 (over z, core), tx: 4 (over y), ty: 4 (over x).
Axes of the slice: x: 4, y: 4, z: 8, core: 2. Of those that a mesh axis runs over, the one named last changes fastest.
Arguments:
- field: float32 [256, 256, 512], P('depth', 'tx', 'ty'), may hold values from -6 to 6
- shear: int32 [6, 256, 2], P(None, 'depth'), may hold values from 0 to 7
- fraction: float32 [6, 256, 2], P(None, 'depth'), may hold values from 0.05 to 0.95
- absorb: float32 [6], replicated, may hold values from 0.004 to 0.012
- palette: float32 [3, 3], replicated, may hold values from -1 to 1
- order: int32 [6], replicated, may hold values from 0 to 1, as said below
Outputs:
- image: float32 [6, 4, 256, 512], P(None, None, 'tx', 'ty')
Inputs may be any that keep to these rules, and one draw needn't show every extreme that they name: `order`: both values occur among the 6 views.
All inputs are finite; a program needn't handle non-finite values.
Results may differ from a plain program's by a relative error of at most 0.0003.
Values sent between devices are 32-bit elements; how exact they have to be, the bound alone decides.
No kernel may reach another device: no remote copies, remote signals or barrier semaphores. Data moves between devices by JAX's collectives and lax.ppermute only.
A program may use at most 64 MiB of HBM per device.

v0:
```python
import jax
import jax.numpy as jnp
from jax import lax
from jax.sharding import PartitionSpec as P

VIEWS = 6
SPILL = 8


def shifted(value, axis, steps):
    count = lax.axis_size(axis)
    initial, last = (max(0, -steps), min(count, count - steps))
    return lax.ppermute(value, axis, [(source, source + steps) for source in range(initial, last)])


def prefix(part, axis, combine, identity, reverse):
    count = lax.axis_size(axis)
    place = lax.axis_index(axis)
    ahead = count - 1 - place if reverse else place
    gathered = lax.all_gather(part, axis)
    state = jnp.zeros_like(part) + jnp.asarray(identity, part.dtype)

    def one(hop, state):
        source = count - 1 - hop if reverse else hop
        return combine(state, lax.dynamic_index_in_dim(gathered, source, 0, False))

    return lax.fori_loop(0, ahead, one, state)


def shear_matrix(offset, weight, length):
    rows_idx = jnp.arange(length + SPILL, dtype=jnp.int32)[None, :, None]
    cols_idx = jnp.arange(length, dtype=jnp.int32)[None, None, :]
    distance = rows_idx - cols_idx
    nearer = jnp.where(distance == offset[:, None, None], (1.0 - weight)[:, None, None], 0.0)
    farther = jnp.where(distance == offset[:, None, None] + 1, weight[:, None, None], 0.0)
    return nearer + farther


def shear_strips(field, offsets, weights):
    rows_count = field.shape[1]
    cols_count = field.shape[2]
    mix_rows = shear_matrix(offsets[:, 0], weights[:, 0], rows_count)
    mix_cols = shear_matrix(offsets[:, 1], weights[:, 1], cols_count)
    partial_rows = jnp.einsum("kij,kjl->kil", mix_rows, field, precision=lax.Precision.HIGHEST)
    sheared = jnp.einsum(
        "kil,kml->kim", partial_rows, mix_cols[:, :cols_count, :], precision=lax.Precision.HIGHEST
    )
    strip_cols = jnp.einsum(
        "kil,kml->kmi", partial_rows, mix_cols[:, cols_count:, :], precision=lax.Precision.HIGHEST
    )
    arrived_cols = shifted(strip_cols, "ty", 1)
    sheared = sheared.at[:, :, :SPILL].add(jnp.swapaxes(arrived_cols, 1, 2))
    arrived_rows = shifted(sheared[:, rows_count:, :], "tx", 1)
    return sheared[:, :rows_count, :].at[:, :SPILL, :].add(arrived_rows)


def shade(tile, absorb_val, palette, flipped):
    squared = tile * tile
    opacity = absorb_val * squared / (1.0 + squared)
    passing = 1.0 - opacity
    onward = jnp.cumprod(passing, axis=0)
    backward = jnp.flip(jnp.cumprod(jnp.flip(passing, 0), axis=0), 0)
    neutral = jnp.ones_like(passing[:1])
    lit_onward = jnp.concatenate([neutral, onward[:-1]], 0)
    lit_backward = jnp.concatenate([backward[1:], neutral], 0)
    lit = jnp.where(flipped == 1, lit_backward, lit_onward)
    through = jnp.where(flipped == 1, backward[0], onward[-1])
    weighted = lit * opacity
    moment_zero = jnp.sum(weighted, 0)
    moment_one = jnp.sum(weighted * tile, 0)
    moment_two = jnp.sum(weighted * squared, 0)
    colour = (
        palette[:, 0, None, None] * moment_zero[None]
        + palette[:, 1, None, None] * moment_one[None]
        + palette[:, 2, None, None] * moment_two[None]
    )
    rgba = jnp.concatenate([colour, (1.0 - through)[None]], 0)
    return (rgba, through)


def multiply(earlier, later):
    return earlier * later


def combine_prefix(rgba, through, flipped):
    neutral = jnp.ones_like(through)
    light_low = prefix(jnp.where(flipped == 1, neutral, through), "depth", multiply, neutral, False)
    light_high = prefix(jnp.where(flipped == 1, through, neutral), "depth", multiply, neutral, True)
    return lax.psum((light_low * light_high)[None] * rgba, "depth")


def shards(field, shear, fraction, absorb, palette, order):
    images = []
    for view_idx in range(VIEWS):
        tile = shear_strips(field, shear[view_idx], fraction[view_idx])
        rgba, through = shade(tile, absorb[view_idx], palette, order[view_idx])
        images.append(combine_prefix(rgba, through, order[view_idx]))
    return jnp.stack(images, 0)


def solution(mesh):
    return jax.shard_map(
        shards,
        mesh=mesh,
        in_specs=(
            P("depth", "tx", "ty"),
            P(None, "depth", None),
            P(None, "depth", None),
            P(),
            P(),
            P(),
        ),
        out_specs=P(None, None, "tx", "ty"),
        check_vma=False,
    )
```

profile of v0, /device:TPU:1, one launch (start us, length us, event | category | flops | bytes accessed | tf_op | source)
XLA Modules:
  0.0 675.1 jit_solution(7082822011683564089)
XLA Ops:
  11.6 3.9 collective-permute-start
  18.0 3.1 collective-permute-start.2
  23.5 2.8 collective-permute-start.10
  35.7 3.1 fusion.10
  38.8 3.1 fusion.8
  44.3 3.1 fusion.6
  65.0 3.1 scatter-add.40
  68.9 3.4 collective-permute-start.1
  89.9 2.9 scatter-add.44
  98.8 3.1 scatter-add.46
  107.2 3.1 scatter-add.54
  112.3 3.2 collective-permute-start.3
  115.5 2.9 collective-permute-start.11
  154.8 25.0 %all_gather.48 = f32[16,64,128]{2,1,0:T(8,128)} all-gather(f32[1,64,128]{2,1,0:T(8,128)S(1)} %get-tuple-element.774), channel_id=1, replica_groups=mesh['depth'=16,'tx'=4,'ty'=4] {'depth'}, dimensions={0}, use_global_device_ids=true | all-gather | bytes 557056 | tf_op jit(solution)/shard_map/all_gather | solution.py:20
  180.5 26.9 %all_gather.49 = f32[16,64,128]{2,1,0:T(8,128)} all-gather(f32[1,64,128]{2,1,0:T(8,128)S(1)} %get-tuple-element.773), channel_id=1, replica_groups=mesh['depth'=16,'tx'=4,'ty'=4] {'depth'}, dimensions={0}, use_global_device_ids=true | all-gather | bytes 557056 | tf_op jit(solution)/shard_map/all_gather | solution.py:20
  207.4 10.7 %while.145 = (s32[]{:T(128)}, f32[64,128]{1,0:T(8,128)S(1)}, s32[]{:T(128)}, f32[16,64,128]{2,1,0:T(8,128)}, s32[]{:T(128)}, /*index=5*/s32[]{:T(128)}, s32[]{:T(128)}, s32[]{:T(128)}) while((s32[]{:T(128)}, f32[64,128]{1,0:T(8,128)S(1)}, s32[]{:T(128)}, f32[16,64,128]{2,1,0:T(8,128)}, s32[]{:T(128)}, /*index=5*/s32[]{:T(128)}, s32[]{:T(128)}, ...), condition=%wide.region_5.6_spmd, body=%wide.region_4.5_spmd.sunk | while | flops 8198 | bytes 98447 | solution.py:27
  250.7 17.9 %all_gather.50 = f32[16,64,128]{2,1,0:T(8,128)} all-gather(f32[1,64,128]{2,1,0:T(8,128)S(1)} %get-tuple-element.771), channel_id=1, replica_groups=mesh['depth'=16,'tx'=4,'ty'=4] {'depth'}, dimensions={0}, use_global_device_ids=true | all-gather | bytes 557056 | tf_op jit(solution)/shard_map/all_gather | solution.py:20
  269.4 28.9 %all_gather.51 = f32[16,64,128]{2,1,0:T(8,128)} all-gather(f32[1,64,128]{2,1,0:T(8,128)S(1)} %get-tuple-element.770), channel_id=1, replica_groups=mesh['depth'=16,'tx'=4,'ty'=4] {'depth'}, dimensions={0}, use_global_device_ids=true | all-gather | bytes 557056 | tf_op jit(solution)/shard_map/all_gather | solution.py:20
  298.3 10.7 %while.147 = (s32[]{:T(128)}, f32[64,128]{1,0:T(8,128)S(1)}, s32[]{:T(128)}, f32[16,64,128]{2,1,0:T(8,128)}, s32[]{:T(128)}, /*index=5*/s32[]{:T(128)}, s32[]{:T(128)}, s32[]{:T(128)}) while((s32[]{:T(128)}, f32[64,128]{1,0:T(8,128)S(1)}, s32[]{:T(128)}, f32[16,64,128]{2,1,0:T(8,128)}, s32[]{:T(128)}, /*index=5*/s32[]{:T(128)}, s32[]{:T(128)}, ...), condition=%wide.region_15.16_spmd, body=%wide.region_14.15_spmd.sunk | while | flops 8198 | bytes 98447 | solution.py:27
  310.4 17.9 %all_gather.52 = f32[16,64,128]{2,1,0:T(8,128)} all-gather(f32[1,64,128]{2,1,0:T(8,128)S(1)} %get-tuple-element.768), channel_id=1, replica_groups=mesh['depth'=16,'tx'=4,'ty'=4] {'depth'}, dimensions={0}, use_global_device_ids=true | all-gather | bytes 557056 | tf_op jit(solution)/shard_map/all_gather | solution.py:20
  329.0 28.9 %all_gather.53 = f32[16,64,128]{2,1,0:T(8,128)} all-gather(f32[1,64,128]{2,1,0:T(8,128)S(1)} %get-tuple-element.767), channel_id=1, replica_groups=mesh['depth'=16,'tx'=4,'ty'=4] {'depth'}, dimensions={0}, use_global_device_ids=true | all-gather | bytes 557056 | tf_op jit(solution)/shard_map/all_gather | solution.py:20
  357.9 10.7 %while.149 = (s32[]{:T(128)}, f32[64,128]{1,0:T(8,128)S(1)}, s32[]{:T(128)}, f32[16,64,128]{2,1,0:T(8,128)}, s32[]{:T(128)}, /*index=5*/s32[]{:T(128)}, s32[]{:T(128)}, s32[]{:T(128)}) while((s32[]{:T(128)}, f32[64,128]{1,0:T(8,128)S(1)}, s32[]{:T(128)}, f32[16,64,128]{2,1,0:T(8,128)}, s32[]{:T(128)}, /*index=5*/s32[]{:T(128)}, s32[]{:T(128)}, ...), condition=%wide.region_25.26_spmd, body=%wide.region_24.25_spmd.sunk | while | flops 8198 | bytes 98447 | solution.py:27
  370.0 17.9 %all_gather.54 = f32[16,64,128]{2,1,0:T(8,128)} all-gather(f32[1,64,128]{2,1,0:T(8,128)S(1)} %get-tuple-element.765), channel_id=1, replica_groups=mesh['depth'=16,'tx'=4,'ty'=4] {'depth'}, dimensions={0}, use_global_device_ids=true | all-gather | bytes 557056 | tf_op jit(solution)/shard_map/all_gather | solution.py:20
  388.7 28.9 %all_gather.55 = f32[16,64,128]{2,1,0:T(8,128)} all-gather(f32[1,64,128]{2,1,0:T(8,128)S(1)} %get-tuple-element.764), channel_id=1, replica_groups=mesh['depth'=16,'tx'=4,'ty'=4] {'depth'}, dimensions={0}, use_global_device_ids=true | all-gather | bytes 557056 | tf_op jit(solution)/shard_map/all_gather | solution.py:20
  417.6 10.7 %while.151 = (s32[]{:T(128)}, f32[64,128]{1,0:T(8,128)S(1)}, s32[]{:T(128)}, f32[16,64,128]{2,1,0:T(8,128)}, s32[]{:T(128)}, /*index=5*/s32[]{:T(128)}, s32[]{:T(128)}, s32[]{:T(128)}) while((s32[]{:T(128)}, f32[64,128]{1,0:T(8,128)S(1)}, s32[]{:T(128)}, f32[16,64,128]{2,1,0:T(8,128)}, s32[]{:T(128)}, /*index=5*/s32[]{:T(128)}, s32[]{:T(128)}, ...), condition=%wide.region_35.36_spmd, body=%wide.region_34.35_spmd.sunk | while | flops 8198 | bytes 98447 | solution.py:27
  429.7 17.9 %all_gather.56 = f32[16,64,128]{2,1,0:T(8,128)} all-gather(f32[1,64,128]{2,1,0:T(8,128)S(1)} %get-tuple-element.762), channel_id=1, replica_groups=mesh['depth'=16,'tx'=4,'ty'=4] {'depth'}, dimensions={0}, use_global_device_ids=true | all-gather | bytes 557056 | tf_op jit(solution)/shard_map/all_gather | solution.py:20
  448.3 28.9 %all_gather.57 = f32[16,64,128]{2,1,0:T(8,128)} all-gather(f32[1,64,128]{2,1,0:T(8,128)S(1)} %get-tuple-element.761), channel_id=1, replica_groups=mesh['depth'=16,'tx'=4,'ty'=4] {'depth'}, dimensions={0}, use_global_device_ids=true | all-gather | bytes 557056 | tf_op jit(solution)/shard_map/all_gather | solution.py:20
  477.3 10.7 %while.153 = (s32[]{:T(128)}, f32[64,128]{1,0:T(8,128)S(1)}, s32[]{:T(128)}, f32[16,64,128]{2,1,0:T(8,128)}, s32[]{:T(128)}, /*index=5*/s32[]{:T(128)}, s32[]{:T(128)}, s32[]{:T(128)}) while((s32[]{:T(128)}, f32[64,128]{1,0:T(8,128)S(1)}, s32[]{:T(128)}, f32[16,64,128]{2,1,0:T(8,128)}, s32[]{:T(128)}, /*index=5*/s32[]{:T(128)}, s32[]{:T(128)}, ...), condition=%wide.region_45.46_spmd, body=%wide.region_44.45_spmd.sunk | while | flops 8198 | bytes 98447 | solution.py:27
  489.4 17.9 %all_gather.58 = f32[16,64,128]{2,1,0:T(8,128)} all-gather(f32[1,64,128]{2,1,0:T(8,128)S(1)} %get-tuple-element.759), channel_id=1, replica_groups=mesh['depth'=16,'tx'=4,'ty'=4] {'depth'}, dimensions={0}, use_global_device_ids=true | all-gather | bytes 557056 | tf_op jit(solution)/shard_map/all_gather | solution.py:20
  508.0 28.9 %all_gather.59 = f32[16,64,128]{2,1,0:T(8,128)} all-gather(f32[1,64,128]{2,1,0:T(8,128)S(1)} %get-tuple-element.758), channel_id=1, replica_groups=mesh['depth'=16,'tx'=4,'ty'=4] {'depth'}, dimensions={0}, use_global_device_ids=true | all-gather | bytes 557056 | tf_op jit(solution)/shard_map/all_gather | solution.py:20
  536.9 10.7 %while.155 = (s32[]{:T(128)}, f32[64,128]{1,0:T(8,128)S(1)}, s32[]{:T(128)}, f32[16,64,128]{2,1,0:T(8,128)}, s32[]{:T(128)}, /*index=5*/s32[]{:T(128)}, s32[]{:T(128)}, s32[]{:T(128)}) while((s32[]{:T(128)}, f32[64,128]{1,0:T(8,128)S(1)}, s32[]{:T(128)}, f32[16,64,128]{2,1,0:T(8,128)}, s32[]{:T(128)}, /*index=5*/s32[]{:T(128)}, s32[]{:T(128)}, ...), condition=%wide.region_55.56_spmd, body=%wide.region_54.55_spmd.sunk | while | flops 8198 | bytes 98447 | solution.py:27
  559.8 103.2 %all-reduce.15.cloned.1.call-done = (f32[1,4,64,128]{3,2,1,0:T(8,128)}, f32[1,4,64,128]{3,2,1,0:T(8,128)}, f32[1,4,64,128]{3,2,1,0:T(8,128)}, f32[1,4,64,128]{3,...) async-done(((f32[1,4,64,128]{3,2,1,0:T(8,128)}, f32[1,4,64,128]{3,2,1,0:T(8,128)}, f32[1,4,64,128]{3,2,1,0:T(8,128)}, f32[1,4,64,128]{3,2,1,0:T(8,128)}, ...) | async-done | bytes 786448 | tf_op jit(solution)/shard_map/psum | solution.py:89
  (337 shorter events, 231.7 us)
Async XLA Ops:
  6.5 1.8 copy-start
  6.5 656.5 %all-reduce.15.cloned.1.call-start = ((), (), s32[]{:S(2)}) async-start(), calls=%async_computation | async-start | bytes 1572864 | tf_op jit(solution)/shard_map/psum | solution.py:89
  11.6 48.3 %collective-permute-start = (f32[16,8,72]{2,1,0:T(8,128)S(1)}, f32[16,8,72]{2,1,0:T(8,128)S(1)}, u32[]{:S(2)}, u32[]{:S(2)}) collective-permute-start(f32[16,8,72]{2,1,0:T(8,128)S(1)} %fusion.142), channel_id=1, source_target_pairs={{0,1},{1,2},{2,3},{4,5},{5,6},{6,7},{8,9},{9,10},{10,11},{12,13},{... | collective-permute-start | bytes 110600 | tf_op jit(solution)/shard_map/ppermute | solution.py:13
  18.0 51.0 %collective-permute-start.2 = (f32[16,8,72]{2,1,0:T(8,128)S(1)}, f32[16,8,72]{2,1,0:T(8,128)S(1)}, u32[]{:S(2)}, u32[]{:S(2)}) collective-permute-start(f32[16,8,72]{2,1,0:T(8,128)S(1)} %fusion.139), channel_id=1, source_target_pairs={{0,1},{1,2},{2,3},{4,5},{5,6},{6,7},{8,9},{9,10},{10,11},{12,13},{... | collective-permute-start | bytes 110600 | tf_op jit(solution)/shard_map/ppermute | solution.py:13
  23.5 52.0 %collective-permute-start.10 = (f32[16,8,72]{2,1,0:T(8,128)S(1)}, f32[16,8,72]{2,1,0:T(8,128)S(1)}, u32[]{:S(2)}, u32[]{:S(2)}) collective-permute-start(f32[16,8,72]{2,1,0:T(8,128)S(1)} %fusion.127), channel_id=1, source_target_pairs={{0,1},{1,2},{2,3},{4,5},{5,6},{6,7},{8,9},{9,10},{10,11},{12,13},{... | collective-permute-start | bytes 110600 | tf_op jit(solution)/shard_map/ppermute | solution.py:13
  29.2 49.3 %collective-permute-start.4 = (f32[16,8,72]{2,1,0:T(8,128)S(1)}, f32[16,8,72]{2,1,0:T(8,128)S(1)}, u32[]{:S(2)}, u32[]{:S(2)}) collective-permute-start(f32[16,8,72]{2,1,0:T(8,128)S(1)} %fusion.136), channel_id=1, source_target_pairs={{0,1},{1,2},{2,3},{4,5},{5,6},{6,7},{8,9},{9,10},{10,11},{12,13},{... | collective-permute-start | bytes 110600 | tf_op jit(solution)/shard_map/ppermute | solution.py:13
  33.6 48.2 %collective-permute-start.6 = (f32[16,8,72]{2,1,0:T(8,128)S(1)}, f32[16,8,72]{2,1,0:T(8,128)S(1)}, u32[]{:S(2)}, u32[]{:S(2)}) collective-permute-start(f32[16,8,72]{2,1,0:T(8,128)S(1)} %fusion.133), channel_id=1, source_target_pairs={{0,1},{1,2},{2,3},{4,5},{5,6},{6,7},{8,9},{9,10},{10,11},{12,13},{... | collective-permute-start | bytes 110600 | tf_op jit(solution)/shard_map/ppermute | solution.py:13
  51.1 3.4 copy-start.28
  51.1 4.0 copy-start.29
  51.1 4.7 copy-start.30
  53.5 32.5 %copy-start.5 = (f32[16,72,128]{2,1,0:T(8,128)}, f32[16,72,128]{2,1,0:T(8,128)S(1)}, u32[]{:S(2)}) copy-start(f32[16,72,128]{2,1,0:T(8,128)S(1)} %fusion.2) | copy-start | bytes 1769476
  59.9 25.0 %collective-permute-start.8 = (f32[16,8,72]{2,1,0:T(8,128)S(1)}, f32[16,8,72]{2,1,0:T(8,128)S(1)}, u32[]{:S(2)}, u32[]{:S(2)}) collective-permute-start(f32[16,8,72]{2,1,0:T(8,128)S(1)} %fusion.130), channel_id=1, source_target_pairs={{0,1},{1,2},{2,3},{4,5},{5,6},{6,7},{8,9},{9,10},{10,11},{12,13},{... | collective-permute-start | bytes 110600 | tf_op jit(solution)/shard_map/ppermute | solution.py:13
  68.9 53.4 %collective-permute-start.1 = (f32[16,8,128]{2,1,0:T(8,128)S(1)}, f32[16,8,128]{2,1,0:T(8,128)S(1)}, u32[]{:S(2)}, u32[]{:S(2)}) collective-permute-start(f32[16,8,128]{2,1,0:T(8,128)S(1)} %slice.758), channel_id=1, source_target_pairs={{0,4},{4,8},{8,12},{1,5},{5,9},{9,13},{2,6},{6,10},{10,14},{3,7},{... | collective-permute-start | bytes 196616 | tf_op jit(solution)/shard_map/ppermute | solution.py:13
  87.9 2.0 copy-start.6
  110.3 2.0 copy-start.26
  110.3 13.9 %copy-start.1 = (f32[16,64,128]{2,1,0:T(8,128)S(1)}, f32[16,64,128]{2,1,0:T(8,128)}, u32[]{:S(2)}) copy-start(f32[16,64,128]{2,1,0:T(8,128)} %slice.756) | copy-start | bytes 1572868
  112.3 15.7 %collective-permute-start.3 = (f32[16,8,128]{2,1,0:T(8,128)S(1)}, f32[16,8,128]{2,1,0:T(8,128)S(1)}, u32[]{:S(2)}, u32[]{:S(2)}) collective-permute-start(f32[16,8,128]{2,1,0:T(8,128)S(1)} %copy-done.26), channel_id=1, source_target_pairs={{0,4},{4,8},{8,12},{1,5},{5,9},{9,13},{2,6},{6,10},{10,14},{3,7},{... | collective-permute-start | bytes 196616 | tf_op jit(solution)/shard_map/ppermute | solution.py:13
  115.5 16.4 %collective-permute-start.11 = (f32[16,8,128]{2,1,0:T(8,128)S(1)}, f32[16,8,128]{2,1,0:T(8,128)S(1)}, u32[]{:S(2)}, u32[]{:S(2)}) collective-permute-start(f32[16,8,128]{2,1,0:T(8,128)S(1)} %slice.808), channel_id=1, source_target_pairs={{0,4},{4,8},{8,12},{1,5},{5,9},{9,13},{2,6},{6,10},{10,14},{3,7},{... | collective-permute-start | bytes 196616 | tf_op jit(solution)/shard_map/ppermute | solution.py:13
  118.5 17.4 %collective-permute-start.5 = (f32[16,8,128]{2,1,0:T(8,128)S(1)}, f32[16,8,128]{2,1,0:T(8,128)S(1)}, u32[]{:S(2)}, u32[]{:S(2)}) collective-permute-start(f32[16,8,128]{2,1,0:T(8,128)S(1)} %slice.778), channel_id=1, source_target_pairs={{0,4},{4,8},{8,12},{1,5},{5,9},{9,13},{2,6},{6,10},{10,14},{3,7},{... | collective-permute-start | bytes 196616 | tf_op jit(solution)/shard_map/ppermute | solution.py:13
  120.4 19.4 %collective-permute-start.7 = (f32[16,8,128]{2,1,0:T(8,128)S(1)}, f32[16,8,128]{2,1,0:T(8,128)S(1)}, u32[]{:S(2)}, u32[]{:S(2)}) collective-permute-start(f32[16,8,128]{2,1,0:T(8,128)S(1)} %slice.788), channel_id=1, source_target_pairs={{0,4},{4,8},{8,12},{1,5},{5,9},{9,13},{2,6},{6,10},{10,14},{3,7},{... | collective-permute-start | bytes 196616 | tf_op jit(solution)/shard_map/ppermute | solution.py:13
  122.3 21.4 %collective-permute-start.9 = (f32[16,8,128]{2,1,0:T(8,128)S(1)}, f32[16,8,128]{2,1,0:T(8,128)S(1)}, u32[]{:S(2)}, u32[]{:S(2)}) collective-permute-start(f32[16,8,128]{2,1,0:T(8,128)S(1)} %slice.798), channel_id=1, source_target_pairs={{0,4},{4,8},{8,12},{1,5},{5,9},{9,13},{2,6},{6,10},{10,14},{3,7},{... | collective-permute-start | bytes 196616 | tf_op jit(solution)/shard_map/ppermute | solution.py:13
  125.1 3.8 copy-start.2
  149.5 1.2 copy-start.12
  221.1 1.2 copy-start.10
  547.6 2.3 slice-start
  547.6 2.3 copy-start.17
  555.4 1.7 copy-start.20
  555.4 2.3 copy-start.21
  555.6 2.9 copy-start.22
  556.3 2.9 copy-start.23
  663.0 3.7 copy-start.25
  663.0 4.6 copy-start.24
  (17 other events, 16.7 us)
Sparse Core Ops, SparseCore 0:
  559.9 103.0 all-reduce.14
where the time goes:
time: 685 us; the launch traced here: 675 us
  blocking collectives  286 us (42%)
  other arithmetic  130 us (19%)
  waiting for transfers between devices  103 us (15%)
  local copies, waits for them, and re-layouts  76.1 us (11%)
  starting transfers between devices  31.1 us (5%)
  matrix products  30.9 us (5%)
  between operations  18 us (3%)
    all_gather x12, blocking collectives, prefix(): gathered = lax.all_gather(part, axis)  286 us
    psum x1, waiting for transfers between devices, combine_prefix(): return lax.psum((light_low * light_high)[None] * rgba, 'depth')  103 us
    mul x90, other arithmetic, multiply(): return earlier * later  68.7 us
    ppermute x12, starting transfers between devices, shifted(): lax.ppermute(value, axis, [(source, source + steps) for source in range(i...  31.1 us
    scatter-add x6, local copies, waits for them, and re-layouts, shear_strips(): sheared = sheared.at[:, :, :SPILL].add(jnp.swapaxes(arrived_cols, 1, 2))  17.4 us
    dot_general x6, matrix products, shear_strips(): jnp.einsum('kil,kml->kim', partial_rows, mix_cols[:, :cols_count, :], pre...  16.3 us
    slice x12, local copies, waits for them, and re-layouts, shade(): lit_backward = jnp.concatenate([backward[1:], neutral], 0)  16.2 us
  transfers between devices with their start and end apart: 13, of which 1 were waited for; matrix products, arithmetic and copies ran while one was open for 14% of the time, Pallas kernels for 0%

commit v1 on v0

v1 whole, which is shorter than its diff:
```python
import jax
import jax.numpy as jnp
from jax import lax
from jax.experimental import pallas as pl
from jax.experimental.pallas import tpu as pltpu
from jax.sharding import PartitionSpec as P

VIEWS = 6
HALF = VIEWS // 2
SPILL = 8
LANES = 128


def vmem():
    return pl.BlockSpec(memory_space=pltpu.VMEM)


def smem():
    return pl.BlockSpec(memory_space=pltpu.SMEM)


def pack_kernel(field_ref, packed_ref):
    depth, rows, lanes = field_ref.shape
    lane = lax.broadcasted_iota(jnp.int32, (rows, lanes), 1)
    packed = jnp.zeros((rows, lanes), jnp.float32)
    for g in range(depth):
        moved = pltpu.roll(field_ref[g], (g * SPILL + SPILL) % lanes, 1)
        packed = jnp.where((lane >= g * SPILL) & (lane < (g + 1) * SPILL), moved, packed)
    packed_ref[...] = packed


def render_kernel(
    shear_ref, fraction_ref, absorb_ref, order_ref, field_ref, rows_ref, cols_ref, corner_ref,
    give_ref, keep_ref, shifted_ref,
):
    depth, rows, lanes = field_ref.shape
    core = lax.rem(lax.axis_index("depth"), 2)
    has_rows = lax.axis_index("tx") > 0
    has_cols = lax.axis_index("ty") > 0
    lane = lax.broadcasted_iota(jnp.int32, (rows + SPILL, lanes), 1)
    beside = jnp.concatenate(
        [jnp.where(has_rows, corner_ref[...], 0.0), cols_ref[...]], 0
    )
    beside = jnp.where(has_cols, beside, 0.0)

    def spread(g, carry):
        own = jnp.concatenate([jnp.where(has_rows, rows_ref[g], 0.0), field_ref[g]], 0)
        edge = pltpu.roll(beside, lanes - SPILL - g * SPILL, 1)
        shifted_ref[g, 0] = own
        for s in range(1, SPILL + 1):
            shifted_ref[g, s] = pltpu.roll(jnp.where(lane >= lanes - s, edge, own), s, 1)
        return carry

    lax.fori_loop(0, depth, spread, 0)

    def view(v, out_ref, k):
        absorb = absorb_ref[v]
        flipped = order_ref[v] == 1

        def one(i, carry):
            through, first, second = carry
            g = jnp.where(flipped, depth - 1 - i, i)
            o_row, o_col = shear_ref[v, g, 0], shear_ref[v, g, 1]
            f_row, f_col = fraction_ref[v, g, 0], fraction_ref[v, g, 1]
            near, far = SPILL - o_row, SPILL - 1 - o_row
            a = shifted_ref[g, o_col, pl.ds(near, rows), :]
            b = shifted_ref[g, o_col + 1, pl.ds(near, rows), :]
            c = shifted_ref[g, o_col, pl.ds(far, rows), :]
            d = shifted_ref[g, o_col + 1, pl.ds(far, rows), :]
            upper = (1.0 - f_col) * a + f_col * b
            lower = (1.0 - f_col) * c + f_col * d
            tile = (1.0 - f_row) * upper + f_row * lower
            squared = tile * tile
            opacity = absorb * squared / (1.0 + squared)
            weight = through * opacity
            return through - weight, first + weight * tile, second + weight * squared

        zero = jnp.zeros((rows, lanes), jnp.float32)
        through, first, second = lax.fori_loop(0, depth, one, (zero + 1.0, zero, zero))
        out_ref[k, 0] = through
        out_ref[k, 1] = first
        out_ref[k, 2] = second

    def give(k, carry):
        view((1 - core) * HALF + k, give_ref, k)
        return carry

    def keep(k, carry):
        view(core * HALF + k, keep_ref, k)
        return carry

    lax.fori_loop(0, HALF, give, 0)
    lax.fori_loop(0, HALF, keep, 0)


def over(mine, other, mine_first):
    first = mine_first[:, None, None]
    t_mine, t_other = mine[:, 0], other[:, 0]
    w_mine = jnp.where(first, 1.0, t_other)
    w_other = jnp.where(first, t_mine, 1.0)
    return jnp.stack(
        [
            t_mine * t_other,
            w_mine * mine[:, 1] + w_other * other[:, 1],
            w_mine * mine[:, 2] + w_other * other[:, 2],
        ],
        1,
    )


def along_z(partner):
    return [(2 * z + c, 2 * partner(z) + c) for z in range(8) for c in range(2)]


def split(value, upper):
    half = value.shape[2] // 2
    kept = lax.dynamic_slice_in_dim(value, upper * half, half, 2)
    sent = lax.dynamic_slice_in_dim(value, (1 - upper) * half, half, 2)
    return kept, sent


def join(mine, other, upper):
    return jnp.where(
        upper == 1, jnp.concatenate([other, mine], 2), jnp.concatenate([mine, other], 2)
    )


def shards(field, shear, fraction, absorb, palette, order):
    depth, rows, lanes = field.shape
    place = lax.axis_index("depth")
    core, z = place % 2, place // 2
    rank = jnp.where(z < 4, z, 7 - z)
    ring = [(i, (i + 1) % 4) for i in range(4)]
    diagonal = [(4 * i + j, (i + 1) % 4 * 4 + (j + 1) % 4) for i in range(4) for j in range(4)]

    packed = pl.pallas_call(
        pack_kernel,
        out_shape=jax.ShapeDtypeStruct((rows, lanes), jnp.float32),
        in_specs=[vmem()],
        out_specs=vmem(),
    )(field)
    row_halo = lax.ppermute(field[:, rows - SPILL:, :], "tx", ring)
    col_halo = lax.ppermute(packed, "ty", ring)
    corner = lax.ppermute(packed[rows - SPILL:], ("tx", "ty"), diagonal)

    part = jax.ShapeDtypeStruct((HALF, 3, rows, lanes), jnp.float32)
    give, keep = pl.pallas_call(
        render_kernel,
        out_shape=(part, part),
        in_specs=[smem()] * 4 + [vmem()] * 4,
        out_specs=(vmem(), vmem()),
        scratch_shapes=[pltpu.VMEM((depth, SPILL + 1, rows + SPILL, lanes), jnp.float32)],
    )(shear, fraction, absorb, order, field, row_halo, col_halo, corner)

    forward = lax.dynamic_slice_in_dim(order, core * HALF, HALF) == 0
    cores = [(i, i ^ 1) for i in range(16)]
    value = over(keep, lax.ppermute(give, "depth", cores), forward == (core == 0))

    near, second = along_z(lambda z: z ^ 1), along_z(lambda z: z ^ 2)
    mirror = along_z(lambda z: 7 - z)
    kept, sent = split(value, rank % 2)
    value = over(kept, lax.ppermute(sent, "depth", near), forward == (z % 2 == 0))
    kept, sent = split(value, rank // 2)
    value = over(kept, lax.ppermute(sent, "depth", second), forward == (z % 4 < 2))
    value = over(value, lax.ppermute(value, "depth", mirror), forward == (z < 4))
    value = join(value, lax.ppermute(value, "depth", second), rank // 2)
    value = join(value, lax.ppermute(value, "depth", near), rank % 2)
    other = lax.ppermute(value, "depth", cores)
    value = jnp.where(core == 1, jnp.concatenate([other, value], 0), jnp.concatenate([value, other], 0))

    alpha = 1.0 - value[:, 0]
    image = [
        palette[c, 0] * alpha + palette[c, 1] * value[:, 1] + palette[c, 2] * value[:, 2]
        for c in range(3)
    ]
    return jnp.stack(image + [alpha], 1)


def solution(mesh):
    return jax.shard_map(
        shards,
        mesh=mesh,
        in_specs=(
            P("depth", "tx", "ty"),
            P(None, "depth", None),
            P(None, "depth", None),
            P(),
            P(),
            P(),
        ),
        out_specs=P(None, None, "tx", "ty"),
        check_vma=False,
    )
```

time: 685 us -> 70.9 us (0.10); the launches traced: 675 us -> 70.4 us
  blocking collectives: 286 us -> 0 us
  other arithmetic: 130 us -> 8.36 us
  waiting for transfers between devices: 103 us -> 19.3 us
  local copies, waits for them, and re-layouts: 76.1 us -> 5.64 us
  matrix products: 30.9 us -> 0 us
  between operations: 18 us -> 0.1 us
  Pallas kernels: 0 us -> 12.3 us
    all_gather x12 -> x0, blocking collectives: 286 us -> none  [prefix(): gathered = lax.all_gather(part, axis)]
    psum x1 -> x0, waiting for transfers between devices: 103 us -> none  [combine_prefix(): return lax.psum((light_low * light_high)[None] * rgba, 'depth')]
    mul x96 -> x0, other arithmetic: 68.8 us -> none  [the longest x90 68.7 us: multiply(): return earlier * later]
    dot_general x18 -> x0, matrix products: 30.9 us -> none  [the longest x6 16.3 us: shear_strips(): jnp.einsum('kil,kml->kim', partial_rows, mix_cols[:, :cols_count, :], pre...]
    slice x38 -> x3, local copies, waits for them, and re-layouts: 28.3 us -> 2.24 us  [the longest x1 0.84 us: shards(): row_halo = lax.ppermute(field[:, rows - SPILL:, :], 'tx', ring)]
    ppermute x12 -> x10, waiting for transfers between devices: 0.03 us -> 19.3 us  [the longest x1 4.51 us: shards(): value = join(value, lax.ppermute(value, 'depth', near), rank % 2)]
    another operation x18 -> x5, other arithmetic: 19.8 us -> 0.98 us  [the longest x1 0.93 us: shards(): return jnp.stack(image + [alpha], 1)]
    scatter-add x6 -> x0, local copies, waits for them, and re-layouts: 17.4 us -> none  [shear_strips(): sheared = sheared.at[:, :, :SPILL].add(jnp.swapaxes(arrived_cols, 1, 2))]
  transfers between devices with their start and end apart: 13 -> 10, of which waited for: 1 -> 8; matrix products, arithmetic and copies ran while one was open for 14% -> 4% of each run, Pallas kernels for 0% -> 3%
where the time goes in v1:
time: 70.9 us; the launch traced here: 70.4 us
  starting transfers between devices  24.8 us (35%)
  waiting for transfers between devices  19.3 us (27%)
  Pallas kernels  12.3 us (17%)
  other arithmetic  8.36 us (12%)
  local copies, waits for them, and re-layouts  5.64 us (8%)
    pallas_call x1, Pallas kernels, shards(): pl.pallas_call(render_kernel, out_shape=(part, part), in_specs=[smem()] *...  10.4 us
    add x1, other arithmetic, shards(): palette[c, 0] * alpha + palette[c, 1] * value[:, 1]  5.87 us
    ppermute x1, starting transfers between devices, shards(): lax.ppermute(value, 'depth', mirror)  5.47 us
    ppermute x1, starting transfers between devices, shards(): other = lax.ppermute(value, 'depth', cores)  5.2 us
    ppermute x1, waiting for transfers between devices, shards(): value = join(value, lax.ppermute(value, 'depth', near), rank % 2)  4.51 us
    ppermute x1, waiting for transfers between devices, shards(): lax.ppermute(sent, 'depth', near)  3.75 us
    ppermute x1, waiting for transfers between devices, shards(): value = join(value, lax.ppermute(value, 'depth', second), rank // 2)  3.69 us
    unnamed x16, local copies, waits for them, and re-layouts  3.37 us
  transfers between devices with their start and end apart: 10, of which 8 were waited for; matrix products, arithmetic and copies ran while one was open for 4% of the time, Pallas kernels for 3%

profile of v1, /device:TPU:1, one launch (start us, length us, event | category | flops | bytes accessed | tf_op | source)
XLA Modules:
  0.0 70.4 jit_solution(8625837015367326752)
XLA Ops:
  0.0 0.8 %slice.110 = f32[16,8,128]{2,1,0:T(8,128)S(1)} slice(f32[16,64,128]{2,1,0:T(8,128)} %field_ref.3), slice={[0:16], [56:64], [0:128]} | slice | bytes 131072 | tf_op jit(solution)/shard_map/slice | solution.py:142
  0.8 2.1 %collective-permute-start = (f32[16,8,128]{2,1,0:T(8,128)S(1)}, f32[16,8,128]{2,1,0:T(8,128)S(1)}, u32[]{:S(2)}, u32[]{:S(2)}) collective-permute-start(f32[16,8,128]{2,1,0:T(8,128)S(1)} %slice.110), channel_id=1, source_target_pairs={{0,4},{4,8},{8,12},{12,0},{1,5},{5,9},{9,13},{13,1},{2,6},{6,10},{... | collective-permute-start | bytes 196616 | tf_op jit(solution)/shard_map/ppermute | solution.py:142
  3.0 1.8 %shard_map.64 = f32[64,128]{1,0:T(8,128)} custom-call(f32[16,64,128]{2,1,0:T(8,128)} %field_ref.3), custom_call_target="tpu_custom_call" | custom-call | tf_op jit(solution)/shard_map/pallas_call | solution.py:136
  4.8 1.2 %collective-permute-start.1 = (f32[64,128]{1,0:T(8,128)}, f32[64,128]{1,0:T(8,128)S(1)}, u32[]{:S(2)}, u32[]{:S(2)}) collective-permute-start(f32[64,128]{1,0:T(8,128)} %shard_map.64), channel_id=1, source_target_pairs={{0,1},{1,2},{2,3},{3,0},{4,5},{5,6},{6,7},{7,4},{8,9},{9,10},{10,1... | collective-permute-start | bytes 98312 | tf_op jit(solution)/shard_map/ppermute | solution.py:143
  6.0 0.7 %slice.144 = f32[8,128]{1,0:T(8,128)S(1)} slice(f32[64,128]{1,0:T(8,128)} %shard_map.64), slice={[56:64], [0:128]} | slice | bytes 8192 | tf_op jit(solution)/shard_map/slice | solution.py:144
  6.7 2.2 %collective-permute-start.2 = (f32[8,128]{1,0:T(8,128)S(1)}, f32[8,128]{1,0:T(8,128)S(1)}, u32[]{:S(2)}, u32[]{:S(2)}) collective-permute-start(f32[8,128]{1,0:T(8,128)S(1)} %slice.144), channel_id=1, source_target_pairs={{0,5},{1,6},{2,7},{3,4},{4,9},{5,10},{6,11},{7,8},{8,13},{9,14},{1... | collective-permute-start | bytes 12296 | tf_op jit(solution)/shard_map/ppermute | solution.py:144
  9.0 0.7 copy-done.3
  9.7 0.7 %copy.7.shear_ref = s32[6,16,2]{2,1,0:T(8,128)} copy(s32[6,16,2]{1,2,0:T(2,128)S(1)} %copy-done.3) | data formatting | bytes 1536 | tf_op args[1]
  10.4 0.7 %copy.8.fraction_ref = f32[6,16,2]{2,1,0:T(8,128)} copy(f32[6,16,2]{1,2,0:T(2,128)S(1)} %copy-done.4) | data formatting | bytes 1536 | tf_op args[2]
  11.1 1.4 %collective-permute-done.2.corner_ref = f32[8,128]{1,0:T(8,128)S(1)} collective-permute-done((f32[8,128]{1,0:T(8,128)S(1)}, f32[8,128]{1,0:T(8,128)S(1)}, u32[]{:S(2)}, u32[]{:S(2)}) %collective-permute-start.2) | collective-permute-done | bytes 4128 | tf_op jit(solution)/shard_map/ppermute | solution.py:144
  12.5 0.6 copy-done.5
  13.1 0.6 copy-done
  13.7 10.4 %shard_map.65 = (f32[3,3,64,128]{3,2,1,0:T(8,128)}, f32[3,3,64,128]{3,2,1,0:T(8,128)}) custom-call(s32[6,16,2]{2,1,0:T(8,128)} %copy.7.shear_ref, f32[6,16,2]{2,1,0:T(8,128)} %copy.8.fraction_ref, f32[6]{0:T(128)} %absorb_ref.1, s32[6]{0:T(128)} %order_ref.1, f32[16,64,128]{2,1,0:T(8,128)} %field_ref.3, f32[16,8,128]{2,1,0:T(8,128)} %copy-done, ...), custom_call_target="tpu_custom_call" | custom-call | tf_op jit(solution)/shard_map/pallas_call | solution.py:147
  24.2 2.4 %collective-permute-start.3 = (f32[3,3,64,128]{3,2,1,0:T(8,128)}, f32[3,3,64,128]{3,2,1,0:T(8,128)S(1)}, u32[]{:S(2)}, u32[]{:S(2)}) collective-permute-start(f32[3,3,64,128]{3,2,1,0:T(8,128)} %get-tuple-element.8), channel_id=1, source_target_pairs={{0,16},{16,0},{32,48},{48,32},{64,80},{80,64},{96,112},{112,96},{1... | collective-permute-start | bytes 884744 | tf_op jit(solution)/shard_map/ppermute | solution.py:157
  26.7 1.3 %collective-permute-done.3 = f32[3,3,64,128]{3,2,1,0:T(8,128)S(1)} collective-permute-done((f32[3,3,64,128]{3,2,1,0:T(8,128)}, f32[3,3,64,128]{3,2,1,0:T(8,128)S(1)}, u32[]{:S(2)}, u32[]{:S(2)}) %collective-permute-start.3) | collective-permute-done | bytes 294944 | tf_op jit(solution)/shard_map/ppermute | solution.py:157
  28.0 1.1 %fusion.1 = (f32[3,1,64,128]{3,2,1,0:T(8,128)S(1)}, f32[3,1,64,128]{3,2,1,0:T(8,128)S(1)}, f32[3,1,64,128]{3,2,1,0:T(8,128)S(1)}) fusion(f32[3,3,64,128]{3,2,1,0:T(8,128)S(1)} %collective-permute-done.3, f32[3,3,64,128]{3,2,1,0:T(8,128)} %get-tuple-element.7, pred[3]{0:T(512)(128)(4,1)S(1)} %get-tuple-element.38), kind=kLoop, calls=%fused_computation.13 | loop fusion | flops 221184 | bytes 884739 | tf_op jit(solution)/shard_map/add | solution.py:104
  29.2 1.7 %collective-permute-start.4 = (f32[3,3,32,128]{3,2,1,0:T(8,128)S(1)}, f32[3,3,32,128]{3,2,1,0:T(8,128)S(1)}, u32[]{:S(2)}, u32[]{:S(2)}) collective-permute-start(f32[3,3,32,128]{3,2,1,0:T(8,128)S(1)} %constant_dynamic-slice_fusion.1), channel_id=1, source_target_pairs={{0,32},{16,48},{32,0},{48,16},{64,96},{80,112},{96,64},{112,80},{1... | collective-permute-start | bytes 442376 | tf_op jit(solution)/shard_map/ppermute | solution.py:162
  30.9 3.8 %collective-permute-done.4 = f32[3,3,32,128]{3,2,1,0:T(8,128)S(1)} collective-permute-done((f32[3,3,32,128]{3,2,1,0:T(8,128)S(1)}, f32[3,3,32,128]{3,2,1,0:T(8,128)S(1)}, u32[]{:S(2)}, u32[]{:S(2)}) %collective-permute-start.4) | collective-permute-done | bytes 147488 | tf_op jit(solution)/shard_map/ppermute | solution.py:162
  34.6 0.1 fusion.3
  34.8 3.1 %collective-permute-start.5 = (f32[3,3,16,128]{3,2,1,0:T(8,128)S(1)}, f32[3,3,16,128]{3,2,1,0:T(8,128)S(1)}, u32[]{:S(2)}, u32[]{:S(2)}) collective-permute-start(f32[3,3,16,128]{3,2,1,0:T(8,128)S(1)} %constant_dynamic-slice_fusion), channel_id=1, source_target_pairs={{0,64},{16,80},{32,96},{48,112},{64,0},{80,16},{96,32},{112,48},{1... | collective-permute-start | bytes 221192 | tf_op jit(solution)/shard_map/ppermute | solution.py:164
  37.8 1.7 %collective-permute-done.5 = f32[3,3,16,128]{3,2,1,0:T(8,128)S(1)} collective-permute-done((f32[3,3,16,128]{3,2,1,0:T(8,128)S(1)}, f32[3,3,16,128]{3,2,1,0:T(8,128)S(1)}, u32[]{:S(2)}, u32[]{:S(2)}) %collective-permute-start.5) | collective-permute-done | bytes 73760 | tf_op jit(solution)/shard_map/ppermute | solution.py:164
  39.7 5.5 %collective-permute-start.6 = (f32[3,3,16,128]{3,2,1,0:T(8,128)S(1)}, f32[3,3,16,128]{3,2,1,0:T(8,128)S(1)}, u32[]{:S(2)}, u32[]{:S(2)}) collective-permute-start(f32[3,3,16,128]{3,2,1,0:T(8,128)S(1)} %pad_maximum_fusion.3), channel_id=1, source_target_pairs={{0,224},{16,240},{32,192},{48,208},{64,160},{80,176},{96,128},{112... | collective-permute-start | bytes 221192 | tf_op jit(solution)/shard_map/ppermute | solution.py:165
  45.1 2.3 %collective-permute-done.6 = f32[3,3,16,128]{3,2,1,0:T(8,128)S(1)} collective-permute-done((f32[3,3,16,128]{3,2,1,0:T(8,128)S(1)}, f32[3,3,16,128]{3,2,1,0:T(8,128)S(1)}, u32[]{:S(2)}, u32[]{:S(2)}) %collective-permute-start.6) | collective-permute-done | bytes 73760 | tf_op jit(solution)/shard_map/ppermute | solution.py:165
  47.5 1.3 %collective-permute-start.7 = (f32[3,3,16,128]{3,2,1,0:T(8,128)S(1)}, f32[3,3,16,128]{3,2,1,0:T(8,128)S(1)}, u32[]{:S(2)}, u32[]{:S(2)}) collective-permute-start(f32[3,3,16,128]{3,2,1,0:T(8,128)S(1)} %pad_maximum_fusion.4), channel_id=1, source_target_pairs={{0,64},{16,80},{32,96},{48,112},{64,0},{80,16},{96,32},{112,48},{1... | collective-permute-start | bytes 221192 | tf_op jit(solution)/shard_map/ppermute | solution.py:166
  48.8 3.7 %collective-permute-done.7 = f32[3,3,16,128]{3,2,1,0:T(8,128)S(1)} collective-permute-done((f32[3,3,16,128]{3,2,1,0:T(8,128)S(1)}, f32[3,3,16,128]{3,2,1,0:T(8,128)S(1)}, u32[]{:S(2)}, u32[]{:S(2)}) %collective-permute-start.7) | collective-permute-done | bytes 73760 | tf_op jit(solution)/shard_map/ppermute | solution.py:166
  52.5 0.1 collective-permute-start.8
  52.6 4.5 %collective-permute-done.8 = f32[3,3,32,128]{3,2,1,0:T(8,128)S(1)} collective-permute-done((f32[3,3,32,128]{3,2,1,0:T(8,128)S(1)}, f32[3,3,32,128]{3,2,1,0:T(8,128)S(1)}, u32[]{:S(2)}, u32[]{:S(2)}) %collective-permute-start.8) | collective-permute-done | bytes 147488 | tf_op jit(solution)/shard_map/ppermute | solution.py:167
  57.2 5.2 %collective-permute-start.9 = (f32[3,3,64,128]{3,2,1,0:T(8,128)S(1)}, f32[3,3,64,128]{3,2,1,0:T(8,128)S(1)}, u32[]{:S(2)}, u32[]{:S(2)}) collective-permute-start(f32[3,3,64,128]{3,2,1,0:T(8,128)S(1)} %maximum_select_fusion.1), channel_id=1, source_target_pairs={{0,16},{16,0},{32,48},{48,32},{64,80},{80,64},{96,112},{112,96},{1... | collective-permute-start | bytes 884744 | tf_op jit(solution)/shard_map/ppermute | solution.py:168
  62.4 0.7 fusion.8
  63.0 0.5 collective-permute-done.9
  63.6 5.9 %multiply_add_fusion.2 = (f32[6,1,64,128]{3,2,1,0:T(8,128)S(1)}, f32[6,1,64,128]{3,2,1,0:T(8,128)S(1)}, f32[6,1,64,128]{3,2,1,0:T(8,128)S(1)}, f32[6,1,64,128]{3,2,1,0:T(8,128)S(1)}) fusion(f32[6,3,64,128]{3,2,1,0:T(8,128)S(1)} %maximum_select_fusion, f32[]{:T(128)} %bitcast.2, f32[]{:T(128)} %bitcast.1, f32[]{:T(128)} %bitcast, f32[]{:T(128)} %bitcast.8, ...), kind=kLoop, calls=%fused_computation.7 | loop fusion | flops 786432 | bytes 1376292 | tf_op jit(solution)/shard_map/add | solution.py:173
  69.5 0.9 %pad_maximum_fusion = f32[6,4,64,128]{3,2,1,0:T(8,128)} fusion(f32[6,1,64,128]{3,2,1,0:T(8,128)S(1)} %get-tuple-element.16, f32[6,1,64,128]{3,2,1,0:T(8,128)S(1)} %get-tuple-element.14, f32[6,1,64,128]{3,2,1,0:T(8,128)S(1)} %get-tuple-element.15, f32[6,1,64,128]{3,2,1,0:T(8,128)S(1)} %get-tuple-element.13), kind=kLoop, calls=%fused_computation | loop fusion | flops 589824 | bytes 1572864 | tf_op jit(solution)/shard_map/stack | solution.py:176
  (26 shorter events, 0.5 us)
Async XLA Ops:
  0.8 11.7 %collective-permute-start = (f32[16,8,128]{2,1,0:T(8,128)S(1)}, f32[16,8,128]{2,1,0:T(8,128)S(1)}, u32[]{:S(2)}, u32[]{:S(2)}) collective-permute-start(f32[16,8,128]{2,1,0:T(8,128)S(1)} %slice.110), channel_id=1, source_target_pairs={{0,4},{4,8},{8,12},{12,0},{1,5},{5,9},{9,13},{13,1},{2,6},{6,10},{... | collective-permute-start | bytes 196616 | tf_op jit(solution)/shard_map/ppermute | solution.py:142
  4.8 7.7 %collective-permute-start.1 = (f32[64,128]{1,0:T(8,128)}, f32[64,128]{1,0:T(8,128)S(1)}, u32[]{:S(2)}, u32[]{:S(2)}) collective-permute-start(f32[64,128]{1,0:T(8,128)} %shard_map.64), channel_id=1, source_target_pairs={{0,1},{1,2},{2,3},{3,0},{4,5},{5,6},{6,7},{7,4},{8,9},{9,10},{10,1... | collective-permute-start | bytes 98312 | tf_op jit(solution)/shard_map/ppermute | solution.py:143
  6.7 5.8 %collective-permute-start.2 = (f32[8,128]{1,0:T(8,128)S(1)}, f32[8,128]{1,0:T(8,128)S(1)}, u32[]{:S(2)}, u32[]{:S(2)}) collective-permute-start(f32[8,128]{1,0:T(8,128)S(1)} %slice.144), channel_id=1, source_target_pairs={{0,5},{1,6},{2,7},{3,4},{4,9},{5,10},{6,11},{7,8},{8,13},{9,14},{1... | collective-permute-start | bytes 12296 | tf_op jit(solution)/shard_map/ppermute | solution.py:144
  9.0 0.7 copy-start.3
  9.7 0.7 %copy-start.4 = (f32[6,16,2]{1,2,0:T(2,128)S(1)}, f32[6,16,2]{1,2,0:T(2,128)}, u32[]{:S(2)}) copy-start(f32[6,16,2]{1,2,0:T(2,128)} %param.8) | copy-start | bytes 2308
  12.5 0.6 copy-start.5
  12.5 0.6 copy-start.1
  13.1 0.6 copy-start
  24.2 2.4 %copy-start.6 = (s32[6]{0:T(128)S(1)}, s32[6]{0:T(128)}, u32[]{:S(2)}) copy-start(s32[6]{0:T(128)} %order_ref.1) | copy-start | bytes 76
  24.2 3.8 %collective-permute-start.3 = (f32[3,3,64,128]{3,2,1,0:T(8,128)}, f32[3,3,64,128]{3,2,1,0:T(8,128)S(1)}, u32[]{:S(2)}, u32[]{:S(2)}) collective-permute-start(f32[3,3,64,128]{3,2,1,0:T(8,128)} %get-tuple-element.8), channel_id=1, source_target_pairs={{0,16},{16,0},{32,48},{48,32},{64,80},{80,64},{96,112},{112,96},{1... | collective-permute-start | bytes 884744 | tf_op jit(solution)/shard_map/ppermute | solution.py:157
  29.2 5.5 %collective-permute-start.4 = (f32[3,3,32,128]{3,2,1,0:T(8,128)S(1)}, f32[3,3,32,128]{3,2,1,0:T(8,128)S(1)}, u32[]{:S(2)}, u32[]{:S(2)}) collective-permute-start(f32[3,3,32,128]{3,2,1,0:T(8,128)S(1)} %constant_dynamic-slice_fusion.1), channel_id=1, source_target_pairs={{0,32},{16,48},{32,0},{48,16},{64,96},{80,112},{96,64},{112,80},{1... | collective-permute-start | bytes 442376 | tf_op jit(solution)/shard_map/ppermute | solution.py:162
  34.8 4.8 %collective-permute-start.5 = (f32[3,3,16,128]{3,2,1,0:T(8,128)S(1)}, f32[3,3,16,128]{3,2,1,0:T(8,128)S(1)}, u32[]{:S(2)}, u32[]{:S(2)}) collective-permute-start(f32[3,3,16,128]{3,2,1,0:T(8,128)S(1)} %constant_dynamic-slice_fusion), channel_id=1, source_target_pairs={{0,64},{16,80},{32,96},{48,112},{64,0},{80,16},{96,32},{112,48},{1... | collective-permute-start | bytes 221192 | tf_op jit(solution)/shard_map/ppermute | solution.py:164
  39.7 7.8 %collective-permute-start.6 = (f32[3,3,16,128]{3,2,1,0:T(8,128)S(1)}, f32[3,3,16,128]{3,2,1,0:T(8,128)S(1)}, u32[]{:S(2)}, u32[]{:S(2)}) collective-permute-start(f32[3,3,16,128]{3,2,1,0:T(8,128)S(1)} %pad_maximum_fusion.3), channel_id=1, source_target_pairs={{0,224},{16,240},{32,192},{48,208},{64,160},{80,176},{96,128},{112... | collective-permute-start | bytes 221192 | tf_op jit(solution)/shard_map/ppermute | solution.py:165
  47.5 5.0 %collective-permute-start.7 = (f32[3,3,16,128]{3,2,1,0:T(8,128)S(1)}, f32[3,3,16,128]{3,2,1,0:T(8,128)S(1)}, u32[]{:S(2)}, u32[]{:S(2)}) collective-permute-start(f32[3,3,16,128]{3,2,1,0:T(8,128)S(1)} %pad_maximum_fusion.4), channel_id=1, source_target_pairs={{0,64},{16,80},{32,96},{48,112},{64,0},{80,16},{96,32},{112,48},{1... | collective-permute-start | bytes 221192 | tf_op jit(solution)/shard_map/ppermute | solution.py:166
  52.5 4.6 %collective-permute-start.8 = (f32[3,3,32,128]{3,2,1,0:T(8,128)S(1)}, f32[3,3,32,128]{3,2,1,0:T(8,128)S(1)}, u32[]{:S(2)}, u32[]{:S(2)}) collective-permute-start(f32[3,3,32,128]{3,2,1,0:T(8,128)S(1)} %maximum_select_fusion.2), channel_id=1, source_target_pairs={{0,32},{16,48},{32,0},{48,16},{64,96},{80,112},{96,64},{112,80},{1... | collective-permute-start | bytes 442376 | tf_op jit(solution)/shard_map/ppermute | solution.py:167
  57.1 5.2 %copy-start.2 = (f32[3,3]{1,0:T(4,128)S(1)}, f32[3,3]{1,0:T(4,128)}, u32[]{:S(2)}) copy-start(f32[3,3]{1,0:T(4,128)} %param.10) | copy-start | bytes 112
  57.2 6.4 %collective-permute-start.9 = (f32[3,3,64,128]{3,2,1,0:T(8,128)S(1)}, f32[3,3,64,128]{3,2,1,0:T(8,128)S(1)}, u32[]{:S(2)}, u32[]{:S(2)}) collective-permute-start(f32[3,3,64,128]{3,2,1,0:T(8,128)S(1)} %maximum_select_fusion.1), channel_id=1, source_target_pairs={{0,16},{16,0},{32,48},{48,32},{64,80},{80,64},{96,112},{112,96},{1... | collective-permute-start | bytes 884744 | tf_op jit(solution)/shard_map/ppermute | solution.py:168

commit v2 on v1

v2 whole, which is shorter than its diff:
```python
import jax
import jax.numpy as jnp
from jax import lax
from jax.experimental import pallas as pl
from jax.experimental.pallas import tpu as pltpu
from jax.sharding import PartitionSpec as P

VIEWS = 6
HALF = VIEWS // 2
SPILL = 8
LANES = 128


def vmem():
    return pl.BlockSpec(memory_space=pltpu.VMEM)


def smem():
    return pl.BlockSpec(memory_space=pltpu.SMEM)


def pack_kernel(field_ref, rows_ref, packed_ref, corner_ref):
    depth, rows, lanes = field_ref.shape
    rows_ref[...] = field_ref[:, rows - SPILL:, :]
    lane = lax.broadcasted_iota(jnp.int32, (rows, lanes), 1)
    packed = jnp.zeros((rows, lanes), jnp.float32)
    for g in range(depth):
        moved = pltpu.roll(field_ref[g], (g * SPILL + SPILL) % lanes, 1)
        packed = jnp.where(lane >= g * SPILL, moved, packed)
    packed_ref[...] = packed
    corner_ref[...] = packed[rows - SPILL:]


def render_kernel(
    shear_ref, fraction_ref, absorb_ref, order_ref, field_ref, rows_ref, cols_ref, corner_ref,
    give_ref, keep_ref, whole_ref, step_ref, beside_ref, beside_step_ref, even_ref, odd_ref,
):
    depth, rows, lanes = field_ref.shape
    tall = rows + SPILL
    core = lax.rem(lax.axis_index("depth"), 2)
    has_rows = lax.axis_index("tx") > 0
    has_cols = lax.axis_index("ty") > 0
    lane = lax.broadcasted_iota(jnp.int32, (tall, lanes), 1)
    beside = jnp.concatenate([jnp.where(has_rows, corner_ref[...], 0.0), cols_ref[...]], 0)
    beside = jnp.where(has_cols, beside, 0.0)
    beside_ref[...] = beside
    beside_step_ref[...] = pltpu.roll(beside, 1, 1) - beside

    def prepare(g, carry):
        own = jnp.concatenate([jnp.where(has_rows, rows_ref[g], 0.0), field_ref[g]], 0)
        edge = pltpu.roll(beside, lanes - SPILL - g * SPILL + 1, 1)
        before = jnp.where(lane == 0, edge, pltpu.roll(own, 1, 1))
        whole_ref[g] = own
        step_ref[g] = before - own
        return carry

    lax.fori_loop(0, depth, prepare, 0)
    group = lax.broadcasted_iota(jnp.int32, (SPILL, lanes), 1) // SPILL

    def edge_of(v):
        weight = jnp.zeros((SPILL, lanes), jnp.float32)
        for g in range(depth):
            weight = jnp.where(group == g, fraction_ref[v, 1, g], weight)
        weight = jnp.concatenate([weight] * (tall // SPILL), 0)
        return beside_ref[...] + weight * beside_step_ref[...]

    def columns(v, g, edge_ref, out_ref):
        offset = shear_ref[v, 1, g]
        mixed = whole_ref[g] + fraction_ref[v, 1, g] * step_ref[g]
        mixed = pltpu.roll(mixed, offset, 1)
        edge = pltpu.roll(edge_ref[...], lanes - SPILL - g * SPILL + offset, 1)
        out_ref[g] = jnp.where(lane < offset, edge, mixed)

    def shade(v, flipped, i, carry, in_ref):
        through, first, second = carry
        g = jnp.where(flipped, depth - 1 - i, i)
        offset, weight = shear_ref[v, 0, g], fraction_ref[v, 0, g]
        near = in_ref[g, pl.ds(SPILL - offset, rows), :]
        far = in_ref[g, pl.ds(SPILL - 1 - offset, rows), :]
        tile = near + weight * (far - near)
        squared = tile * tile
        opacity = absorb_ref[v] * squared / (1.0 + squared)
        lost = through * opacity
        return through - lost, first + lost * tile, second + lost * squared

    def view_of(k):
        return (1 - core) * HALF + k if k < HALF else core * HALF + k - HALF

    def scoped(edge_ref):
        def first_view(g, carry):
            columns(view_of(0), g, edge_ref, even_ref)
            return carry

        edge_ref[...] = edge_of(view_of(0))
        lax.fori_loop(0, depth, first_view, 0)
        zero = jnp.zeros((rows, lanes), jnp.float32)
        for k in range(VIEWS):
            v = view_of(k)
            flipped = order_ref[v] == 1
            here, there = (even_ref, odd_ref) if k % 2 == 0 else (odd_ref, even_ref)
            if k + 1 < VIEWS:
                edge_ref[...] = edge_of(view_of(k + 1))

            def one(i, carry):
                carry = shade(v, flipped, i, carry, here)
                if k + 1 < VIEWS:
                    columns(view_of(k + 1), i, edge_ref, there)
                return carry

            through, first, second = lax.fori_loop(0, depth, one, (zero + 1.0, zero, zero))
            out_ref = give_ref if k < HALF else keep_ref
            out_ref[k % HALF, 0] = through
            out_ref[k % HALF, 1] = first
            out_ref[k % HALF, 2] = second

    pl.run_scoped(scoped, pltpu.VMEM((tall, lanes), jnp.float32))


def paint_kernel(palette_ref, mine_ref, other_ref, image_ref):
    core = lax.rem(lax.axis_index("depth"), 2)
    for part_ref, base in ((mine_ref, core * HALF), (other_ref, (1 - core) * HALF)):
        for k in range(HALF):
            alpha = 1.0 - part_ref[k, 0]
            first, second = part_ref[k, 1], part_ref[k, 2]
            for c in range(3):
                image_ref[base + k, c] = (
                    palette_ref[c, 0] * alpha + palette_ref[c, 1] * first + palette_ref[c, 2] * second
                )
            image_ref[base + k, 3] = alpha


def over(mine, other, mine_first):
    first = mine_first[:, None, None]
    t_mine, t_other = mine[:, 0], other[:, 0]
    w_mine = jnp.where(first, 1.0, t_other)
    w_other = jnp.where(first, t_mine, 1.0)
    return jnp.stack(
        [
            t_mine * t_other,
            w_mine * mine[:, 1] + w_other * other[:, 1],
            w_mine * mine[:, 2] + w_other * other[:, 2],
        ],
        1,
    )


def along_z(partner):
    return [(2 * z + c, 2 * partner(z) + c) for z in range(8) for c in range(2)]


def split(value, upper):
    half = value.shape[2] // 2
    kept = lax.dynamic_slice_in_dim(value, upper * half, half, 2)
    sent = lax.dynamic_slice_in_dim(value, (1 - upper) * half, half, 2)
    return kept, sent


def join(mine, other, upper):
    return jnp.where(
        upper == 1, jnp.concatenate([other, mine], 2), jnp.concatenate([mine, other], 2)
    )


def shards(field, shear, fraction, absorb, palette, order):
    depth, rows, lanes = field.shape
    place = lax.axis_index("depth")
    core, z = place % 2, place // 2
    rank = jnp.where(z < 4, z, (z % 4) ^ 2)
    ring = [(i, (i + 1) % 4) for i in range(4)]
    diagonal = [(4 * i + j, (i + 1) % 4 * 4 + (j + 1) % 4) for i in range(4) for j in range(4)]

    small = pltpu.CompilerParams(vmem_limit_bytes=4 << 20)
    row_halo, packed, corner = pl.pallas_call(
        pack_kernel,
        out_shape=(
            jax.ShapeDtypeStruct((depth, SPILL, lanes), jnp.float32),
            jax.ShapeDtypeStruct((rows, lanes), jnp.float32),
            jax.ShapeDtypeStruct((SPILL, lanes), jnp.float32),
        ),
        in_specs=[vmem()],
        out_specs=(vmem(), vmem(), vmem()),
        compiler_params=small,
    )(field)
    row_halo = lax.ppermute(row_halo, "tx", ring)
    col_halo = lax.ppermute(packed, "ty", ring)
    corner = lax.ppermute(corner, ("tx", "ty"), diagonal)

    part = jax.ShapeDtypeStruct((HALF, 3, rows, lanes), jnp.float32)
    slab = pltpu.VMEM((depth, rows + SPILL, lanes), jnp.float32)
    strip = pltpu.VMEM((rows + SPILL, lanes), jnp.float32)
    give, keep = pl.pallas_call(
        render_kernel,
        out_shape=(part, part),
        in_specs=[smem()] * 4 + [vmem()] * 4,
        out_specs=(vmem(), vmem()),
        scratch_shapes=[slab, slab, strip, strip, slab, slab],
        compiler_params=pltpu.CompilerParams(vmem_limit_bytes=8 << 20),
    )(
        jnp.transpose(shear, (0, 2, 1)), jnp.transpose(fraction, (0, 2, 1)), absorb, order,
        field, row_halo, col_halo, corner,
    )

    forward = lax.dynamic_slice_in_dim(order, core * HALF, HALF) == 0
    cores = [(i, i ^ 1) for i in range(16)]
    value = over(keep, lax.ppermute(give, "depth", cores), forward == (core == 0))

    near, second = along_z(lambda z: z ^ 1), along_z(lambda z: z ^ 2)
    third = along_z(lambda z: z ^ 6)
    kept, sent = split(value, rank % 2)
    value = over(kept, lax.ppermute(sent, "depth", near), forward == (z % 2 == 0))
    kept, sent = split(value, rank // 2)
    value = over(kept, lax.ppermute(sent, "depth", second), forward == (z % 4 < 2))
    value = over(value, lax.ppermute(value, "depth", third), forward == (z < 4))
    value = join(value, lax.ppermute(value, "depth", second), rank // 2)
    value = join(value, lax.ppermute(value, "depth", near), rank % 2)
    other = lax.ppermute(value, "depth", cores)
    return pl.pallas_call(
        paint_kernel,
        out_shape=jax.ShapeDtypeStruct((VIEWS, 4, rows, lanes), jnp.float32),
        in_specs=[smem(), vmem(), vmem()],
        out_specs=vmem(),
        compiler_params=small,
    )(palette, value, other)


def solution(mesh):
    return jax.shard_map(
        shards,
        mesh=mesh,
        in_specs=(
            P("depth", "tx", "ty"),
            P(None, "depth", None),
            P(None, "depth", None),
            P(),
            P(),
            P(),
        ),
        out_specs=P(None, None, "tx", "ty"),
        check_vma=False,
    )
```

time: 70.9 us -> 61.7 us (0.87)
  other arithmetic: 8.36 us -> 0.52 us
  local copies, waits for them, and re-layouts: 5.64 us -> 1.72 us
  starting transfers between devices: 24.8 us -> 27.4 us
  Pallas kernels: 12.3 us -> 13.3 us
  waiting for transfers between devices: 19.3 us -> 18.5 us
    add x1 -> x0, other arithmetic: 5.87 us -> none  [shards(): palette[c, 0] * alpha + palette[c, 1] * value[:, 1]]
    slice x3 -> x0, local copies, waits for them, and re-layouts: 2.24 us -> none  [the longest x1 0.84 us: shards(): row_halo = lax.ppermute(field[:, rows - SPILL:, :], 'tx', ring)]
    ppermute x1, waiting for transfers between devices: 3.69 us -> 1.84 us  [shards(): value = join(value, lax.ppermute(value, 'depth', second), rank // 2)]
    ppermute x3, waiting for transfers between devices: 3.7 us -> 5.54 us  [the longest x1 3.55 us: shards(): corner = lax.ppermute(corner, ('tx', 'ty'), diagonal)]
    unnamed x16 -> x14, local copies, waits for them, and re-layouts: 3.37 us -> 1.69 us
    ppermute x1, starting transfers between devices: 0.09 us -> 1.67 us  [shards(): value = join(value, lax.ppermute(value, 'depth', near), rank % 2)]
    ppermute x1, waiting for transfers between devices: 4.51 us -> 3.25 us  [shards(): value = join(value, lax.ppermute(value, 'depth', near), rank % 2)]
    ppermute x1, starting transfers between devices: 1.29 us -> 2.5 us  [shards(): value = join(value, lax.ppermute(value, 'depth', second), rank // 2)]
  transfers between devices with their start and end apart: 10 -> 10, of which waited for: 8 -> 8; matrix products, arithmetic and copies ran while one was open for 4% -> 0% of each run, Pallas kernels for 3% -> 0%
where the time goes in v2:
time: 61.7 us; the launch traced here: 61.5 us
  starting transfers between devices  27.4 us (44%)
  waiting for transfers between devices  18.5 us (30%)
  Pallas kernels  13.3 us (22%)
  local copies, waits for them, and re-layouts  1.72 us (3%)
    pallas_call x1, Pallas kernels, shards(): pl.pallas_call(render_kernel, out_shape=(part, part), in_specs=[smem()] *...  11.6 us
    ppermute x1, starting transfers between devices, shards(): value = over(value, lax.ppermute(value, 'depth', third), forward == (z < 4))  5.23 us
    ppermute x1, starting transfers between devices, shards(): other = lax.ppermute(value, 'depth', cores)  5.14 us
    ppermute x1, waiting for transfers between devices, shards(): lax.ppermute(sent, 'depth', near)  3.75 us
    ppermute x1, waiting for transfers between devices, shards(): corner = lax.ppermute(corner, ('tx', 'ty'), diagonal)  3.55 us
    ppermute x1, waiting for transfers between devices, shards(): value = join(value, lax.ppermute(value, 'depth', near), rank % 2)  3.25 us
    ppermute x1, starting transfers between devices, shards(): lax.ppermute(sent, 'depth', second)  3.07 us
    ppermute x1, starting transfers between devices, shards(): value = join(value, lax.ppermute(value, 'depth', second), rank // 2)  2.5 us
  transfers between devices with their start and end apart: 10, of which 8 were waited for; matrix products, arithmetic and copies ran while one was open for 0% of the time, Pallas kernels for 0%

profile of v2, /device:TPU:1, one launch (start us, length us, event | category | flops | bytes accessed | tf_op | source)
XLA Modules:
  0.0 61.5 jit_solution(9482666895869625923)
XLA Ops:
  0.0 1.0 %copy-done = f32[16,64,128]{2,1,0:T(8,128)S(1)} copy-done((f32[16,64,128]{2,1,0:T(8,128)S(1)}, f32[16,64,128]{2,1,0:T(8,128)}, u32[]{:S(2)}) %copy-start) | copy-done | bytes 524312
  1.0 0.2 shard_map.64
  1.2 2.2 %collective-permute-start = (f32[16,8,128]{2,1,0:T(8,128)S(1)}, f32[16,8,128]{2,1,0:T(8,128)S(1)}, u32[]{:S(2)}, u32[]{:S(2)}) collective-permute-start(f32[16,8,128]{2,1,0:T(8,128)S(1)} %get-tuple-element.10), channel_id=1, source_target_pairs={{0,4},{4,8},{8,12},{12,0},{1,5},{5,9},{9,13},{13,1},{2,6},{6,10},{... | collective-permute-start | bytes 196616 | tf_op jit(solution)/shard_map/ppermute | solution.py:184
  3.4 1.2 %collective-permute-start.1 = (f32[64,128]{1,0:T(8,128)S(1)}, f32[64,128]{1,0:T(8,128)S(1)}, u32[]{:S(2)}, u32[]{:S(2)}) collective-permute-start(f32[64,128]{1,0:T(8,128)S(1)} %get-tuple-element.11), channel_id=1, source_target_pairs={{0,1},{1,2},{2,3},{3,0},{4,5},{5,6},{6,7},{7,4},{8,9},{9,10},{10,1... | collective-permute-start | bytes 98312 | tf_op jit(solution)/shard_map/ppermute | solution.py:185
  4.6 2.2 %collective-permute-start.2 = (f32[8,128]{1,0:T(8,128)S(1)}, f32[8,128]{1,0:T(8,128)S(1)}, u32[]{:S(2)}, u32[]{:S(2)}) collective-permute-start(f32[8,128]{1,0:T(8,128)S(1)} %get-tuple-element.12), channel_id=1, source_target_pairs={{0,5},{1,6},{2,7},{3,4},{4,9},{5,10},{6,11},{7,8},{8,13},{9,14},{1... | collective-permute-start | bytes 12296 | tf_op jit(solution)/shard_map/ppermute | solution.py:186
  6.9 3.5 %collective-permute-done.2.corner_ref = f32[8,128]{1,0:T(8,128)S(1)} collective-permute-done((f32[8,128]{1,0:T(8,128)S(1)}, f32[8,128]{1,0:T(8,128)S(1)}, u32[]{:S(2)}, u32[]{:S(2)}) %collective-permute-start.2) | collective-permute-done | bytes 4128 | tf_op jit(solution)/shard_map/ppermute | solution.py:186
  10.4 0.0 collective-permute-done.1.cols_ref
  10.4 0.0 collective-permute-done.rows_ref
  10.4 0.0 copy-start.6
  10.5 0.6 copy-done.5
  11.1 0.0 copy-done.6
  11.1 11.6 %shard_map.65 = (f32[3,3,64,128]{3,2,1,0:T(8,128)S(1)}, f32[3,3,64,128]{3,2,1,0:T(8,128)S(1)}) custom-call(s32[6,2,16]{2,1,0:T(2,128)S(1)} %bitcast.2, f32[6,2,16]{2,1,0:T(2,128)S(1)} %bitcast.3, f32[6]{0:T(128)S(1)} %copy-done.6, s32[6]{0:T(128)S(1)} %copy-done.5, f32[16,64,128]{2,1,0:T(8,128)S(1)} %copy-done.1, ...), custom_call_target="tpu_custom_call" | custom-call | tf_op jit(solution)/shard_map/pallas_call | solution.py:191
  22.7 2.5 %collective-permute-start.3 = (f32[3,3,64,128]{3,2,1,0:T(8,128)S(1)}, f32[3,3,64,128]{3,2,1,0:T(8,128)S(1)}, u32[]{:S(2)}, u32[]{:S(2)}) collective-permute-start(f32[3,3,64,128]{3,2,1,0:T(8,128)S(1)} %get-tuple-element.14), channel_id=1, source_target_pairs={{0,16},{16,0},{32,48},{48,32},{64,80},{80,64},{96,112},{112,96},{1... | collective-permute-start | bytes 884744 | tf_op jit(solution)/shard_map/ppermute | solution.py:205
  25.1 0.1 broadcast_compare_fusion
  25.2 1.1 %collective-permute-done.3 = f32[3,3,64,128]{3,2,1,0:T(8,128)S(1)} collective-permute-done((f32[3,3,64,128]{3,2,1,0:T(8,128)S(1)}, f32[3,3,64,128]{3,2,1,0:T(8,128)S(1)}, u32[]{:S(2)}, u32[]{:S(2)}) %collective-permute-start.3) | collective-permute-done | bytes 294944 | tf_op jit(solution)/shard_map/ppermute | solution.py:205
  26.4 0.1 fusion.1
  26.5 1.7 %collective-permute-start.4 = (f32[3,3,32,128]{3,2,1,0:T(8,128)S(1)}, f32[3,3,32,128]{3,2,1,0:T(8,128)S(1)}, u32[]{:S(2)}, u32[]{:S(2)}) collective-permute-start(f32[3,3,32,128]{3,2,1,0:T(8,128)S(1)} %constant_dynamic-slice_fusion.1), channel_id=1, source_target_pairs={{0,32},{16,48},{32,0},{48,16},{64,96},{80,112},{96,64},{112,80},{1... | collective-permute-start | bytes 442376 | tf_op jit(solution)/shard_map/ppermute | solution.py:210
  28.2 3.8 %collective-permute-done.4 = f32[3,3,32,128]{3,2,1,0:T(8,128)S(1)} collective-permute-done((f32[3,3,32,128]{3,2,1,0:T(8,128)S(1)}, f32[3,3,32,128]{3,2,1,0:T(8,128)S(1)}, u32[]{:S(2)}, u32[]{:S(2)}) %collective-permute-start.4) | collective-permute-done | bytes 147488 | tf_op jit(solution)/shard_map/ppermute | solution.py:210
  32.0 0.1 fusion.3
  32.1 3.1 %collective-permute-start.5 = (f32[3,3,16,128]{3,2,1,0:T(8,128)S(1)}, f32[3,3,16,128]{3,2,1,0:T(8,128)S(1)}, u32[]{:S(2)}, u32[]{:S(2)}) collective-permute-start(f32[3,3,16,128]{3,2,1,0:T(8,128)S(1)} %constant_dynamic-slice_fusion), channel_id=1, source_target_pairs={{0,64},{16,80},{32,96},{48,112},{64,0},{80,16},{96,32},{112,48},{1... | collective-permute-start | bytes 221192 | tf_op jit(solution)/shard_map/ppermute | solution.py:212
  35.2 1.7 %collective-permute-done.5 = f32[3,3,16,128]{3,2,1,0:T(8,128)S(1)} collective-permute-done((f32[3,3,16,128]{3,2,1,0:T(8,128)S(1)}, f32[3,3,16,128]{3,2,1,0:T(8,128)S(1)}, u32[]{:S(2)}, u32[]{:S(2)}) %collective-permute-start.5) | collective-permute-done | bytes 73760 | tf_op jit(solution)/shard_map/ppermute | solution.py:212
  36.9 0.1 fusion.7
  37.0 5.2 %collective-permute-start.6 = (f32[3,3,16,128]{3,2,1,0:T(8,128)S(1)}, f32[3,3,16,128]{3,2,1,0:T(8,128)S(1)}, u32[]{:S(2)}, u32[]{:S(2)}) collective-permute-start(f32[3,3,16,128]{3,2,1,0:T(8,128)S(1)} %pad_maximum_fusion.2), channel_id=1, source_target_pairs={{0,192},{16,208},{32,224},{48,240},{64,128},{80,144},{96,160},{112... | collective-permute-start | bytes 221192 | tf_op jit(solution)/shard_map/ppermute | solution.py:213
  42.3 2.0 %collective-permute-done.6 = f32[3,3,16,128]{3,2,1,0:T(8,128)S(1)} collective-permute-done((f32[3,3,16,128]{3,2,1,0:T(8,128)S(1)}, f32[3,3,16,128]{3,2,1,0:T(8,128)S(1)}, u32[]{:S(2)}, u32[]{:S(2)}) %collective-permute-start.6) | collective-permute-done | bytes 73760 | tf_op jit(solution)/shard_map/ppermute | solution.py:213
  44.2 0.1 fusion.5
  44.3 2.5 %collective-permute-start.7 = (f32[3,3,16,128]{3,2,1,0:T(8,128)S(1)}, f32[3,3,16,128]{3,2,1,0:T(8,128)S(1)}, u32[]{:S(2)}, u32[]{:S(2)}) collective-permute-start(f32[3,3,16,128]{3,2,1,0:T(8,128)S(1)} %pad_maximum_fusion.3), channel_id=1, source_target_pairs={{0,64},{16,80},{32,96},{48,112},{64,0},{80,16},{96,32},{112,48},{1... | collective-permute-start | bytes 221192 | tf_op jit(solution)/shard_map/ppermute | solution.py:214
  46.8 1.8 %collective-permute-done.7 = f32[3,3,16,128]{3,2,1,0:T(8,128)S(1)} collective-permute-done((f32[3,3,16,128]{3,2,1,0:T(8,128)S(1)}, f32[3,3,16,128]{3,2,1,0:T(8,128)S(1)}, u32[]{:S(2)}, u32[]{:S(2)}) %collective-permute-start.7) | collective-permute-done | bytes 73760 | tf_op jit(solution)/shard_map/ppermute | solution.py:214
  48.7 1.7 %collective-permute-start.8 = (f32[3,3,32,128]{3,2,1,0:T(8,128)S(1)}, f32[3,3,32,128]{3,2,1,0:T(8,128)S(1)}, u32[]{:S(2)}, u32[]{:S(2)}) collective-permute-start(f32[3,3,32,128]{3,2,1,0:T(8,128)S(1)} %maximum_select_fusion.1), channel_id=1, source_target_pairs={{0,32},{16,48},{32,0},{48,16},{64,96},{80,112},{96,64},{112,80},{1... | collective-permute-start | bytes 442376 | tf_op jit(solution)/shard_map/ppermute | solution.py:215
  50.4 3.3 %collective-permute-done.8 = f32[3,3,32,128]{3,2,1,0:T(8,128)S(1)} collective-permute-done((f32[3,3,32,128]{3,2,1,0:T(8,128)S(1)}, f32[3,3,32,128]{3,2,1,0:T(8,128)S(1)}, u32[]{:S(2)}, u32[]{:S(2)}) %collective-permute-start.8) | collective-permute-done | bytes 147488 | tf_op jit(solution)/shard_map/ppermute | solution.py:215
  53.6 5.1 %collective-permute-start.9 = (f32[3,3,64,128]{3,2,1,0:T(8,128)S(1)}, f32[3,3,64,128]{3,2,1,0:T(8,128)S(1)}, u32[]{:S(2)}, u32[]{:S(2)}) collective-permute-start(f32[3,3,64,128]{3,2,1,0:T(8,128)S(1)} %maximum_select_fusion.mine_ref), channel_id=1, source_target_pairs={{0,16},{16,0},{32,48},{48,32},{64,80},{80,64},{96,112},{112,96},{1... | collective-permute-start | bytes 884744 | tf_op jit(solution)/shard_map/ppermute | solution.py:216
  58.8 1.2 %collective-permute-done.9.other_ref = f32[3,3,64,128]{3,2,1,0:T(8,128)S(1)} collective-permute-done((f32[3,3,64,128]{3,2,1,0:T(8,128)S(1)}, f32[3,3,64,128]{3,2,1,0:T(8,128)S(1)}, u32[]{:S(2)}, u32[]{:S(2)}) %collective-permute-start.9) | collective-permute-done | bytes 294944 | tf_op jit(solution)/shard_map/ppermute | solution.py:216
  60.0 1.6 %shard_map.66 = f32[6,4,64,128]{3,2,1,0:T(8,128)} custom-call(f32[3,3]{1,0:T(4,128)S(1)} %copy-done.4, f32[3,3,64,128]{3,2,1,0:T(8,128)S(1)} %maximum_select_fusion.mine_ref, f32[3,3,64,128]{3,2,1,0:T(8,128)S(1)} %collective-permute-done.9.other_ref), custom_call_target="tpu_custom_call" | custom-call | tf_op jit(solution)/shard_map/pallas_call | solution.py:217
  (19 shorter events, 0.1 us)
Async XLA Ops:
  0.0 1.0 %copy-start = (f32[16,64,128]{2,1,0:T(8,128)S(1)}, f32[16,64,128]{2,1,0:T(8,128)}, u32[]{:S(2)}) copy-start(f32[16,64,128]{2,1,0:T(8,128)} %field_ref.3) | copy-start | bytes 1572868
  1.0 9.4 %copy-start.1 = (f32[16,64,128]{2,1,0:T(8,128)S(1)}, f32[16,64,128]{2,1,0:T(8,128)}, u32[]{:S(2)}) copy-start(f32[16,64,128]{2,1,0:T(8,128)} %field_ref.3) | copy-start | bytes 1572868
  1.2 9.2 %collective-permute-start = (f32[16,8,128]{2,1,0:T(8,128)S(1)}, f32[16,8,128]{2,1,0:T(8,128)S(1)}, u32[]{:S(2)}, u32[]{:S(2)}) collective-permute-start(f32[16,8,128]{2,1,0:T(8,128)S(1)} %get-tuple-element.10), channel_id=1, source_target_pairs={{0,4},{4,8},{8,12},{12,0},{1,5},{5,9},{9,13},{13,1},{2,6},{6,10},{... | collective-permute-start | bytes 196616 | tf_op jit(solution)/shard_map/ppermute | solution.py:184
  3.4 7.0 %collective-permute-start.1 = (f32[64,128]{1,0:T(8,128)S(1)}, f32[64,128]{1,0:T(8,128)S(1)}, u32[]{:S(2)}, u32[]{:S(2)}) collective-permute-start(f32[64,128]{1,0:T(8,128)S(1)} %get-tuple-element.11), channel_id=1, source_target_pairs={{0,1},{1,2},{2,3},{3,0},{4,5},{5,6},{6,7},{7,4},{8,9},{9,10},{10,1... | collective-permute-start | bytes 98312 | tf_op jit(solution)/shard_map/ppermute | solution.py:185
  4.6 5.8 %collective-permute-start.2 = (f32[8,128]{1,0:T(8,128)S(1)}, f32[8,128]{1,0:T(8,128)S(1)}, u32[]{:S(2)}, u32[]{:S(2)}) collective-permute-start(f32[8,128]{1,0:T(8,128)S(1)} %get-tuple-element.12), channel_id=1, source_target_pairs={{0,5},{1,6},{2,7},{3,4},{4,9},{5,10},{6,11},{7,8},{8,13},{9,14},{1... | collective-permute-start | bytes 12296 | tf_op jit(solution)/shard_map/ppermute | solution.py:186
  6.9 3.6 %copy-start.3 = (f32[6,16,2]{1,2,0:T(2,128)S(1)}, f32[6,16,2]{1,2,0:T(2,128)}, u32[]{:S(2)}) copy-start(f32[6,16,2]{1,2,0:T(2,128)} %param.8) | copy-start | bytes 2308
  6.9 3.6 %copy-start.2 = (s32[6,16,2]{1,2,0:T(2,128)S(1)}, s32[6,16,2]{1,2,0:T(2,128)}, u32[]{:S(2)}) copy-start(s32[6,16,2]{1,2,0:T(2,128)} %param.7) | copy-start | bytes 2308
  10.4 0.7 %copy-start.5 = (s32[6]{0:T(128)S(1)}, s32[6]{0:T(128)}, u32[]{:S(2)}) copy-start(s32[6]{0:T(128)} %order_ref.1) | copy-start | bytes 76
  10.4 0.7 %copy-start.6 = (f32[6]{0:T(128)S(1)}, f32[6]{0:T(128)}, u32[]{:S(2)}) copy-start(f32[6]{0:T(128)} %absorb_ref.1) | copy-start | bytes 76
  22.7 3.7 %collective-permute-start.3 = (f32[3,3,64,128]{3,2,1,0:T(8,128)S(1)}, f32[3,3,64,128]{3,2,1,0:T(8,128)S(1)}, u32[]{:S(2)}, u32[]{:S(2)}) collective-permute-start(f32[3,3,64,128]{3,2,1,0:T(8,128)S(1)} %get-tuple-element.14), channel_id=1, source_target_pairs={{0,16},{16,0},{32,48},{48,32},{64,80},{80,64},{96,112},{112,96},{1... | collective-permute-start | bytes 884744 | tf_op jit(solution)/shard_map/ppermute | solution.py:205
  26.5 5.5 %collective-permute-start.4 = (f32[3,3,32,128]{3,2,1,0:T(8,128)S(1)}, f32[3,3,32,128]{3,2,1,0:T(8,128)S(1)}, u32[]{:S(2)}, u32[]{:S(2)}) collective-permute-start(f32[3,3,32,128]{3,2,1,0:T(8,128)S(1)} %constant_dynamic-slice_fusion.1), channel_id=1, source_target_pairs={{0,32},{16,48},{32,0},{48,16},{64,96},{80,112},{96,64},{112,80},{1... | collective-permute-start | bytes 442376 | tf_op jit(solution)/shard_map/ppermute | solution.py:210
  32.1 4.8 %collective-permute-start.5 = (f32[3,3,16,128]{3,2,1,0:T(8,128)S(1)}, f32[3,3,16,128]{3,2,1,0:T(8,128)S(1)}, u32[]{:S(2)}, u32[]{:S(2)}) collective-permute-start(f32[3,3,16,128]{3,2,1,0:T(8,128)S(1)} %constant_dynamic-slice_fusion), channel_id=1, source_target_pairs={{0,64},{16,80},{32,96},{48,112},{64,0},{80,16},{96,32},{112,48},{1... | collective-permute-start | bytes 221192 | tf_op jit(solution)/shard_map/ppermute | solution.py:212
  37.0 7.2 %collective-permute-start.6 = (f32[3,3,16,128]{3,2,1,0:T(8,128)S(1)}, f32[3,3,16,128]{3,2,1,0:T(8,128)S(1)}, u32[]{:S(2)}, u32[]{:S(2)}) collective-permute-start(f32[3,3,16,128]{3,2,1,0:T(8,128)S(1)} %pad_maximum_fusion.2), channel_id=1, source_target_pairs={{0,192},{16,208},{32,224},{48,240},{64,128},{80,144},{96,160},{112... | collective-permute-start | bytes 221192 | tf_op jit(solution)/shard_map/ppermute | solution.py:213
  44.3 4.3 %collective-permute-start.7 = (f32[3,3,16,128]{3,2,1,0:T(8,128)S(1)}, f32[3,3,16,128]{3,2,1,0:T(8,128)S(1)}, u32[]{:S(2)}, u32[]{:S(2)}) collective-permute-start(f32[3,3,16,128]{3,2,1,0:T(8,128)S(1)} %pad_maximum_fusion.3), channel_id=1, source_target_pairs={{0,64},{16,80},{32,96},{48,112},{64,0},{80,16},{96,32},{112,48},{1... | collective-permute-start | bytes 221192 | tf_op jit(solution)/shard_map/ppermute | solution.py:214
  48.7 4.9 %collective-permute-start.8 = (f32[3,3,32,128]{3,2,1,0:T(8,128)S(1)}, f32[3,3,32,128]{3,2,1,0:T(8,128)S(1)}, u32[]{:S(2)}, u32[]{:S(2)}) collective-permute-start(f32[3,3,32,128]{3,2,1,0:T(8,128)S(1)} %maximum_select_fusion.1), channel_id=1, source_target_pairs={{0,32},{16,48},{32,0},{48,16},{64,96},{80,112},{96,64},{112,80},{1... | collective-permute-start | bytes 442376 | tf_op jit(solution)/shard_map/ppermute | solution.py:215
  50.3 9.6 %copy-start.4 = (f32[3,3]{1,0:T(4,128)S(1)}, f32[3,3]{1,0:T(4,128)}, u32[]{:S(2)}) copy-start(f32[3,3]{1,0:T(4,128)} %palette_ref.1) | copy-start | bytes 112
  53.6 6.4 %collective-permute-start.9 = (f32[3,3,64,128]{3,2,1,0:T(8,128)S(1)}, f32[3,3,64,128]{3,2,1,0:T(8,128)S(1)}, u32[]{:S(2)}, u32[]{:S(2)}) collective-permute-start(f32[3,3,64,128]{3,2,1,0:T(8,128)S(1)} %maximum_select_fusion.mine_ref), channel_id=1, source_target_pairs={{0,16},{16,0},{32,48},{48,32},{64,80},{80,64},{96,112},{112,96},{1... | collective-permute-start | bytes 884744 | tf_op jit(solution)/shard_map/ppermute | solution.py:216

commit v3 on v2

--- a/solution.py
+++ b/solution.py
@@ -31,89 +31,84 @@
     corner_ref[...] = packed[rows - SPILL:]
 
 
-def render_kernel(
-    shear_ref, fraction_ref, absorb_ref, order_ref, field_ref, rows_ref, cols_ref, corner_ref,
-    give_ref, keep_ref, whole_ref, step_ref, beside_ref, beside_step_ref, even_ref, odd_ref,
-):
+def prepare(field_ref, rows_ref, cols_ref, corner_ref, table_ref):
     depth, rows, lanes = field_ref.shape
-    tall = rows + SPILL
-    core = lax.rem(lax.axis_index("depth"), 2)
     has_rows = lax.axis_index("tx") > 0
     has_cols = lax.axis_index("ty") > 0
-    lane = lax.broadcasted_iota(jnp.int32, (tall, lanes), 1)
+    last_lane = lax.broadcasted_iota(jnp.int32, (rows + SPILL, lanes), 1) == lanes - 1
     beside = jnp.concatenate([jnp.where(has_rows, corner_ref[...], 0.0), cols_ref[...]], 0)
     beside = jnp.where(has_cols, beside, 0.0)
-    beside_ref[...] = beside
-    beside_step_ref[...] = pltpu.roll(beside, 1, 1) - beside
-
-    def prepare(g, carry):
+    beside_step = pltpu.roll(beside, 1, 1) - beside
+
+    for g in range(depth):
         own = jnp.concatenate([jnp.where(has_rows, rows_ref[g], 0.0), field_ref[g]], 0)
-        edge = pltpu.roll(beside, lanes - SPILL - g * SPILL + 1, 1)
-        before = jnp.where(lane == 0, edge, pltpu.roll(own, 1, 1))
-        whole_ref[g] = own
-        step_ref[g] = before - own
+        turn = lanes - SPILL - g * SPILL
+        edge = pltpu.roll(beside, turn, 1)
+        before = pltpu.roll(jnp.where(last_lane, edge, own), 1, 1)
+        table_ref[0, g] = own
+        table_ref[1, g] = before - own
+        table_ref[2, g] = edge
+        table_ref[3, g] = pltpu.roll(beside_step, turn, 1)
+
+
+def render(shear_ref, fraction_ref, absorb_ref, order_ref, table_ref, out_ref, base, mixed_refs):
+    _, depth, tall, lanes = table_ref.shape
+    rows = tall - SPILL
+    lane = lax.broadcasted_iota(jnp.int32, (tall, lanes), 1)
+
+    def view(k, carry):
+        v = base + k
+        flipped = order_ref[v] == 1
+        absorb = absorb_ref[v]
+        through = jnp.ones((rows, lanes), jnp.float32)
+        first = second = jnp.zeros((rows, lanes), jnp.float32)
+
+        def columns(i):
+            g = jnp.where(flipped, depth - 1 - i, i)
+            offset, weight = shear_ref[v, 1, g], fraction_ref[v, 1, g]
+            outside = lane >= lanes - offset
+            own = jnp.where(outside, table_ref[2, g], table_ref[0, g])
+            step = jnp.where(outside, table_ref[3, g], table_ref[1, g])
+            mixed_refs[i % len(mixed_refs)][...] = pltpu.roll(own + weight * step, offset, 1)
+
+        def tile_of(i):
+            g = jnp.where(flipped, depth - 1 - i, i)
+            offset, weight = shear_ref[v, 0, g], fraction_ref[v, 0, g]
+            mixed_ref = mixed_refs[i % len(mixed_refs)]
+            near = mixed_ref[pl.ds(SPILL - offset, rows), :]
+            far = mixed_ref[pl.ds(SPILL - 1 - offset, rows), :]
+            return near + weight * (far - near)
+
+        columns(0)
+        for i in range(depth):
+            if i + 1 < depth:
+                columns(i + 1)
+            tile = tile_of(i)
+            squared = tile * tile
+            lost = through * (absorb * squared / (1.0 + squared))
+            through = through - lost
+            first = first + lost * tile
+            second = second + lost * squared
+        out_ref[k, 0] = through
+        out_ref[k, 1] = first
+        out_ref[k, 2] = second
         return carry
 
-    lax.fori_loop(0, depth, prepare, 0)
-    group = lax.broadcasted_iota(jnp.int32, (SPILL, lanes), 1) // SPILL
-
-    def edge_of(v):
-        weight = jnp.zeros((SPILL, lanes), jnp.float32)
-        for g in range(depth):
-            weight = jnp.where(group == g, fraction_ref[v, 1, g], weight)
-        weight = jnp.concatenate([weight] * (tall // SPILL), 0)
-        return beside_ref[...] + weight * beside_step_ref[...]
-
-    def columns(v, g, edge_ref, out_ref):
-        offset = shear_ref[v, 1, g]
-        mixed = whole_ref[g] + fraction_ref[v, 1, g] * step_ref[g]
-        mixed = pltpu.roll(mixed, offset, 1)
-        edge = pltpu.roll(edge_ref[...], lanes - SPILL - g * SPILL + offset, 1)
-        out_ref[g] = jnp.where(lane < offset, edge, mixed)
-
-    def shade(v, flipped, i, carry, in_ref):
-        through, first, second = carry
-        g = jnp.where(flipped, depth - 1 - i, i)
-        offset, weight = shear_ref[v, 0, g], fraction_ref[v, 0, g]
-        near = in_ref[g, pl.ds(SPILL - offset, rows), :]
-        far = in_ref[g, pl.ds(SPILL - 1 - offset, rows), :]
-        tile = near + weight * (far - near)
-        squared = tile * tile
-        opacity = absorb_ref[v] * squared / (1.0 + squared)
-        lost = through * opacity
-        return through - lost, first + lost * tile, second + lost * squared
-
-    def view_of(k):
-        return (1 - core) * HALF + k if k < HALF else core * HALF + k - HALF
-
-    def scoped(edge_ref):
-        def first_view(g, carry):
-            columns(view_of(0), g, edge_ref, even_ref)
-            return carry
-
-        edge_ref[...] = edge_of(view_of(0))
-        lax.fori_loop(0, depth, first_view, 0)
-        zero = jnp.zeros((rows, lanes), jnp.float32)
-        for k in range(VIEWS):
-            v = view_of(k)
-            flipped = order_ref[v] == 1
-            here, there = (even_ref, odd_ref) if k % 2 == 0 else (odd_ref, even_ref)
-            if k + 1 < VIEWS:
-                edge_ref[...] = edge_of(view_of(k + 1))
-
-            def one(i, carry):
-                carry = shade(v, flipped, i, carry, here)
-                if k + 1 < VIEWS:
-                    columns(view_of(k + 1), i, edge_ref, there)
-                return carry
-
-            through, first, second = lax.fori_loop(0, depth, one, (zero + 1.0, zero, zero))
-            out_ref = give_ref if k < HALF else keep_ref
-            out_ref[k % HALF, 0] = through
-            out_ref[k % HALF, 1] = first
-            out_ref[k % HALF, 2] = second
-
-    pl.run_scoped(scoped, pltpu.VMEM((tall, lanes), jnp.float32))
+    lax.fori_loop(0, HALF, view, 0)
+
+
+def give_kernel(
+    shear_ref, fraction_ref, absorb_ref, order_ref, field_ref, rows_ref, cols_ref, corner_ref,
+    out_ref, table_ref, *mixed_refs,
+):
+    prepare(field_ref, rows_ref, cols_ref, corner_ref, table_ref)
+    base = (1 - lax.rem(lax.axis_index("depth"), 2)) * HALF
+    render(shear_ref, fraction_ref, absorb_ref, order_ref, table_ref, out_ref, base, mixed_refs)
+
+
+def keep_kernel(shear_ref, fraction_ref, absorb_ref, order_ref, table_ref, out_ref, *mixed_refs):
+    base = lax.rem(lax.axis_index("depth"), 2) * HALF
+    render(shear_ref, fraction_ref, absorb_ref, order_ref, table_ref, out_ref, base, mixed_refs)
 
 
 def paint_kernel(palette_ref, mine_ref, other_ref, image_ref):
@@ -186,19 +181,24 @@
     corner = lax.ppermute(corner, ("tx", "ty"), diagonal)
 
     part = jax.ShapeDtypeStruct((HALF, 3, rows, lanes), jnp.float32)
-    slab = pltpu.VMEM((depth, rows + SPILL, lanes), jnp.float32)
-    strip = pltpu.VMEM((rows + SPILL, lanes), jnp.float32)
-    give, keep = pl.pallas_call(
-        render_kernel,
-        out_shape=(part, part),
+    tables = (jnp.transpose(shear, (0, 2, 1)), jnp.transpose(fraction, (0, 2, 1)), absorb, order)
+    scratch = [pltpu.VMEM((rows + SPILL, lanes), jnp.float32)] * 4
+    give, table = pl.pallas_call(
+        give_kernel,
+        out_shape=(part, jax.ShapeDtypeStruct((4, depth, rows + SPILL, lanes), jnp.float32)),
         in_specs=[smem()] * 4 + [vmem()] * 4,
         out_specs=(vmem(), vmem()),
-        scratch_shapes=[slab, slab, strip, strip, slab, slab],
-        compiler_params=pltpu.CompilerParams(vmem_limit_bytes=8 << 20),
-    )(
-        jnp.transpose(shear, (0, 2, 1)), jnp.transpose(fraction, (0, 2, 1)), absorb, order,
-        field, row_halo, col_halo, corner,
-    )
+        scratch_shapes=scratch,
+        compiler_params=small,
+    )(*tables, field, row_halo, col_halo, corner)
+    keep = pl.pallas_call(
+        keep_kernel,
+        out_shape=part,
+        in_specs=[smem()] * 4 + [vmem()],
+        out_specs=vmem(),
+        scratch_shapes=scratch,
+        compiler_params=small,
+    )(*tables, table)
 
     forward = lax.dynamic_slice_in_dim(order, core * HALF, HALF) == 0
     cores = [(i, i ^ 1) for i in range(16)]

time: 61.7 us -> 61.2 us (level)
  Pallas kernels: 13.3 us -> 6.94 us
  local copies, waits for them, and re-layouts: 1.72 us -> 7.5 us
  other arithmetic: 0.52 us -> 1.17 us
    pallas_call x1 -> x2, Pallas kernels: 11.6 us -> 5.19 us  [the longest x1 3.19 us: shards(): pl.pallas_call(give_kernel, out_shape=(part, jax.ShapeDtypeStruct((4, dep...]
    unnamed x14 -> x22, local copies, waits for them, and re-layouts: 1.69 us -> 7.47 us
    ppermute x1, waiting for transfers between devices: 1.12 us -> 0.01 us  [shards(): lax.ppermute(give, 'depth', cores)]
    eq x1, other arithmetic: 0.08 us -> 0.73 us  [shards(): value = over(value, lax.ppermute(value, 'depth', third), forward == (z < 4))]
  transfers between devices with their start and end apart: 10 -> 10, of which waited for: 8 -> 7; matrix products, arithmetic and copies ran while one was open for 0% -> 1% of each run, Pallas kernels for 0% -> 3%
where the time goes in v3:
time: 61.2 us; the launch traced here: 60.7 us
  starting transfers between devices  26.8 us (44%)
  waiting for transfers between devices  18.2 us (30%)
  local copies, waits for them, and re-layouts  7.5 us (12%)
  Pallas kernels  6.94 us (11%)
  other arithmetic  1.17 us (2%)
    unnamed x22, local copies, waits for them, and re-layouts  7.47 us
    ppermute x1, starting transfers between devices, shards(): value = over(value, lax.ppermute(value, 'depth', third), forward == (z < 4))  5.23 us
    ppermute x1, starting transfers between devices, shards(): other = lax.ppermute(value, 'depth', cores)  4.77 us
    ppermute x1, waiting for transfers between devices, shards(): lax.ppermute(sent, 'depth', near)  4.08 us
    ppermute x1, waiting for transfers between devices, shards(): corner = lax.ppermute(corner, ('tx', 'ty'), diagonal)  3.55 us
    pallas_call x1, Pallas kernels, shards(): pl.pallas_call(give_kernel, out_shape=(part, jax.ShapeDtypeStruct((4, dep...  3.19 us
    ppermute x1, waiting for transfers between devices, shards(): value = join(value, lax.ppermute(value, 'depth', near), rank % 2)  3.14 us
    ppermute x1, starting transfers between devices, shards(): lax.ppermute(sent, 'depth', second)  3.08 us
  transfers between devices with their start and end apart: 10, of which 7 were waited for; matrix products, arithmetic and copies ran while one was open for 1% of the time, Pallas kernels for 3%

profile of v3, /device:TPU:1, one launch (start us, length us, event | category | flops | bytes accessed | tf_op | source)
XLA Modules:
  0.0 60.7 jit_solution(15980852233895195253)
XLA Ops:
  0.0 1.0 %copy-done = f32[16,64,128]{2,1,0:T(8,128)S(1)} copy-done((f32[16,64,128]{2,1,0:T(8,128)S(1)}, f32[16,64,128]{2,1,0:T(8,128)}, u32[]{:S(2)}) %copy-start) | copy-done | bytes 524312
  1.0 0.2 shard_map.64
  1.2 2.2 %collective-permute-start = (f32[16,8,128]{2,1,0:T(8,128)S(1)}, f32[16,8,128]{2,1,0:T(8,128)S(1)}, u32[]{:S(2)}, u32[]{:S(2)}) collective-permute-start(f32[16,8,128]{2,1,0:T(8,128)S(1)} %get-tuple-element.10), channel_id=1, source_target_pairs={{0,4},{4,8},{8,12},{12,0},{1,5},{5,9},{9,13},{13,1},{2,6},{6,10},{... | collective-permute-start | bytes 196616 | tf_op jit(solution)/shard_map/ppermute | solution.py:179
  3.4 1.2 %collective-permute-start.1 = (f32[64,128]{1,0:T(8,128)S(1)}, f32[64,128]{1,0:T(8,128)S(1)}, u32[]{:S(2)}, u32[]{:S(2)}) collective-permute-start(f32[64,128]{1,0:T(8,128)S(1)} %get-tuple-element.11), channel_id=1, source_target_pairs={{0,1},{1,2},{2,3},{3,0},{4,5},{5,6},{6,7},{7,4},{8,9},{9,10},{10,1... | collective-permute-start | bytes 98312 | tf_op jit(solution)/shard_map/ppermute | solution.py:180
  4.6 2.2 %collective-permute-start.2 = (f32[8,128]{1,0:T(8,128)S(1)}, f32[8,128]{1,0:T(8,128)S(1)}, u32[]{:S(2)}, u32[]{:S(2)}) collective-permute-start(f32[8,128]{1,0:T(8,128)S(1)} %get-tuple-element.12), channel_id=1, source_target_pairs={{0,5},{1,6},{2,7},{3,4},{4,9},{5,10},{6,11},{7,8},{8,13},{9,14},{1... | collective-permute-start | bytes 12296 | tf_op jit(solution)/shard_map/ppermute | solution.py:181
  6.9 3.6 %collective-permute-done.2.corner_ref = f32[8,128]{1,0:T(8,128)S(1)} collective-permute-done((f32[8,128]{1,0:T(8,128)S(1)}, f32[8,128]{1,0:T(8,128)S(1)}, u32[]{:S(2)}, u32[]{:S(2)}) %collective-permute-start.2) | collective-permute-done | bytes 4128 | tf_op jit(solution)/shard_map/ppermute | solution.py:181
  10.4 1.0 %copy-done.1 = f32[16,64,128]{2,1,0:T(8,128)S(1)} copy-done((f32[16,64,128]{2,1,0:T(8,128)S(1)}, f32[16,64,128]{2,1,0:T(8,128)}, u32[]{:S(2)}) %copy-start.1) | copy-done | bytes 524312
  11.5 0.7 %copy-done.2 = s32[6,16,2]{1,2,0:T(2,128)S(1)} copy-done((s32[6,16,2]{1,2,0:T(2,128)S(1)}, s32[6,16,2]{1,2,0:T(2,128)}, u32[]{:S(2)}) %copy-start.2) | copy-done | bytes 792
  12.2 0.7 %copy-done.4 = f32[6,16,2]{1,2,0:T(2,128)S(1)} copy-done((f32[6,16,2]{1,2,0:T(2,128)S(1)}, f32[6,16,2]{1,2,0:T(2,128)}, u32[]{:S(2)}) %copy-start.4) | copy-done | bytes 792
  12.9 0.7 %copy-done.6 = s32[6]{0:T(128)S(1)} copy-done((s32[6]{0:T(128)S(1)}, s32[6]{0:T(128)}, u32[]{:S(2)}) %copy-start.6) | copy-done | bytes 48
  13.5 0.7 %copy-done.9 = f32[6]{0:T(128)S(1)} copy-done((f32[6]{0:T(128)S(1)}, f32[6]{0:T(128)}, u32[]{:S(2)}) %copy-start.9) | copy-done | bytes 48
  14.2 3.2 %shard_map.65 = (f32[3,3,64,128]{3,2,1,0:T(8,128)S(1)}, f32[4,16,72,128]{3,2,1,0:T(8,128)S(1)}) custom-call(s32[6,2,16]{2,1,0:T(2,128)S(1)} %bitcast.2, f32[6,2,16]{2,1,0:T(2,128)S(1)} %bitcast.4, f32[6]{0:T(128)S(1)} %copy-done.9, s32[6]{0:T(128)S(1)} %copy-done.6, f32[16,64,128]{2,1,0:T(8,128)S(1)} %copy-done.1, ...), custom_call_target="tpu_custom_call" | custom-call | tf_op jit(solution)/shard_map/pallas_call | solution.py:186
  17.4 2.5 %collective-permute-start.3 = (f32[3,3,64,128]{3,2,1,0:T(8,128)S(1)}, f32[3,3,64,128]{3,2,1,0:T(8,128)S(1)}, u32[]{:S(2)}, u32[]{:S(2)}) collective-permute-start(f32[3,3,64,128]{3,2,1,0:T(8,128)S(1)} %get-tuple-element.14), channel_id=1, source_target_pairs={{0,16},{16,0},{32,48},{48,32},{64,80},{80,64},{96,112},{112,96},{1... | collective-permute-start | bytes 884744 | tf_op jit(solution)/shard_map/ppermute | solution.py:205
  19.8 0.7 %broadcast_compare_fusion = (pred[3]{0:T(512)(128)(4,1)S(1)}, pred[3]{0:T(512)(128)(4,1)S(1)}) fusion(pred[]{:T(512)S(6)} %lt.44, s32[6]{0:T(128)} %order_ref.3, s32[]{:T(128)S(6)} %select_n.123), kind=kLoop, calls=%fused_computation.39 | loop fusion | flops 6 | bytes 23 | tf_op jit(solution)/shard_map/eq | solution.py:213
  20.6 0.7 %copy-done.3 = s32[6,16,2]{1,2,0:T(2,128)S(1)} copy-done((s32[6,16,2]{1,2,0:T(2,128)S(1)}, s32[6,16,2]{1,2,0:T(2,128)}, u32[]{:S(2)}) %copy-start.3) | copy-done | bytes 792
  21.3 0.7 %copy-done.5 = f32[6,16,2]{1,2,0:T(2,128)S(1)} copy-done((f32[6,16,2]{1,2,0:T(2,128)S(1)}, f32[6,16,2]{1,2,0:T(2,128)}, u32[]{:S(2)}) %copy-start.5) | copy-done | bytes 792
  22.0 0.7 %copy-done.7 = s32[6]{0:T(128)S(1)} copy-done((s32[6]{0:T(128)S(1)}, s32[6]{0:T(128)}, u32[]{:S(2)}) %copy-start.7) | copy-done | bytes 48
  22.6 0.7 %copy-done.10 = f32[6]{0:T(128)S(1)} copy-done((f32[6]{0:T(128)S(1)}, f32[6]{0:T(128)}, u32[]{:S(2)}) %copy-start.10) | copy-done | bytes 48
  23.3 2.0 %shard_map.66 = f32[3,3,64,128]{3,2,1,0:T(8,128)S(1)} custom-call(s32[6,2,16]{2,1,0:T(2,128)S(1)} %bitcast.3, f32[6,2,16]{2,1,0:T(2,128)S(1)} %bitcast.5, f32[6]{0:T(128)S(1)} %copy-done.10, s32[6]{0:T(128)S(1)} %copy-done.7, f32[4,16,72,128]{3,2,1,0:T(8,128)S(1)} %get-tuple-element.13.table_ref), custom_call_target="tpu_custom_call" | custom-call | tf_op jit(solution)/shard_map/pallas_call | solution.py:194
  25.5 1.7 %collective-permute-start.4 = (f32[3,3,32,128]{3,2,1,0:T(8,128)S(1)}, f32[3,3,32,128]{3,2,1,0:T(8,128)S(1)}, u32[]{:S(2)}, u32[]{:S(2)}) collective-permute-start(f32[3,3,32,128]{3,2,1,0:T(8,128)S(1)} %constant_dynamic-slice_fusion.1), channel_id=1, source_target_pairs={{0,32},{16,48},{32,0},{48,16},{64,96},{80,112},{96,64},{112,80},{1... | collective-permute-start | bytes 442376 | tf_op jit(solution)/shard_map/ppermute | solution.py:210
  27.2 4.1 %collective-permute-done.4 = f32[3,3,32,128]{3,2,1,0:T(8,128)S(1)} collective-permute-done((f32[3,3,32,128]{3,2,1,0:T(8,128)S(1)}, f32[3,3,32,128]{3,2,1,0:T(8,128)S(1)}, u32[]{:S(2)}, u32[]{:S(2)}) %collective-permute-start.4) | collective-permute-done | bytes 147488 | tf_op jit(solution)/shard_map/ppermute | solution.py:210
  31.4 3.1 %collective-permute-start.5 = (f32[3,3,16,128]{3,2,1,0:T(8,128)S(1)}, f32[3,3,16,128]{3,2,1,0:T(8,128)S(1)}, u32[]{:S(2)}, u32[]{:S(2)}) collective-permute-start(f32[3,3,16,128]{3,2,1,0:T(8,128)S(1)} %constant_dynamic-slice_fusion), channel_id=1, source_target_pairs={{0,64},{16,80},{32,96},{48,112},{64,0},{80,16},{96,32},{112,48},{1... | collective-permute-start | bytes 221192 | tf_op jit(solution)/shard_map/ppermute | solution.py:212
  34.5 1.7 %collective-permute-done.5 = f32[3,3,16,128]{3,2,1,0:T(8,128)S(1)} collective-permute-done((f32[3,3,16,128]{3,2,1,0:T(8,128)S(1)}, f32[3,3,16,128]{3,2,1,0:T(8,128)S(1)}, u32[]{:S(2)}, u32[]{:S(2)}) %collective-permute-start.5) | collective-permute-done | bytes 73760 | tf_op jit(solution)/shard_map/ppermute | solution.py:212
  36.3 5.2 %collective-permute-start.6 = (f32[3,3,16,128]{3,2,1,0:T(8,128)S(1)}, f32[3,3,16,128]{3,2,1,0:T(8,128)S(1)}, u32[]{:S(2)}, u32[]{:S(2)}) collective-permute-start(f32[3,3,16,128]{3,2,1,0:T(8,128)S(1)} %pad_maximum_fusion.2), channel_id=1, source_target_pairs={{0,192},{16,208},{32,224},{48,240},{64,128},{80,144},{96,160},{112... | collective-permute-start | bytes 221192 | tf_op jit(solution)/shard_map/ppermute | solution.py:213
  41.5 2.2 %collective-permute-done.6 = f32[3,3,16,128]{3,2,1,0:T(8,128)S(1)} collective-permute-done((f32[3,3,16,128]{3,2,1,0:T(8,128)S(1)}, f32[3,3,16,128]{3,2,1,0:T(8,128)S(1)}, u32[]{:S(2)}, u32[]{:S(2)}) %collective-permute-start.6) | collective-permute-done | bytes 73760 | tf_op jit(solution)/shard_map/ppermute | solution.py:213
  43.8 2.0 %collective-permute-start.7 = (f32[3,3,16,128]{3,2,1,0:T(8,128)S(1)}, f32[3,3,16,128]{3,2,1,0:T(8,128)S(1)}, u32[]{:S(2)}, u32[]{:S(2)}) collective-permute-start(f32[3,3,16,128]{3,2,1,0:T(8,128)S(1)} %pad_maximum_fusion.3), channel_id=1, source_target_pairs={{0,64},{16,80},{32,96},{48,112},{64,0},{80,16},{96,32},{112,48},{1... | collective-permute-start | bytes 221192 | tf_op jit(solution)/shard_map/ppermute | solution.py:214
  45.9 2.3 %collective-permute-done.7 = f32[3,3,16,128]{3,2,1,0:T(8,128)S(1)} collective-permute-done((f32[3,3,16,128]{3,2,1,0:T(8,128)S(1)}, f32[3,3,16,128]{3,2,1,0:T(8,128)S(1)}, u32[]{:S(2)}, u32[]{:S(2)}) %collective-permute-start.7) | collective-permute-done | bytes 73760 | tf_op jit(solution)/shard_map/ppermute | solution.py:214
  48.1 1.9 %collective-permute-start.8 = (f32[3,3,32,128]{3,2,1,0:T(8,128)S(1)}, f32[3,3,32,128]{3,2,1,0:T(8,128)S(1)}, u32[]{:S(2)}, u32[]{:S(2)}) collective-permute-start(f32[3,3,32,128]{3,2,1,0:T(8,128)S(1)} %maximum_select_fusion.1), channel_id=1, source_target_pairs={{0,32},{16,48},{32,0},{48,16},{64,96},{80,112},{96,64},{112,80},{1... | collective-permute-start | bytes 442376 | tf_op jit(solution)/shard_map/ppermute | solution.py:215
  50.0 3.1 %collective-permute-done.8 = f32[3,3,32,128]{3,2,1,0:T(8,128)S(1)} collective-permute-done((f32[3,3,32,128]{3,2,1,0:T(8,128)S(1)}, f32[3,3,32,128]{3,2,1,0:T(8,128)S(1)}, u32[]{:S(2)}, u32[]{:S(2)}) %collective-permute-start.8) | collective-permute-done | bytes 147488 | tf_op jit(solution)/shard_map/ppermute | solution.py:215
  53.2 4.8 %collective-permute-start.9 = (f32[3,3,64,128]{3,2,1,0:T(8,128)S(1)}, f32[3,3,64,128]{3,2,1,0:T(8,128)S(1)}, u32[]{:S(2)}, u32[]{:S(2)}) collective-permute-start(f32[3,3,64,128]{3,2,1,0:T(8,128)S(1)} %maximum_select_fusion.mine_ref), channel_id=1, source_target_pairs={{0,16},{16,0},{32,48},{48,32},{64,80},{80,64},{96,112},{112,96},{1... | collective-permute-start | bytes 884744 | tf_op jit(solution)/shard_map/ppermute | solution.py:216
  58.0 1.2 %collective-permute-done.9.other_ref = f32[3,3,64,128]{3,2,1,0:T(8,128)S(1)} collective-permute-done((f32[3,3,64,128]{3,2,1,0:T(8,128)S(1)}, f32[3,3,64,128]{3,2,1,0:T(8,128)S(1)}, u32[]{:S(2)}, u32[]{:S(2)}) %collective-permute-start.9) | collective-permute-done | bytes 294944 | tf_op jit(solution)/shard_map/ppermute | solution.py:216
  59.2 1.6 %shard_map.67 = f32[6,4,64,128]{3,2,1,0:T(8,128)} custom-call(f32[3,3]{1,0:T(4,128)S(1)} %copy-done.8, f32[3,3,64,128]{3,2,1,0:T(8,128)S(1)} %maximum_select_fusion.mine_ref, f32[3,3,64,128]{3,2,1,0:T(8,128)S(1)} %collective-permute-done.9.other_ref), custom_call_target="tpu_custom_call" | custom-call | tf_op jit(solution)/shard_map/pallas_call | solution.py:217
  (28 shorter events, 0.5 us)
Async XLA Ops:
  0.0 1.0 %copy-start = (f32[16,64,128]{2,1,0:T(8,128)S(1)}, f32[16,64,128]{2,1,0:T(8,128)}, u32[]{:S(2)}) copy-start(f32[16,64,128]{2,1,0:T(8,128)} %field_ref.3) | copy-start | bytes 1572868
  1.2 9.2 %collective-permute-start = (f32[16,8,128]{2,1,0:T(8,128)S(1)}, f32[16,8,128]{2,1,0:T(8,128)S(1)}, u32[]{:S(2)}, u32[]{:S(2)}) collective-permute-start(f32[16,8,128]{2,1,0:T(8,128)S(1)} %get-tuple-element.10), channel_id=1, source_target_pairs={{0,4},{4,8},{8,12},{12,0},{1,5},{5,9},{9,13},{13,1},{2,6},{6,10},{... | collective-permute-start | bytes 196616 | tf_op jit(solution)/shard_map/ppermute | solution.py:179
  3.4 7.0 %collective-permute-start.1 = (f32[64,128]{1,0:T(8,128)S(1)}, f32[64,128]{1,0:T(8,128)S(1)}, u32[]{:S(2)}, u32[]{:S(2)}) collective-permute-start(f32[64,128]{1,0:T(8,128)S(1)} %get-tuple-element.11), channel_id=1, source_target_pairs={{0,1},{1,2},{2,3},{3,0},{4,5},{5,6},{6,7},{7,4},{8,9},{9,10},{10,1... | collective-permute-start | bytes 98312 | tf_op jit(solution)/shard_map/ppermute | solution.py:180
  4.6 5.8 %collective-permute-start.2 = (f32[8,128]{1,0:T(8,128)S(1)}, f32[8,128]{1,0:T(8,128)S(1)}, u32[]{:S(2)}, u32[]{:S(2)}) collective-permute-start(f32[8,128]{1,0:T(8,128)S(1)} %get-tuple-element.12), channel_id=1, source_target_pairs={{0,5},{1,6},{2,7},{3,4},{4,9},{5,10},{6,11},{7,8},{8,13},{9,14},{1... | collective-permute-start | bytes 12296 | tf_op jit(solution)/shard_map/ppermute | solution.py:181
  10.4 1.0 %copy-start.1 = (f32[16,64,128]{2,1,0:T(8,128)S(1)}, f32[16,64,128]{2,1,0:T(8,128)}, u32[]{:S(2)}) copy-start(f32[16,64,128]{2,1,0:T(8,128)} %field_ref.3) | copy-start | bytes 1572868
  11.5 0.7 %copy-start.2 = (s32[6,16,2]{1,2,0:T(2,128)S(1)}, s32[6,16,2]{1,2,0:T(2,128)}, u32[]{:S(2)}) copy-start(s32[6,16,2]{1,2,0:T(2,128)} %param.7) | copy-start | bytes 2308
  12.2 0.7 %copy-start.4 = (f32[6,16,2]{1,2,0:T(2,128)S(1)}, f32[6,16,2]{1,2,0:T(2,128)}, u32[]{:S(2)}) copy-start(f32[6,16,2]{1,2,0:T(2,128)} %param.8) | copy-start | bytes 2308
  12.9 0.7 %copy-start.6 = (s32[6]{0:T(128)S(1)}, s32[6]{0:T(128)}, u32[]{:S(2)}) copy-start(s32[6]{0:T(128)} %order_ref.3) | copy-start | bytes 76
  13.5 0.7 %copy-start.9 = (f32[6]{0:T(128)S(1)}, f32[6]{0:T(128)}, u32[]{:S(2)}) copy-start(f32[6]{0:T(128)} %absorb_ref.3) | copy-start | bytes 76
  17.4 7.9 %collective-permute-start.3 = (f32[3,3,64,128]{3,2,1,0:T(8,128)S(1)}, f32[3,3,64,128]{3,2,1,0:T(8,128)S(1)}, u32[]{:S(2)}, u32[]{:S(2)}) collective-permute-start(f32[3,3,64,128]{3,2,1,0:T(8,128)S(1)} %get-tuple-element.14), channel_id=1, source_target_pairs={{0,16},{16,0},{32,48},{48,32},{64,80},{80,64},{96,112},{112,96},{1... | collective-permute-start | bytes 884744 | tf_op jit(solution)/shard_map/ppermute | solution.py:205
  20.6 0.7 %copy-start.3 = (s32[6,16,2]{1,2,0:T(2,128)S(1)}, s32[6,16,2]{1,2,0:T(2,128)}, u32[]{:S(2)}) copy-start(s32[6,16,2]{1,2,0:T(2,128)} %param.7) | copy-start | bytes 2308
  21.3 0.7 %copy-start.5 = (f32[6,16,2]{1,2,0:T(2,128)S(1)}, f32[6,16,2]{1,2,0:T(2,128)}, u32[]{:S(2)}) copy-start(f32[6,16,2]{1,2,0:T(2,128)} %param.8) | copy-start | bytes 2308
  21.9 0.7 %copy-start.7 = (s32[6]{0:T(128)S(1)}, s32[6]{0:T(128)}, u32[]{:S(2)}) copy-start(s32[6]{0:T(128)} %order_ref.3) | copy-start | bytes 76
  22.6 0.7 %copy-start.10 = (f32[6]{0:T(128)S(1)}, f32[6]{0:T(128)}, u32[]{:S(2)}) copy-start(f32[6]{0:T(128)} %absorb_ref.3) | copy-start | bytes 76
  25.3 33.9 %copy-start.8 = (f32[3,3]{1,0:T(4,128)S(1)}, f32[3,3]{1,0:T(4,128)}, u32[]{:S(2)}) copy-start(f32[3,3]{1,0:T(4,128)} %palette_ref.1) | copy-start | bytes 112
  25.5 5.8 %collective-permute-start.4 = (f32[3,3,32,128]{3,2,1,0:T(8,128)S(1)}, f32[3,3,32,128]{3,2,1,0:T(8,128)S(1)}, u32[]{:S(2)}, u32[]{:S(2)}) collective-permute-start(f32[3,3,32,128]{3,2,1,0:T(8,128)S(1)} %constant_dynamic-slice_fusion.1), channel_id=1, source_target_pairs={{0,32},{16,48},{32,0},{48,16},{64,96},{80,112},{96,64},{112,80},{1... | collective-permute-start | bytes 442376 | tf_op jit(solution)/shard_map/ppermute | solution.py:210
  31.4 4.8 %collective-permute-start.5 = (f32[3,3,16,128]{3,2,1,0:T(8,128)S(1)}, f32[3,3,16,128]{3,2,1,0:T(8,128)S(1)}, u32[]{:S(2)}, u32[]{:S(2)}) collective-permute-start(f32[3,3,16,128]{3,2,1,0:T(8,128)S(1)} %constant_dynamic-slice_fusion), channel_id=1, source_target_pairs={{0,64},{16,80},{32,96},{48,112},{64,0},{80,16},{96,32},{112,48},{1... | collective-permute-start | bytes 221192 | tf_op jit(solution)/shard_map/ppermute | solution.py:212
  36.3 7.4 %collective-permute-start.6 = (f32[3,3,16,128]{3,2,1,0:T(8,128)S(1)}, f32[3,3,16,128]{3,2,1,0:T(8,128)S(1)}, u32[]{:S(2)}, u32[]{:S(2)}) collective-permute-start(f32[3,3,16,128]{3,2,1,0:T(8,128)S(1)} %pad_maximum_fusion.2), channel_id=1, source_target_pairs={{0,192},{16,208},{32,224},{48,240},{64,128},{80,144},{96,160},{112... | collective-permute-start | bytes 221192 | tf_op jit(solution)/shard_map/ppermute | solution.py:213
  43.8 4.3 %collective-permute-start.7 = (f32[3,3,16,128]{3,2,1,0:T(8,128)S(1)}, f32[3,3,16,128]{3,2,1,0:T(8,128)S(1)}, u32[]{:S(2)}, u32[]{:S(2)}) collective-permute-start(f32[3,3,16,128]{3,2,1,0:T(8,128)S(1)} %pad_maximum_fusion.3), channel_id=1, source_target_pairs={{0,64},{16,80},{32,96},{48,112},{64,0},{80,16},{96,32},{112,48},{1... | collective-permute-start | bytes 221192 | tf_op jit(solution)/shard_map/ppermute | solution.py:214
  48.1 5.1 %collective-permute-start.8 = (f32[3,3,32,128]{3,2,1,0:T(8,128)S(1)}, f32[3,3,32,128]{3,2,1,0:T(8,128)S(1)}, u32[]{:S(2)}, u32[]{:S(2)}) collective-permute-start(f32[3,3,32,128]{3,2,1,0:T(8,128)S(1)} %maximum_select_fusion.1), channel_id=1, source_target_pairs={{0,32},{16,48},{32,0},{48,16},{64,96},{80,112},{96,64},{112,80},{1... | collective-permute-start | bytes 442376 | tf_op jit(solution)/shard_map/ppermute | solution.py:215
  53.2 6.0 %collective-permute-start.9 = (f32[3,3,64,128]{3,2,1,0:T(8,128)S(1)}, f32[3,3,64,128]{3,2,1,0:T(8,128)S(1)}, u32[]{:S(2)}, u32[]{:S(2)}) collective-permute-start(f32[3,3,64,128]{3,2,1,0:T(8,128)S(1)} %maximum_select_fusion.mine_ref), channel_id=1, source_target_pairs={{0,16},{16,0},{32,48},{48,32},{64,80},{80,64},{96,112},{112,96},{1... | collective-permute-start | bytes 884744 | tf_op jit(solution)/shard_map/ppermute | solution.py:216

commit v4 on v3

v4 whole, which is shorter than its diff:
```python
import jax
import jax.numpy as jnp
from jax import lax
from jax.experimental import pallas as pl
from jax.experimental.pallas import tpu as pltpu
from jax.sharding import PartitionSpec as P

VIEWS = 6
HALF = VIEWS // 2
SPILL = 8
STREAMS = 1
LANES = 128


def vmem():
    return pl.BlockSpec(memory_space=pltpu.VMEM)


def smem():
    return pl.BlockSpec(memory_space=pltpu.SMEM)


def hbm():
    return pl.BlockSpec(memory_space=pltpu.HBM)


def pack_kernel(field_ref, rows_ref, packed_ref, corner_ref):
    depth, rows, lanes = field_ref.shape
    rows_ref[...] = field_ref[:, rows - SPILL:, :]
    lane = lax.broadcasted_iota(jnp.int32, (rows, lanes), 1)
    packed = jnp.zeros((rows, lanes), jnp.float32)
    for g in range(depth):
        moved = pltpu.roll(field_ref[g], (g * SPILL + SPILL) % lanes, 1)
        packed = jnp.where(lane >= g * SPILL, moved, packed)
    packed_ref[...] = packed
    corner_ref[...] = packed[rows - SPILL:]


def begin_kernel(field_ref, table_ref):
    rows = field_ref.shape[1]
    for g in range(field_ref.shape[0]):
        own = field_ref[g]
        table_ref[0, g, pl.ds(SPILL, rows), :] = own
        table_ref[1, g, pl.ds(SPILL, rows), :] = pltpu.roll(own, 1, 1) - own


def prepare(begun_ref, rows_ref, cols_ref, corner_ref, table_ref):
    _, depth, tall, lanes = table_ref.shape
    rows = tall - SPILL
    has_rows = lax.axis_index("tx") > 0
    has_cols = lax.axis_index("ty") > 0
    first_lane = lax.broadcasted_iota(jnp.int32, (tall, lanes), 1) == 0
    beside = jnp.concatenate([jnp.where(has_rows, corner_ref[...], 0.0), cols_ref[...]], 0)
    beside = jnp.where(has_cols, beside, 0.0)
    shifted = pltpu.roll(beside, 1, 1)

    for g in range(depth):
        turn = lanes - SPILL - g * SPILL
        edge = pltpu.roll(beside, turn, 1)
        before = pltpu.roll(shifted, turn, 1)
        above = jnp.where(has_rows, rows_ref[g], 0.0)
        own = begun_ref[0, g, pl.ds(SPILL, rows), :]
        step = jnp.concatenate([pltpu.roll(above, 1, 1) - above, begun_ref[1, g, pl.ds(SPILL, rows), :]], 0)
        own = jnp.concatenate([above, own], 0)
        table_ref[0, g] = own
        table_ref[1, g] = jnp.where(first_lane, before - own, step)
        table_ref[2, g] = edge
        table_ref[3, g] = before - edge


def render(whole_ref, parts_ref, table_ref, out_ref, base, mixed_refs):
    _, depth, tall, lanes = table_ref.shape
    rows = tall - SPILL
    lane = lax.broadcasted_iota(jnp.int32, (tall, lanes), 1)

    def view(k, carry):
        v = base + k
        flipped = whole_ref[v, 0, depth] == 1
        absorb = parts_ref[v, 0, depth]
        through = jnp.ones((rows, lanes), jnp.float32)
        first = second = jnp.zeros((rows, lanes), jnp.float32)

        def columns(i):
            g = jnp.where(flipped, depth - 1 - i, i)
            offset, weight = whole_ref[v, 1, g], parts_ref[v, 1, g]
            outside = lane >= lanes - offset
            own = jnp.where(outside, table_ref[2, g], table_ref[0, g])
            step = jnp.where(outside, table_ref[3, g], table_ref[1, g])
            mixed_refs[i % len(mixed_refs)][...] = pltpu.roll(own + weight * step, offset, 1)

        def tile_of(i):
            g = jnp.where(flipped, depth - 1 - i, i)
            offset, weight = whole_ref[v, 0, g], parts_ref[v, 0, g]
            mixed_ref = mixed_refs[i % len(mixed_refs)]
            near = mixed_ref[pl.ds(SPILL - offset, rows), :]
            far = mixed_ref[pl.ds(SPILL - 1 - offset, rows), :]
            return near + weight * (far - near)

        columns(0)
        for i in range(depth):
            if i + 1 < depth:
                columns(i + 1)
            tile = tile_of(i)
            squared = tile * tile
            lost = through * (absorb * squared / (1.0 + squared))
            through = through - lost
            first = first + lost * tile
            second = second + lost * squared
        out_ref[k, 0] = through
        out_ref[k, 1] = first
        out_ref[k, 2] = second
        return carry

    lax.fori_loop(0, HALF, view, 0)


def give_kernel(whole_ref, parts_ref, begun_ref, rows_ref, cols_ref, corner_ref, out_ref, table_ref, *mixed_refs):
    prepare(begun_ref, rows_ref, cols_ref, corner_ref, table_ref)
    base = (1 - lax.rem(lax.axis_index("depth"), 2)) * HALF
    render(whole_ref, parts_ref, table_ref, out_ref, base, mixed_refs)


def keep_kernel(whole_ref, parts_ref, table_ref, out_ref, *mixed_refs):
    base = lax.rem(lax.axis_index("depth"), 2) * HALF
    render(whole_ref, parts_ref, table_ref, out_ref, base, mixed_refs)


def paint_kernel(palette_ref, *refs):
    parts, (image_ref, canvas_ref, sems) = refs[:-3], refs[-3:]
    height = parts[0].shape[2]
    core = lax.rem(lax.axis_index("depth"), 2)
    copies = []
    for side in range(2):
        base = (core if side == 0 else 1 - core) * HALF
        for k in range(HALF):
            n = len(copies)
            for stream in range(STREAMS):
                part_ref = parts[side * STREAMS + stream]
                band = pl.ds(stream * height, height)
                alpha = 1.0 - part_ref[k, 0]
                first, second = part_ref[k, 1], part_ref[k, 2]
                for c in range(3):
                    canvas_ref[n, c, band, :] = (
                        palette_ref[c, 0] * alpha + palette_ref[c, 1] * first + palette_ref[c, 2] * second
                    )
                canvas_ref[n, 3, band, :] = alpha
            copies.append(pltpu.make_async_copy(canvas_ref.at[n], image_ref.at[base + k], sems.at[n]))
            copies[-1].start()
    for copy in copies:
        copy.wait()


def over(mine, other, mine_first):
    first = mine_first[:, None, None]
    t_mine, t_other = mine[:, 0], other[:, 0]
    w_mine = jnp.where(first, 1.0, t_other)
    w_other = jnp.where(first, t_mine, 1.0)
    return jnp.stack(
        [
            t_mine * t_other,
            w_mine * mine[:, 1] + w_other * other[:, 1],
            w_mine * mine[:, 2] + w_other * other[:, 2],
        ],
        1,
    )


def along_z(partner):
    return [(2 * z + c, 2 * partner(z) + c) for z in range(8) for c in range(2)]


def join(mine, other, upper):
    return jnp.where(
        upper == 1, jnp.concatenate([other, mine], 2), jnp.concatenate([mine, other], 2)
    )


def shards(field, shear, fraction, absorb, palette, order):
    depth, rows, lanes = field.shape
    place = lax.axis_index("depth")
    core, z = place % 2, place // 2
    rank = jnp.where(z < 4, z, (z % 4) ^ 2)
    ring = [(i, (i + 1) % 4) for i in range(4)]
    diagonal = [(4 * i + j, (i + 1) % 4 * 4 + (j + 1) % 4) for i in range(4) for j in range(4)]

    small = pltpu.CompilerParams(vmem_limit_bytes=4 << 20)
    row_halo, packed, corner = pl.pallas_call(
        pack_kernel,
        out_shape=(
            jax.ShapeDtypeStruct((depth, SPILL, lanes), jnp.float32),
            jax.ShapeDtypeStruct((rows, lanes), jnp.float32),
            jax.ShapeDtypeStruct((SPILL, lanes), jnp.float32),
        ),
        in_specs=[vmem()],
        out_specs=(vmem(), vmem(), vmem()),
        compiler_params=small,
    )(field)
    row_halo = lax.ppermute(row_halo, "tx", ring)
    col_halo = lax.ppermute(packed, "ty", ring)
    corner = lax.ppermute(corner, ("tx", "ty"), diagonal)

    def array(*shape):
        return jax.ShapeDtypeStruct(shape, jnp.float32)

    begun = pl.pallas_call(
        begin_kernel,
        out_shape=array(4, depth, rows + SPILL, lanes),
        in_specs=[vmem()],
        out_specs=vmem(),
        compiler_params=small,
        cost_estimate=pl.CostEstimate(flops=1000000, bytes_accessed=2000000, transcendentals=0),
    )(field)

    last = lax.broadcasted_iota(jnp.int32, (VIEWS, 2, depth + 1), 2) == depth

    def with_last(values, extra):
        values = jnp.pad(jnp.transpose(values, (0, 2, 1)), ((0, 0), (0, 0), (0, 1)))
        return jnp.where(last, extra[:, None, None], values)

    tables = (with_last(shear, order), with_last(fraction, absorb))
    part = array(HALF, 3, rows, lanes)
    scratch = [pltpu.VMEM((rows + SPILL, lanes), jnp.float32)] * 4
    give, table = pl.pallas_call(
        give_kernel,
        out_shape=(part, array(4, depth, rows + SPILL, lanes)),
        in_specs=[smem()] * 2 + [vmem()] * 4,
        out_specs=(vmem(),) * 2,
        scratch_shapes=scratch,
        input_output_aliases={2: 1},
        compiler_params=small,
    )(*tables, begun, row_halo, col_halo, corner)
    keep = pl.pallas_call(
        keep_kernel,
        out_shape=part,
        in_specs=[smem()] * 2 + [vmem()],
        out_specs=vmem(),
        scratch_shapes=scratch,
        compiler_params=small,
        cost_estimate=pl.CostEstimate(flops=10000000, bytes_accessed=5000000, transcendentals=0),
    )(*tables, table)

    forward = lax.dynamic_slice_in_dim(tables[0][:, 0, depth], core * HALF, HALF) == 0
    cores = [(i, i ^ 1) for i in range(16)]
    full = over(keep, lax.ppermute(give, "depth", cores), forward == (core == 0))

    height = rows // 4
    within = [along_z(lambda z, step=step: z ^ step) for step in range(4)]
    across = along_z(lambda z: z ^ 6)

    def quarter(step):
        return lax.dynamic_slice_in_dim(full, (rank ^ step) * height, height, 2)

    came = [quarter(0)] + [None] * 3
    for step in (3, 2, 1):
        came[step] = lax.ppermute(quarter(step), "depth", within[step])
    even = forward == (z % 2 == 0)
    value = over(over(came[0], came[1], even), over(came[2], came[3], even), forward == (z % 4 < 2))
    value = over(value, lax.ppermute(value, "depth", across), forward == (z < 4))
    came = [value] + [None] * 3
    for step in (3, 2, 1):
        came[step] = lax.ppermute(value, "depth", within[step])
    value = join(join(came[0], came[1], rank % 2), join(came[2], came[3], rank % 2), rank // 2)
    values, others = [value], [lax.ppermute(value, "depth", cores)]
    return pl.pallas_call(
        paint_kernel,
        out_shape=array(VIEWS, 4, rows, lanes),
        in_specs=[smem()] + [vmem()] * (2 * STREAMS),
        out_specs=hbm(),
        scratch_shapes=[
            pltpu.VMEM((VIEWS, 4, rows, lanes), jnp.float32),
            pltpu.SemaphoreType.DMA((VIEWS,)),
        ],
        compiler_params=pltpu.CompilerParams(vmem_limit_bytes=6 << 20),
    )(palette, *values, *others)


def solution(mesh):
    return jax.shard_map(
        shards,
        mesh=mesh,
        in_specs=(
            P("depth", "tx", "ty"),
            P(None, "depth", None),
            P(None, "depth", None),
            P(),
            P(),
            P(),
        ),
        out_specs=P(None, None, "tx", "ty"),
        check_vma=False,
    )
```

time: 61.2 us -> 50.6 us (0.83)
  local copies, waits for them, and re-layouts: 7.5 us -> 2.19 us
  waiting for transfers between devices: 18.2 us -> 15.1 us
  starting transfers between devices: 26.8 us -> 24.1 us
  other arithmetic: 1.17 us -> 2.23 us
    unnamed x22 -> x6, local copies, waits for them, and re-layouts: 7.47 us -> 2.09 us
    ppermute x1, waiting for transfers between devices: 3.55 us -> 0.76 us  [shards(): corner = lax.ppermute(corner, ('tx', 'ty'), diagonal)]
    ppermute x6 -> x8, starting transfers between devices: 18.7 us -> 16 us  [the longest x3 6.12 us: shards(): came[step] = lax.ppermute(value, 'depth', within[step])]
    select_n x0 -> x2, other arithmetic: none -> 1.53 us  [with_last(): return jnp.where(last, extra[:, None, None], values)]
    pallas_call x3 -> x4, Pallas kernels: 6.75 us -> 6.42 us  [the longest x1 2.68 us: shards(): pl.pallas_call(give_kernel, out_shape=(part, array(4, depth, rows + SPILL...]
    ppermute x6 -> x8, waiting for transfers between devices: 14.6 us -> 14.4 us  [the longest x3 5.7 us: shards(): came[step] = lax.ppermute(quarter(step), 'depth', within[step])]
  transfers between devices with their start and end apart: 10 -> 12, of which waited for: 7 -> 6; matrix products, arithmetic and copies ran while one was open for 1% -> 4% of each run, Pallas kernels for 3% -> 4%
where the time goes in v4:
time: 50.6 us; the launch traced here: 50.4 us
  starting transfers between devices  24.1 us (48%)
  waiting for transfers between devices  15.1 us (30%)
  Pallas kernels  6.61 us (13%)
  other arithmetic  2.23 us (4%)
  local copies, waits for them, and re-layouts  2.19 us (4%)
    ppermute x3, starting transfers between devices, shards(): came[step] = lax.ppermute(value, 'depth', within[step])  6.12 us
    ppermute x3, waiting for transfers between devices, shards(): came[step] = lax.ppermute(quarter(step), 'depth', within[step])  5.7 us
    ppermute x3, waiting for transfers between devices, shards(): came[step] = lax.ppermute(value, 'depth', within[step])  5.61 us
    ppermute x3, starting transfers between devices, shards(): came[step] = lax.ppermute(quarter(step), 'depth', within[step])  4.81 us
    ppermute x1, starting transfers between devices, shards(): lax.ppermute(value, 'depth', across)  3.55 us
    pallas_call x1, Pallas kernels, shards(): pl.pallas_call(give_kernel, out_shape=(part, array(4, depth, rows + SPILL...  2.68 us
    ppermute x1, starting transfers between devices, shards(): lax.ppermute(give, 'depth', cores)  2.47 us
    ppermute x1, starting transfers between devices, shards(): corner = lax.ppermute(corner, ('tx', 'ty'), diagonal)  2.22 us
  transfers between devices with their start and end apart: 12, of which 6 were waited for; matrix products, arithmetic and copies ran while one was open for 4% of the time, Pallas kernels for 4%

profile of v4, /device:TPU:1, one launch (start us, length us, event | category | flops | bytes accessed | tf_op | source)
XLA Modules:
  0.0 50.4 jit_solution(7687450863532483212)
XLA Ops:
  0.0 1.0 %copy-done = f32[16,64,128]{2,1,0:T(8,128)S(1)} copy-done((f32[16,64,128]{2,1,0:T(8,128)S(1)}, f32[16,64,128]{2,1,0:T(8,128)}, u32[]{:S(2)}) %copy-start) | copy-done | bytes 524312
  1.0 0.2 shard_map.65
  1.2 2.2 %collective-permute-start = (f32[16,8,128]{2,1,0:T(8,128)S(1)}, f32[16,8,128]{2,1,0:T(8,128)S(1)}, u32[]{:S(2)}, u32[]{:S(2)}) collective-permute-start(f32[16,8,128]{2,1,0:T(8,128)S(1)} %get-tuple-element.10), channel_id=1, source_target_pairs={{0,4},{4,8},{8,12},{12,0},{1,5},{5,9},{9,13},{13,1},{2,6},{6,10},{... | collective-permute-start | bytes 196616 | tf_op jit(solution)/shard_map/ppermute | solution.py:198
  3.4 1.2 %collective-permute-start.1 = (f32[64,128]{1,0:T(8,128)S(1)}, f32[64,128]{1,0:T(8,128)S(1)}, u32[]{:S(2)}, u32[]{:S(2)}) collective-permute-start(f32[64,128]{1,0:T(8,128)S(1)} %get-tuple-element.11), channel_id=1, source_target_pairs={{0,1},{1,2},{2,3},{3,0},{4,5},{5,6},{6,7},{7,4},{8,9},{9,10},{10,1... | collective-permute-start | bytes 98312 | tf_op jit(solution)/shard_map/ppermute | solution.py:199
  4.6 2.2 %collective-permute-start.2 = (f32[8,128]{1,0:T(8,128)S(1)}, f32[8,128]{1,0:T(8,128)S(1)}, u32[]{:S(2)}, u32[]{:S(2)}) collective-permute-start(f32[8,128]{1,0:T(8,128)S(1)} %get-tuple-element.12), channel_id=1, source_target_pairs={{0,5},{1,6},{2,7},{3,4},{4,9},{5,10},{6,11},{7,8},{8,13},{9,14},{1... | collective-permute-start | bytes 12296 | tf_op jit(solution)/shard_map/ppermute | solution.py:200
  6.9 0.8 %pad_select_fusion.1.whole_ref = s32[6,2,17]{2,1,0:T(2,128)S(1)} fusion(s32[6,2,16]{2,1,0:T(2,128)} %bitcast.2, pred[17]{0:T(512)(128)(4,1)S(1)} %iota_compare_fusion, s32[6]{0:T(128)} %param.11), kind=kLoop, calls=%fused_computation.45 | loop fusion | flops 204 | bytes 1625 | tf_op jit(solution)/shard_map/jit(_where)/select_n | solution.py:218
  7.6 0.8 %pad_select_fusion.parts_ref = f32[6,2,17]{2,1,0:T(2,128)S(1)} fusion(f32[6,2,16]{2,1,0:T(2,128)} %bitcast.3, pred[17]{0:T(512)(128)(4,1)S(1)} %iota_compare_fusion, f32[6]{0:T(128)} %param.9), kind=kLoop, calls=%fused_computation.44 | loop fusion | flops 204 | bytes 1625 | tf_op jit(solution)/shard_map/jit(_where)/select_n | solution.py:218
  8.4 1.0 %copy-done.1 = f32[16,64,128]{2,1,0:T(8,128)S(1)} copy-done((f32[16,64,128]{2,1,0:T(8,128)S(1)}, f32[16,64,128]{2,1,0:T(8,128)}, u32[]{:S(2)}) %copy-start.1) | copy-done | bytes 524312
  9.4 0.2 shard_map.64.begun_ref
  9.7 0.8 %collective-permute-done.2.corner_ref = f32[8,128]{1,0:T(8,128)S(1)} collective-permute-done((f32[8,128]{1,0:T(8,128)S(1)}, f32[8,128]{1,0:T(8,128)S(1)}, u32[]{:S(2)}, u32[]{:S(2)}) %collective-permute-start.2) | collective-permute-done | bytes 4128 | tf_op jit(solution)/shard_map/ppermute | solution.py:200
  10.4 2.7 %shard_map.66 = (f32[3,3,64,128]{3,2,1,0:T(8,128)S(1)}, f32[4,16,72,128]{3,2,1,0:T(8,128)S(1)}) custom-call(s32[6,2,17]{2,1,0:T(2,128)S(1)} %pad_select_fusion.1.whole_ref, f32[6,2,17]{2,1,0:T(2,128)S(1)} %pad_select_fusion.parts_ref, f32[4,16,72,128]{3,2,1,0:T(8,128)S(1)} %shard_map.64.begun_ref, ...), custom_call_target="tpu_custom_call", output_to_operand_aliasing={{1}: (2, {})} | custom-call | tf_op jit(solution)/shard_map/pallas_call | solution.py:223
  13.1 2.5 %collective-permute-start.3 = (f32[3,3,64,128]{3,2,1,0:T(8,128)S(1)}, f32[3,3,64,128]{3,2,1,0:T(8,128)S(1)}, u32[]{:S(2)}, u32[]{:S(2)}) collective-permute-start(f32[3,3,64,128]{3,2,1,0:T(8,128)S(1)} %get-tuple-element.14), channel_id=1, source_target_pairs={{0,16},{16,0},{32,48},{48,32},{64,80},{80,64},{96,112},{112,96},{1... | collective-permute-start | bytes 884744 | tf_op jit(solution)/shard_map/ppermute | solution.py:244
  15.6 0.1 slice.90
  15.7 0.3 compare_reduce_fusion
  16.0 2.0 %shard_map.67 = f32[3,3,64,128]{3,2,1,0:T(8,128)S(1)} custom-call(s32[6,2,17]{2,1,0:T(2,128)S(1)} %pad_select_fusion.1.whole_ref, f32[6,2,17]{2,1,0:T(2,128)S(1)} %pad_select_fusion.parts_ref, f32[4,16,72,128]{3,2,1,0:T(8,128)S(1)} %get-tuple-element.13.table_ref), custom_call_target="tpu_custom_call" | custom-call | flops 10000000 | bytes 5000000 | tf_op jit(solution)/shard_map/pallas_call | solution.py:232
  18.0 0.0 copy-start.2
  18.0 0.1 fusion.1
  18.2 4.4 %collective-permute-start.6 = (f32[3,3,16,128]{3,2,1,0:T(8,128)S(1)}, f32[3,3,16,128]{3,2,1,0:T(8,128)S(1)}, u32[]{:S(2)}, u32[]{:S(2)}) collective-permute-start(f32[3,3,16,128]{3,2,1,0:T(8,128)S(1)} %get-tuple-element.25), channel_id=1, source_target_pairs={{0,96},{16,112},{32,64},{48,80},{64,32},{80,48},{96,0},{112,16},{1... | collective-permute-start | bytes 221192 | tf_op jit(solution)/shard_map/ppermute | solution.py:255
  22.6 0.4 collective-permute-start.4
  23.0 2.3 %collective-permute-done.6 = f32[3,3,16,128]{3,2,1,0:T(8,128)S(1)} collective-permute-done((f32[3,3,16,128]{3,2,1,0:T(8,128)S(1)}, f32[3,3,16,128]{3,2,1,0:T(8,128)S(1)}, u32[]{:S(2)}, u32[]{:S(2)}) %collective-permute-start.6) | collective-permute-done | bytes 73760 | tf_op jit(solution)/shard_map/ppermute | solution.py:255
  25.3 3.4 %collective-permute-done.5 = f32[3,3,16,128]{3,2,1,0:T(8,128)S(1)} collective-permute-done((f32[3,3,16,128]{3,2,1,0:T(8,128)S(1)}, f32[3,3,16,128]{3,2,1,0:T(8,128)S(1)}, u32[]{:S(2)}, u32[]{:S(2)}) %collective-permute-start.5) | collective-permute-done | bytes 73760 | tf_op jit(solution)/shard_map/ppermute | solution.py:255
  28.7 0.1 fusion.11
  28.9 3.6 %collective-permute-start.7 = (f32[3,3,16,128]{3,2,1,0:T(8,128)S(1)}, f32[3,3,16,128]{3,2,1,0:T(8,128)S(1)}, u32[]{:S(2)}, u32[]{:S(2)}) collective-permute-start(f32[3,3,16,128]{3,2,1,0:T(8,128)S(1)} %pad_maximum_fusion.1), channel_id=1, source_target_pairs={{0,192},{16,208},{32,224},{48,240},{64,128},{80,144},{96,160},{112... | collective-permute-start | bytes 221192 | tf_op jit(solution)/shard_map/ppermute | solution.py:258
  32.4 1.8 %collective-permute-done.7 = f32[3,3,16,128]{3,2,1,0:T(8,128)S(1)} collective-permute-done((f32[3,3,16,128]{3,2,1,0:T(8,128)S(1)}, f32[3,3,16,128]{3,2,1,0:T(8,128)S(1)}, u32[]{:S(2)}, u32[]{:S(2)}) %collective-permute-start.7) | collective-permute-done | bytes 73760 | tf_op jit(solution)/shard_map/ppermute | solution.py:258
  34.3 0.1 fusion.3
  34.3 3.9 %collective-permute-start.10 = (f32[3,3,16,128]{3,2,1,0:T(8,128)S(1)}, f32[3,3,16,128]{3,2,1,0:T(8,128)S(1)}, u32[]{:S(2)}, u32[]{:S(2)}) collective-permute-start(f32[3,3,16,128]{3,2,1,0:T(8,128)S(1)} %pad_maximum_fusion.2), channel_id=1, source_target_pairs={{0,32},{16,48},{32,0},{48,16},{64,96},{80,112},{96,64},{112,80},{1... | collective-permute-start | bytes 221192 | tf_op jit(solution)/shard_map/ppermute | solution.py:261
  38.3 0.7 %collective-permute-start.9 = (f32[3,3,16,128]{3,2,1,0:T(8,128)S(1)}, f32[3,3,16,128]{3,2,1,0:T(8,128)S(1)}, u32[]{:S(2)}, u32[]{:S(2)}) collective-permute-start(f32[3,3,16,128]{3,2,1,0:T(8,128)S(1)} %pad_maximum_fusion.2), channel_id=1, source_target_pairs={{0,64},{16,80},{32,96},{48,112},{64,0},{80,16},{96,32},{112,48},{1... | collective-permute-start | bytes 221192 | tf_op jit(solution)/shard_map/ppermute | solution.py:261
  38.9 1.5 %collective-permute-start.8 = (f32[3,3,16,128]{3,2,1,0:T(8,128)S(1)}, f32[3,3,16,128]{3,2,1,0:T(8,128)S(1)}, u32[]{:S(2)}, u32[]{:S(2)}) collective-permute-start(f32[3,3,16,128]{3,2,1,0:T(8,128)S(1)} %pad_maximum_fusion.2), channel_id=1, source_target_pairs={{0,96},{16,112},{32,64},{48,80},{64,32},{80,48},{96,0},{112,16},{1... | collective-permute-start | bytes 221192 | tf_op jit(solution)/shard_map/ppermute | solution.py:261
  40.5 5.6 %collective-permute-done.9 = f32[3,3,16,128]{3,2,1,0:T(8,128)S(1)} collective-permute-done((f32[3,3,16,128]{3,2,1,0:T(8,128)S(1)}, f32[3,3,16,128]{3,2,1,0:T(8,128)S(1)}, u32[]{:S(2)}, u32[]{:S(2)}) %collective-permute-start.9) | collective-permute-done | bytes 73760 | tf_op jit(solution)/shard_map/ppermute | solution.py:261
  46.1 1.5 %collective-permute-start.11 = (f32[3,3,64,128]{3,2,1,0:T(8,128)S(1)}, f32[3,3,64,128]{3,2,1,0:T(8,128)S(1)}, u32[]{:S(2)}, u32[]{:S(2)}) collective-permute-start(f32[3,3,64,128]{3,2,1,0:T(8,128)S(1)} %maximum_select_fusion.refs_0_), channel_id=1, source_target_pairs={{0,16},{16,0},{32,48},{48,32},{64,80},{80,64},{96,112},{112,96},{1... | collective-permute-start | bytes 884744 | tf_op jit(solution)/shard_map/ppermute | solution.py:263
  47.6 1.2 %collective-permute-done.11.refs_1_ = f32[3,3,64,128]{3,2,1,0:T(8,128)S(1)} collective-permute-done((f32[3,3,64,128]{3,2,1,0:T(8,128)S(1)}, f32[3,3,64,128]{3,2,1,0:T(8,128)S(1)}, u32[]{:S(2)}, u32[]{:S(2)}) %collective-permute-start.11) | collective-permute-done | bytes 294944 | tf_op jit(solution)/shard_map/ppermute | solution.py:263
  48.8 1.5 %shard_map.68 = f32[6,4,64,128]{3,2,1,0:T(8,128)} custom-call(f32[3,3]{1,0:T(4,128)S(1)} %copy-done.2, f32[3,3,64,128]{3,2,1,0:T(8,128)S(1)} %maximum_select_fusion.refs_0_, f32[3,3,64,128]{3,2,1,0:T(8,128)S(1)} %collective-permute-done.11.refs_1_), custom_call_target="tpu_custom_call" | custom-call | tf_op jit(solution)/shard_map/pallas_call | solution.py:264
  (19 shorter events, 0.2 us)
Async XLA Ops:
  0.0 1.0 %copy-start = (f32[16,64,128]{2,1,0:T(8,128)S(1)}, f32[16,64,128]{2,1,0:T(8,128)}, u32[]{:S(2)}) copy-start(f32[16,64,128]{2,1,0:T(8,128)} %field_ref.3) | copy-start | bytes 1572868
  1.2 9.2 %collective-permute-start = (f32[16,8,128]{2,1,0:T(8,128)S(1)}, f32[16,8,128]{2,1,0:T(8,128)S(1)}, u32[]{:S(2)}, u32[]{:S(2)}) collective-permute-start(f32[16,8,128]{2,1,0:T(8,128)S(1)} %get-tuple-element.10), channel_id=1, source_target_pairs={{0,4},{4,8},{8,12},{12,0},{1,5},{5,9},{9,13},{13,1},{2,6},{6,10},{... | collective-permute-start | bytes 196616 | tf_op jit(solution)/shard_map/ppermute | solution.py:198
  3.4 7.0 %collective-permute-start.1 = (f32[64,128]{1,0:T(8,128)S(1)}, f32[64,128]{1,0:T(8,128)S(1)}, u32[]{:S(2)}, u32[]{:S(2)}) collective-permute-start(f32[64,128]{1,0:T(8,128)S(1)} %get-tuple-element.11), channel_id=1, source_target_pairs={{0,1},{1,2},{2,3},{3,0},{4,5},{5,6},{6,7},{7,4},{8,9},{9,10},{10,1... | collective-permute-start | bytes 98312 | tf_op jit(solution)/shard_map/ppermute | solution.py:199
  4.6 5.8 %collective-permute-start.2 = (f32[8,128]{1,0:T(8,128)S(1)}, f32[8,128]{1,0:T(8,128)S(1)}, u32[]{:S(2)}, u32[]{:S(2)}) collective-permute-start(f32[8,128]{1,0:T(8,128)S(1)} %get-tuple-element.12), channel_id=1, source_target_pairs={{0,5},{1,6},{2,7},{3,4},{4,9},{5,10},{6,11},{7,8},{8,13},{9,14},{1... | collective-permute-start | bytes 12296 | tf_op jit(solution)/shard_map/ppermute | solution.py:200
  8.4 1.0 %copy-start.1 = (f32[16,64,128]{2,1,0:T(8,128)S(1)}, f32[16,64,128]{2,1,0:T(8,128)}, u32[]{:S(2)}) copy-start(f32[16,64,128]{2,1,0:T(8,128)} %field_ref.3) | copy-start | bytes 1572868
  13.1 4.9 %collective-permute-start.3 = (f32[3,3,64,128]{3,2,1,0:T(8,128)S(1)}, f32[3,3,64,128]{3,2,1,0:T(8,128)S(1)}, u32[]{:S(2)}, u32[]{:S(2)}) collective-permute-start(f32[3,3,64,128]{3,2,1,0:T(8,128)S(1)} %get-tuple-element.14), channel_id=1, source_target_pairs={{0,16},{16,0},{32,48},{48,32},{64,80},{80,64},{96,112},{112,96},{1... | collective-permute-start | bytes 884744 | tf_op jit(solution)/shard_map/ppermute | solution.py:244
  18.0 30.8 %copy-start.2 = (f32[3,3]{1,0:T(4,128)S(1)}, f32[3,3]{1,0:T(4,128)}, u32[]{:S(2)}) copy-start(f32[3,3]{1,0:T(4,128)} %palette_ref.1) | copy-start | bytes 112
  18.2 7.1 %collective-permute-start.6 = (f32[3,3,16,128]{3,2,1,0:T(8,128)S(1)}, f32[3,3,16,128]{3,2,1,0:T(8,128)S(1)}, u32[]{:S(2)}, u32[]{:S(2)}) collective-permute-start(f32[3,3,16,128]{3,2,1,0:T(8,128)S(1)} %get-tuple-element.25), channel_id=1, source_target_pairs={{0,96},{16,112},{32,64},{48,80},{64,32},{80,48},{96,0},{112,16},{1... | collective-permute-start | bytes 221192 | tf_op jit(solution)/shard_map/ppermute | solution.py:255
  22.6 6.1 %collective-permute-start.5 = (f32[3,3,16,128]{3,2,1,0:T(8,128)S(1)}, f32[3,3,16,128]{3,2,1,0:T(8,128)S(1)}, u32[]{:S(2)}, u32[]{:S(2)}) collective-permute-start(f32[3,3,16,128]{3,2,1,0:T(8,128)S(1)} %get-tuple-element.26), channel_id=1, source_target_pairs={{0,64},{16,80},{32,96},{48,112},{64,0},{80,16},{96,32},{112,48},{1... | collective-permute-start | bytes 221192 | tf_op jit(solution)/shard_map/ppermute | solution.py:255
  22.6 6.1 %collective-permute-start.4 = (f32[3,3,16,128]{3,2,1,0:T(8,128)S(1)}, f32[3,3,16,128]{3,2,1,0:T(8,128)S(1)}, u32[]{:S(2)}, u32[]{:S(2)}) collective-permute-start(f32[3,3,16,128]{3,2,1,0:T(8,128)S(1)} %get-tuple-element.24), channel_id=1, source_target_pairs={{0,32},{16,48},{32,0},{48,16},{64,96},{80,112},{96,64},{112,80},{1... | collective-permute-start | bytes 221192 | tf_op jit(solution)/shard_map/ppermute | solution.py:255
  28.9 5.4 %collective-permute-start.7 = (f32[3,3,16,128]{3,2,1,0:T(8,128)S(1)}, f32[3,3,16,128]{3,2,1,0:T(8,128)S(1)}, u32[]{:S(2)}, u32[]{:S(2)}) collective-permute-start(f32[3,3,16,128]{3,2,1,0:T(8,128)S(1)} %pad_maximum_fusion.1), channel_id=1, source_target_pairs={{0,192},{16,208},{32,224},{48,240},{64,128},{80,144},{96,160},{112... | collective-permute-start | bytes 221192 | tf_op jit(solution)/shard_map/ppermute | solution.py:258
  34.3 6.1 %collective-permute-start.10 = (f32[3,3,16,128]{3,2,1,0:T(8,128)S(1)}, f32[3,3,16,128]{3,2,1,0:T(8,128)S(1)}, u32[]{:S(2)}, u32[]{:S(2)}) collective-permute-start(f32[3,3,16,128]{3,2,1,0:T(8,128)S(1)} %pad_maximum_fusion.2), channel_id=1, source_target_pairs={{0,32},{16,48},{32,0},{48,16},{64,96},{80,112},{96,64},{112,80},{1... | collective-permute-start | bytes 221192 | tf_op jit(solution)/shard_map/ppermute | solution.py:261
  38.3 7.8 %collective-permute-start.9 = (f32[3,3,16,128]{3,2,1,0:T(8,128)S(1)}, f32[3,3,16,128]{3,2,1,0:T(8,128)S(1)}, u32[]{:S(2)}, u32[]{:S(2)}) collective-permute-start(f32[3,3,16,128]{3,2,1,0:T(8,128)S(1)} %pad_maximum_fusion.2), channel_id=1, source_target_pairs={{0,64},{16,80},{32,96},{48,112},{64,0},{80,16},{96,32},{112,48},{1... | collective-permute-start | bytes 221192 | tf_op jit(solution)/shard_map/ppermute | solution.py:261
  38.9 7.2 %collective-permute-start.8 = (f32[3,3,16,128]{3,2,1,0:T(8,128)S(1)}, f32[3,3,16,128]{3,2,1,0:T(8,128)S(1)}, u32[]{:S(2)}, u32[]{:S(2)}) collective-permute-start(f32[3,3,16,128]{3,2,1,0:T(8,128)S(1)} %pad_maximum_fusion.2), channel_id=1, source_target_pairs={{0,96},{16,112},{32,64},{48,80},{64,32},{80,48},{96,0},{112,16},{1... | collective-permute-start | bytes 221192 | tf_op jit(solution)/shard_map/ppermute | solution.py:261
  46.1 2.7 %collective-permute-start.11 = (f32[3,3,64,128]{3,2,1,0:T(8,128)S(1)}, f32[3,3,64,128]{3,2,1,0:T(8,128)S(1)}, u32[]{:S(2)}, u32[]{:S(2)}) collective-permute-start(f32[3,3,64,128]{3,2,1,0:T(8,128)S(1)} %maximum_select_fusion.refs_0_), channel_id=1, source_target_pairs={{0,16},{16,0},{32,48},{48,32},{64,80},{80,64},{96,112},{112,96},{1... | collective-permute-start | bytes 884744 | tf_op jit(solution)/shard_map/ppermute | solution.py:263

commit v5 on v4

--- a/solution.py
+++ b/solution.py
@@ -8,8 +8,6 @@
 VIEWS = 6
 HALF = VIEWS // 2
 SPILL = 8
-STREAMS = 1
-LANES = 128
 
 
 def vmem():
@@ -24,8 +22,9 @@
     return pl.BlockSpec(memory_space=pltpu.HBM)
 
 
-def pack_kernel(field_ref, rows_ref, packed_ref, corner_ref):
+def pack_kernel(field_ref, held_ref, rows_ref, packed_ref, corner_ref):
     depth, rows, lanes = field_ref.shape
+    held_ref[...] = field_ref[...]
     rows_ref[...] = field_ref[:, rows - SPILL:, :]
     lane = lax.broadcasted_iota(jnp.int32, (rows, lanes), 1)
     packed = jnp.zeros((rows, lanes), jnp.float32)
@@ -66,6 +65,13 @@
         table_ref[1, g] = jnp.where(first_lane, before - own, step)
         table_ref[2, g] = edge
         table_ref[3, g] = before - edge
+
+
+def spot():
+    place = lax.axis_index("depth")
+    core, z = lax.rem(place, 2), lax.div(place, 2)
+    rank = jnp.where(z < 4, z, 7 - z)
+    return core, z, lax.rem(rank, 2), lax.div(rank, 2)
 
 
 def render(whole_ref, parts_ref, table_ref, out_ref, base, mixed_refs):
@@ -116,34 +122,26 @@
 
 def give_kernel(whole_ref, parts_ref, begun_ref, rows_ref, cols_ref, corner_ref, out_ref, table_ref, *mixed_refs):
     prepare(begun_ref, rows_ref, cols_ref, corner_ref, table_ref)
-    base = (1 - lax.rem(lax.axis_index("depth"), 2)) * HALF
-    render(whole_ref, parts_ref, table_ref, out_ref, base, mixed_refs)
+    render(whole_ref, parts_ref, table_ref, out_ref, (1 - spot()[0]) * HALF, mixed_refs)
 
 
 def keep_kernel(whole_ref, parts_ref, table_ref, out_ref, *mixed_refs):
-    base = lax.rem(lax.axis_index("depth"), 2) * HALF
-    render(whole_ref, parts_ref, table_ref, out_ref, base, mixed_refs)
-
-
-def paint_kernel(palette_ref, *refs):
-    parts, (image_ref, canvas_ref, sems) = refs[:-3], refs[-3:]
-    height = parts[0].shape[2]
-    core = lax.rem(lax.axis_index("depth"), 2)
+    render(whole_ref, parts_ref, table_ref, out_ref, spot()[0] * HALF, mixed_refs)
+
+
+def paint_kernel(palette_ref, mine_ref, other_ref, image_ref, canvas_ref, sems):
+    core = spot()[0]
     copies = []
-    for side in range(2):
-        base = (core if side == 0 else 1 - core) * HALF
+    for part_ref, base in ((mine_ref, core * HALF), (other_ref, (1 - core) * HALF)):
         for k in range(HALF):
             n = len(copies)
-            for stream in range(STREAMS):
-                part_ref = parts[side * STREAMS + stream]
-                band = pl.ds(stream * height, height)
-                alpha = 1.0 - part_ref[k, 0]
-                first, second = part_ref[k, 1], part_ref[k, 2]
-                for c in range(3):
-                    canvas_ref[n, c, band, :] = (
-                        palette_ref[c, 0] * alpha + palette_ref[c, 1] * first + palette_ref[c, 2] * second
-                    )
-                canvas_ref[n, 3, band, :] = alpha
+            alpha = 1.0 - part_ref[k, 0]
+            first, second = part_ref[k, 1], part_ref[k, 2]
+            for c in range(3):
+                canvas_ref[n, c] = (
+                    palette_ref[c, 0] * alpha + palette_ref[c, 1] * first + palette_ref[c, 2] * second
+                )
+            canvas_ref[n, 3] = alpha
             copies.append(pltpu.make_async_copy(canvas_ref.at[n], image_ref.at[base + k], sems.at[n]))
             copies[-1].start()
     for copy in copies:
@@ -177,22 +175,21 @@
 
 def shards(field, shear, fraction, absorb, palette, order):
     depth, rows, lanes = field.shape
-    place = lax.axis_index("depth")
-    core, z = place % 2, place // 2
-    rank = jnp.where(z < 4, z, (z % 4) ^ 2)
     ring = [(i, (i + 1) % 4) for i in range(4)]
-    diagonal = [(4 * i + j, (i + 1) % 4 * 4 + (j + 1) % 4) for i in range(4) for j in range(4)]
+    diagonal = [(4 * i + j, 4 * i + j + 5) for i in range(3) for j in range(3)]
+    diagonal += [(12, 4), (7, 3), (15, 12), (3, 0), (13, 1), (14, 2), (11, 8)]
 
     small = pltpu.CompilerParams(vmem_limit_bytes=4 << 20)
-    row_halo, packed, corner = pl.pallas_call(
+    held, row_halo, packed, corner = pl.pallas_call(
         pack_kernel,
         out_shape=(
+            jax.ShapeDtypeStruct((depth, rows, lanes), jnp.float32),
             jax.ShapeDtypeStruct((depth, SPILL, lanes), jnp.float32),
             jax.ShapeDtypeStruct((rows, lanes), jnp.float32),
             jax.ShapeDtypeStruct((SPILL, lanes), jnp.float32),
         ),
         in_specs=[vmem()],
-        out_specs=(vmem(), vmem(), vmem()),
+        out_specs=(vmem(),) * 4,
         compiler_params=small,
     )(field)
     row_halo = lax.ppermute(row_halo, "tx", ring)
@@ -209,7 +206,7 @@
         out_specs=vmem(),
         compiler_params=small,
         cost_estimate=pl.CostEstimate(flops=1000000, bytes_accessed=2000000, transcendentals=0),
-    )(field)
+    )(held)
 
     last = lax.broadcasted_iota(jnp.int32, (VIEWS, 2, depth + 1), 2) == depth
 
@@ -239,39 +236,35 @@
         cost_estimate=pl.CostEstimate(flops=10000000, bytes_accessed=5000000, transcendentals=0),
     )(*tables, table)
 
+    core, z, odd, half = spot()
     forward = lax.dynamic_slice_in_dim(tables[0][:, 0, depth], core * HALF, HALF) == 0
     cores = [(i, i ^ 1) for i in range(16)]
     full = over(keep, lax.ppermute(give, "depth", cores), forward == (core == 0))
 
     height = rows // 4
     within = [along_z(lambda z, step=step: z ^ step) for step in range(4)]
-    across = along_z(lambda z: z ^ 6)
 
     def quarter(step):
-        return lax.dynamic_slice_in_dim(full, (rank ^ step) * height, height, 2)
-
-    came = [quarter(0)] + [None] * 3
-    for step in (3, 2, 1):
-        came[step] = lax.ppermute(quarter(step), "depth", within[step])
+        return lax.dynamic_slice_in_dim(full, ((2 * half + odd) ^ step) * height, height, 2)
+
+    came = [quarter(0)]
+    for step in (1, 2, 3):
+        came.append(lax.ppermute(quarter(step), "depth", within[step]))
     even = forward == (z % 2 == 0)
     value = over(over(came[0], came[1], even), over(came[2], came[3], even), forward == (z % 4 < 2))
-    value = over(value, lax.ppermute(value, "depth", across), forward == (z < 4))
-    came = [value] + [None] * 3
-    for step in (3, 2, 1):
-        came[step] = lax.ppermute(value, "depth", within[step])
-    value = join(join(came[0], came[1], rank % 2), join(came[2], came[3], rank % 2), rank // 2)
-    values, others = [value], [lax.ppermute(value, "depth", cores)]
+    value = over(value, lax.ppermute(value, "depth", along_z(lambda z: 7 - z)), forward == (z < 4))
+    came = [value]
+    for step in (1, 2, 3):
+        came.append(lax.ppermute(value, "depth", within[step]))
+    mine = join(join(came[0], came[1], odd), join(came[2], came[3], odd), half)
     return pl.pallas_call(
         paint_kernel,
         out_shape=array(VIEWS, 4, rows, lanes),
-        in_specs=[smem()] + [vmem()] * (2 * STREAMS),
+        in_specs=[smem(), vmem(), vmem()],
         out_specs=hbm(),
-        scratch_shapes=[
-            pltpu.VMEM((VIEWS, 4, rows, lanes), jnp.float32),
-            pltpu.SemaphoreType.DMA((VIEWS,)),
-        ],
+        scratch_shapes=[pltpu.VMEM((VIEWS, 4, rows, lanes), jnp.float32), pltpu.SemaphoreType.DMA((VIEWS,))],
         compiler_params=pltpu.CompilerParams(vmem_limit_bytes=6 << 20),
-    )(palette, *values, *others)
+    )(palette, mine, lax.ppermute(mine, "depth", cores))
 
 
 def solution(mesh):

time: 50.6 us -> 48.2 us (0.953)
  waiting for transfers between devices: 15.1 us -> 13.8 us
  local copies, waits for them, and re-layouts: 2.19 us -> 1.15 us
    unnamed x6 -> x4, local copies, waits for them, and re-layouts: 2.09 us -> 1.05 us
    ppermute x1, waiting for transfers between devices: 0.76 us -> 0.01 us  [shards(): corner = lax.ppermute(corner, ('tx', 'ty'), diagonal)]
    ppermute x8, waiting for transfers between devices: 14.4 us -> 13.7 us  [the longest x3 5.7 us: shards(): came.append(lax.ppermute(quarter(step), 'depth', within[step]))]
  transfers between devices with their start and end apart: 12 -> 12, of which waited for: 6 -> 6; matrix products, arithmetic and copies ran while one was open for 4% -> 4% of each run, Pallas kernels for 4% -> 5%
where the time goes in v5:
time: 48.2 us; the launch traced here: 47.9 us
  starting transfers between devices  24 us (50%)
  waiting for transfers between devices  13.8 us (29%)
  Pallas kernels  6.63 us (14%)
  other arithmetic  2.23 us (5%)
  local copies, waits for them, and re-layouts  1.15 us (2%)
    ppermute x3, waiting for transfers between devices, shards(): came.append(lax.ppermute(quarter(step), 'depth', within[step]))  5.7 us
    ppermute x3, starting transfers between devices, shards(): came.append(lax.ppermute(quarter(step), 'depth', within[step]))  4.81 us
    ppermute x1, starting transfers between devices, shards(): lax.ppermute(value, 'depth', along_z(lambda z: 7 - z))  4.57 us
    ppermute x1, waiting for transfers between devices, shards(): lax.ppermute(value, 'depth', along_z(lambda z: 7 - z))  3.93 us
    ppermute x3, starting transfers between devices, shards(): came.append(lax.ppermute(value, 'depth', within[step]))  3.62 us
    ppermute x1, starting transfers between devices, shards(): lax.ppermute(mine, 'depth', cores)  3.27 us
    ppermute x3, waiting for transfers between devices, shards(): came.append(lax.ppermute(value, 'depth', within[step]))  2.9 us
    pallas_call x1, Pallas kernels, shards(): pl.pallas_call(give_kernel, out_shape=(part, array(4, depth, rows + SPILL...  2.69 us
  transfers between devices with their start and end apart: 12, of which 6 were waited for; matrix products, arithmetic and copies ran while one was open for 4% of the time, Pallas kernels for 5%

profile of v5, /device:TPU:1, one launch (start us, length us, event | category | flops | bytes accessed | tf_op | source)
XLA Modules:
  0.0 47.9 jit_solution(3527889558129477617)
XLA Ops:
  0.0 1.0 %copy-done = f32[16,64,128]{2,1,0:T(8,128)S(1)} copy-done((f32[16,64,128]{2,1,0:T(8,128)S(1)}, f32[16,64,128]{2,1,0:T(8,128)}, u32[]{:S(2)}) %copy-start) | copy-done | bytes 524312
  1.0 0.2 shard_map.64
  1.3 2.2 %collective-permute-start = (f32[16,8,128]{2,1,0:T(8,128)S(1)}, f32[16,8,128]{2,1,0:T(8,128)S(1)}, u32[]{:S(2)}, u32[]{:S(2)}) collective-permute-start(f32[16,8,128]{2,1,0:T(8,128)S(1)} %get-tuple-element.12), channel_id=1, source_target_pairs={{0,4},{4,8},{8,12},{12,0},{1,5},{5,9},{9,13},{13,1},{2,6},{6,10},{... | collective-permute-start | bytes 196616 | tf_op jit(solution)/shard_map/ppermute | solution.py:195
  3.4 1.2 %collective-permute-start.1 = (f32[64,128]{1,0:T(8,128)S(1)}, f32[64,128]{1,0:T(8,128)S(1)}, u32[]{:S(2)}, u32[]{:S(2)}) collective-permute-start(f32[64,128]{1,0:T(8,128)S(1)} %get-tuple-element.13), channel_id=1, source_target_pairs={{0,1},{1,2},{2,3},{3,0},{4,5},{5,6},{6,7},{7,4},{8,9},{9,10},{10,1... | collective-permute-start | bytes 98312 | tf_op jit(solution)/shard_map/ppermute | solution.py:196
  4.7 2.2 %collective-permute-start.2 = (f32[8,128]{1,0:T(8,128)S(1)}, f32[8,128]{1,0:T(8,128)S(1)}, u32[]{:S(2)}, u32[]{:S(2)}) collective-permute-start(f32[8,128]{1,0:T(8,128)S(1)} %get-tuple-element.14), channel_id=1, source_target_pairs={{0,5},{1,6},{2,7},{4,9},{5,10},{6,11},{8,13},{9,14},{10,15},{12,4}... | collective-permute-start | bytes 12296 | tf_op jit(solution)/shard_map/ppermute | solution.py:197
  6.9 0.8 %pad_select_fusion.1.whole_ref = s32[6,2,17]{2,1,0:T(2,128)S(1)} fusion(s32[6,2,16]{2,1,0:T(2,128)} %bitcast.2, pred[17]{0:T(512)(128)(4,1)S(1)} %iota_compare_fusion, s32[6]{0:T(128)} %param.11), kind=kLoop, calls=%fused_computation.45 | loop fusion | flops 204 | bytes 1625 | tf_op jit(solution)/shard_map/jit(_where)/select_n | solution.py:215
  7.7 0.8 %pad_select_fusion.parts_ref = f32[6,2,17]{2,1,0:T(2,128)S(1)} fusion(f32[6,2,16]{2,1,0:T(2,128)} %bitcast.3, pred[17]{0:T(512)(128)(4,1)S(1)} %iota_compare_fusion, f32[6]{0:T(128)} %param.9), kind=kLoop, calls=%fused_computation.44 | loop fusion | flops 204 | bytes 1625 | tf_op jit(solution)/shard_map/jit(_where)/select_n | solution.py:215
  8.4 0.2 shard_map.65.begun_ref
  8.6 0.0 collective-permute-done.1.cols_ref
  8.7 2.7 %shard_map.66 = (f32[3,3,64,128]{3,2,1,0:T(8,128)S(1)}, f32[4,16,72,128]{3,2,1,0:T(8,128)S(1)}) custom-call(s32[6,2,17]{2,1,0:T(2,128)S(1)} %pad_select_fusion.1.whole_ref, f32[6,2,17]{2,1,0:T(2,128)S(1)} %pad_select_fusion.parts_ref, f32[4,16,72,128]{3,2,1,0:T(8,128)S(1)} %shard_map.65.begun_ref, ...), custom_call_target="tpu_custom_call", output_to_operand_aliasing={{1}: (2, {})} | custom-call | tf_op jit(solution)/shard_map/pallas_call | solution.py:220
  11.3 2.1 %collective-permute-start.3 = (f32[3,3,64,128]{3,2,1,0:T(8,128)S(1)}, f32[3,3,64,128]{3,2,1,0:T(8,128)S(1)}, u32[]{:S(2)}, u32[]{:S(2)}) collective-permute-start(f32[3,3,64,128]{3,2,1,0:T(8,128)S(1)} %get-tuple-element.16), channel_id=1, source_target_pairs={{0,16},{16,0},{32,48},{48,32},{64,80},{80,64},{96,112},{112,96},{1... | collective-permute-start | bytes 884744 | tf_op jit(solution)/shard_map/ppermute | solution.py:242
  13.5 0.1 slice.90
  13.6 0.3 compare_reduce_fusion
  13.9 2.0 %shard_map.67 = f32[3,3,64,128]{3,2,1,0:T(8,128)S(1)} custom-call(s32[6,2,17]{2,1,0:T(2,128)S(1)} %pad_select_fusion.1.whole_ref, f32[6,2,17]{2,1,0:T(2,128)S(1)} %pad_select_fusion.parts_ref, f32[4,16,72,128]{3,2,1,0:T(8,128)S(1)} %get-tuple-element.15.table_ref), custom_call_target="tpu_custom_call" | custom-call | flops 10000000 | bytes 5000000 | tf_op jit(solution)/shard_map/pallas_call | solution.py:229
  15.9 0.0 copy-start.1
  15.9 0.1 fusion.1
  16.1 4.4 %collective-permute-start.6 = (f32[3,3,16,128]{3,2,1,0:T(8,128)S(1)}, f32[3,3,16,128]{3,2,1,0:T(8,128)S(1)}, u32[]{:S(2)}, u32[]{:S(2)}) collective-permute-start(f32[3,3,16,128]{3,2,1,0:T(8,128)S(1)} %get-tuple-element.27), channel_id=1, source_target_pairs={{0,96},{16,112},{32,64},{48,80},{64,32},{80,48},{96,0},{112,16},{1... | collective-permute-start | bytes 221192 | tf_op jit(solution)/shard_map/ppermute | solution.py:252
  20.5 0.4 collective-permute-start.4
  20.9 2.3 %collective-permute-done.6 = f32[3,3,16,128]{3,2,1,0:T(8,128)S(1)} collective-permute-done((f32[3,3,16,128]{3,2,1,0:T(8,128)S(1)}, f32[3,3,16,128]{3,2,1,0:T(8,128)S(1)}, u32[]{:S(2)}, u32[]{:S(2)}) %collective-permute-start.6) | collective-permute-done | bytes 73760 | tf_op jit(solution)/shard_map/ppermute | solution.py:252
  23.2 3.4 %collective-permute-done.5 = f32[3,3,16,128]{3,2,1,0:T(8,128)S(1)} collective-permute-done((f32[3,3,16,128]{3,2,1,0:T(8,128)S(1)}, f32[3,3,16,128]{3,2,1,0:T(8,128)S(1)}, u32[]{:S(2)}, u32[]{:S(2)}) %collective-permute-start.5) | collective-permute-done | bytes 73760 | tf_op jit(solution)/shard_map/ppermute | solution.py:252
  26.6 0.1 fusion.11
  26.8 4.6 %collective-permute-start.7 = (f32[3,3,16,128]{3,2,1,0:T(8,128)S(1)}, f32[3,3,16,128]{3,2,1,0:T(8,128)S(1)}, u32[]{:S(2)}, u32[]{:S(2)}) collective-permute-start(f32[3,3,16,128]{3,2,1,0:T(8,128)S(1)} %pad_maximum_fusion.1), channel_id=1, source_target_pairs={{0,224},{16,240},{32,192},{48,208},{64,160},{80,176},{96,128},{112... | collective-permute-start | bytes 221192 | tf_op jit(solution)/shard_map/ppermute | solution.py:255
  31.3 3.9 %collective-permute-done.7 = f32[3,3,16,128]{3,2,1,0:T(8,128)S(1)} collective-permute-done((f32[3,3,16,128]{3,2,1,0:T(8,128)S(1)}, f32[3,3,16,128]{3,2,1,0:T(8,128)S(1)}, u32[]{:S(2)}, u32[]{:S(2)}) %collective-permute-start.7) | collective-permute-done | bytes 73760 | tf_op jit(solution)/shard_map/ppermute | solution.py:255
  35.3 0.1 fusion.3
  35.4 0.1 collective-permute-start.10
  35.5 1.1 %collective-permute-start.9 = (f32[3,3,16,128]{3,2,1,0:T(8,128)S(1)}, f32[3,3,16,128]{3,2,1,0:T(8,128)S(1)}, u32[]{:S(2)}, u32[]{:S(2)}) collective-permute-start(f32[3,3,16,128]{3,2,1,0:T(8,128)S(1)} %pad_maximum_fusion.2), channel_id=1, source_target_pairs={{0,64},{16,80},{32,96},{48,112},{64,0},{80,16},{96,32},{112,48},{1... | collective-permute-start | bytes 221192 | tf_op jit(solution)/shard_map/ppermute | solution.py:258
  36.6 2.4 %collective-permute-start.8 = (f32[3,3,16,128]{3,2,1,0:T(8,128)S(1)}, f32[3,3,16,128]{3,2,1,0:T(8,128)S(1)}, u32[]{:S(2)}, u32[]{:S(2)}) collective-permute-start(f32[3,3,16,128]{3,2,1,0:T(8,128)S(1)} %pad_maximum_fusion.2), channel_id=1, source_target_pairs={{0,96},{16,112},{32,64},{48,80},{64,32},{80,48},{96,0},{112,16},{1... | collective-permute-start | bytes 221192 | tf_op jit(solution)/shard_map/ppermute | solution.py:258
  39.0 0.7 %collective-permute-done.9 = f32[3,3,16,128]{3,2,1,0:T(8,128)S(1)} collective-permute-done((f32[3,3,16,128]{3,2,1,0:T(8,128)S(1)}, f32[3,3,16,128]{3,2,1,0:T(8,128)S(1)}, u32[]{:S(2)}, u32[]{:S(2)}) %collective-permute-start.9) | collective-permute-done | bytes 73760 | tf_op jit(solution)/shard_map/ppermute | solution.py:258
  39.7 2.2 %collective-permute-done.8 = f32[3,3,16,128]{3,2,1,0:T(8,128)S(1)} collective-permute-done((f32[3,3,16,128]{3,2,1,0:T(8,128)S(1)}, f32[3,3,16,128]{3,2,1,0:T(8,128)S(1)}, u32[]{:S(2)}, u32[]{:S(2)}) %collective-permute-start.8) | collective-permute-done | bytes 73760 | tf_op jit(solution)/shard_map/ppermute | solution.py:258
  42.0 3.3 %collective-permute-start.11 = (f32[3,3,64,128]{3,2,1,0:T(8,128)S(1)}, f32[3,3,64,128]{3,2,1,0:T(8,128)S(1)}, u32[]{:S(2)}, u32[]{:S(2)}) collective-permute-start(f32[3,3,64,128]{3,2,1,0:T(8,128)S(1)} %maximum_select_fusion.mine_ref), channel_id=1, source_target_pairs={{0,16},{16,0},{32,48},{48,32},{64,80},{80,64},{96,112},{112,96},{1... | collective-permute-start | bytes 884744 | tf_op jit(solution)/shard_map/ppermute | solution.py:267
  45.2 1.2 %collective-permute-done.11.other_ref = f32[3,3,64,128]{3,2,1,0:T(8,128)S(1)} collective-permute-done((f32[3,3,64,128]{3,2,1,0:T(8,128)S(1)}, f32[3,3,64,128]{3,2,1,0:T(8,128)S(1)}, u32[]{:S(2)}, u32[]{:S(2)}) %collective-permute-start.11) | collective-permute-done | bytes 294944 | tf_op jit(solution)/shard_map/ppermute | solution.py:267
  46.4 1.5 %shard_map.68 = f32[6,4,64,128]{3,2,1,0:T(8,128)} custom-call(f32[3,3]{1,0:T(4,128)S(1)} %copy-done.1, f32[3,3,64,128]{3,2,1,0:T(8,128)S(1)} %maximum_select_fusion.mine_ref, f32[3,3,64,128]{3,2,1,0:T(8,128)S(1)} %collective-permute-done.11.other_ref), custom_call_target="tpu_custom_call" | custom-call | tf_op jit(solution)/shard_map/pallas_call | solution.py:260
  (17 shorter events, 0.1 us)
Async XLA Ops:
  0.0 1.0 %copy-start = (f32[16,64,128]{2,1,0:T(8,128)S(1)}, f32[16,64,128]{2,1,0:T(8,128)}, u32[]{:S(2)}) copy-start(f32[16,64,128]{2,1,0:T(8,128)} %field_ref.1) | copy-start | bytes 1572868
  1.3 7.4 %collective-permute-start = (f32[16,8,128]{2,1,0:T(8,128)S(1)}, f32[16,8,128]{2,1,0:T(8,128)S(1)}, u32[]{:S(2)}, u32[]{:S(2)}) collective-permute-start(f32[16,8,128]{2,1,0:T(8,128)S(1)} %get-tuple-element.12), channel_id=1, source_target_pairs={{0,4},{4,8},{8,12},{12,0},{1,5},{5,9},{9,13},{13,1},{2,6},{6,10},{... | collective-permute-start | bytes 196616 | tf_op jit(solution)/shard_map/ppermute | solution.py:195
  3.4 5.2 %collective-permute-start.1 = (f32[64,128]{1,0:T(8,128)S(1)}, f32[64,128]{1,0:T(8,128)S(1)}, u32[]{:S(2)}, u32[]{:S(2)}) collective-permute-start(f32[64,128]{1,0:T(8,128)S(1)} %get-tuple-element.13), channel_id=1, source_target_pairs={{0,1},{1,2},{2,3},{3,0},{4,5},{5,6},{6,7},{7,4},{8,9},{9,10},{10,1... | collective-permute-start | bytes 98312 | tf_op jit(solution)/shard_map/ppermute | solution.py:196
  4.7 4.0 %collective-permute-start.2 = (f32[8,128]{1,0:T(8,128)S(1)}, f32[8,128]{1,0:T(8,128)S(1)}, u32[]{:S(2)}, u32[]{:S(2)}) collective-permute-start(f32[8,128]{1,0:T(8,128)S(1)} %get-tuple-element.14), channel_id=1, source_target_pairs={{0,5},{1,6},{2,7},{4,9},{5,10},{6,11},{8,13},{9,14},{10,15},{12,4}... | collective-permute-start | bytes 12296 | tf_op jit(solution)/shard_map/ppermute | solution.py:197
  11.3 4.6 %collective-permute-start.3 = (f32[3,3,64,128]{3,2,1,0:T(8,128)S(1)}, f32[3,3,64,128]{3,2,1,0:T(8,128)S(1)}, u32[]{:S(2)}, u32[]{:S(2)}) collective-permute-start(f32[3,3,64,128]{3,2,1,0:T(8,128)S(1)} %get-tuple-element.16), channel_id=1, source_target_pairs={{0,16},{16,0},{32,48},{48,32},{64,80},{80,64},{96,112},{112,96},{1... | collective-permute-start | bytes 884744 | tf_op jit(solution)/shard_map/ppermute | solution.py:242
  15.9 30.5 %copy-start.1 = (f32[3,3]{1,0:T(4,128)S(1)}, f32[3,3]{1,0:T(4,128)}, u32[]{:S(2)}) copy-start(f32[3,3]{1,0:T(4,128)} %palette_ref.1) | copy-start | bytes 112
  16.1 7.1 %collective-permute-start.6 = (f32[3,3,16,128]{3,2,1,0:T(8,128)S(1)}, f32[3,3,16,128]{3,2,1,0:T(8,128)S(1)}, u32[]{:S(2)}, u32[]{:S(2)}) collective-permute-start(f32[3,3,16,128]{3,2,1,0:T(8,128)S(1)} %get-tuple-element.27), channel_id=1, source_target_pairs={{0,96},{16,112},{32,64},{48,80},{64,32},{80,48},{96,0},{112,16},{1... | collective-permute-start | bytes 221192 | tf_op jit(solution)/shard_map/ppermute | solution.py:252
  20.5 6.1 %collective-permute-start.5 = (f32[3,3,16,128]{3,2,1,0:T(8,128)S(1)}, f32[3,3,16,128]{3,2,1,0:T(8,128)S(1)}, u32[]{:S(2)}, u32[]{:S(2)}) collective-permute-start(f32[3,3,16,128]{3,2,1,0:T(8,128)S(1)} %get-tuple-element.28), channel_id=1, source_target_pairs={{0,64},{16,80},{32,96},{48,112},{64,0},{80,16},{96,32},{112,48},{1... | collective-permute-start | bytes 221192 | tf_op jit(solution)/shard_map/ppermute | solution.py:252
  20.5 6.1 %collective-permute-start.4 = (f32[3,3,16,128]{3,2,1,0:T(8,128)S(1)}, f32[3,3,16,128]{3,2,1,0:T(8,128)S(1)}, u32[]{:S(2)}, u32[]{:S(2)}) collective-permute-start(f32[3,3,16,128]{3,2,1,0:T(8,128)S(1)} %get-tuple-element.26), channel_id=1, source_target_pairs={{0,32},{16,48},{32,0},{48,16},{64,96},{80,112},{96,64},{112,80},{1... | collective-permute-start | bytes 221192 | tf_op jit(solution)/shard_map/ppermute | solution.py:252
  26.8 8.5 %collective-permute-start.7 = (f32[3,3,16,128]{3,2,1,0:T(8,128)S(1)}, f32[3,3,16,128]{3,2,1,0:T(8,128)S(1)}, u32[]{:S(2)}, u32[]{:S(2)}) collective-permute-start(f32[3,3,16,128]{3,2,1,0:T(8,128)S(1)} %pad_maximum_fusion.1), channel_id=1, source_target_pairs={{0,224},{16,240},{32,192},{48,208},{64,160},{80,176},{96,128},{112... | collective-permute-start | bytes 221192 | tf_op jit(solution)/shard_map/ppermute | solution.py:255
  35.4 3.6 %collective-permute-start.10 = (f32[3,3,16,128]{3,2,1,0:T(8,128)S(1)}, f32[3,3,16,128]{3,2,1,0:T(8,128)S(1)}, u32[]{:S(2)}, u32[]{:S(2)}) collective-permute-start(f32[3,3,16,128]{3,2,1,0:T(8,128)S(1)} %pad_maximum_fusion.2), channel_id=1, source_target_pairs={{0,32},{16,48},{32,0},{48,16},{64,96},{80,112},{96,64},{112,80},{1... | collective-permute-start | bytes 221192 | tf_op jit(solution)/shard_map/ppermute | solution.py:258
  35.5 4.3 %collective-permute-start.9 = (f32[3,3,16,128]{3,2,1,0:T(8,128)S(1)}, f32[3,3,16,128]{3,2,1,0:T(8,128)S(1)}, u32[]{:S(2)}, u32[]{:S(2)}) collective-permute-start(f32[3,3,16,128]{3,2,1,0:T(8,128)S(1)} %pad_maximum_fusion.2), channel_id=1, source_target_pairs={{0,64},{16,80},{32,96},{48,112},{64,0},{80,16},{96,32},{112,48},{1... | collective-permute-start | bytes 221192 | tf_op jit(solution)/shard_map/ppermute | solution.py:258
  36.6 5.4 %collective-permute-start.8 = (f32[3,3,16,128]{3,2,1,0:T(8,128)S(1)}, f32[3,3,16,128]{3,2,1,0:T(8,128)S(1)}, u32[]{:S(2)}, u32[]{:S(2)}) collective-permute-start(f32[3,3,16,128]{3,2,1,0:T(8,128)S(1)} %pad_maximum_fusion.2), channel_id=1, source_target_pairs={{0,96},{16,112},{32,64},{48,80},{64,32},{80,48},{96,0},{112,16},{1... | collective-permute-start | bytes 221192 | tf_op jit(solution)/shard_map/ppermute | solution.py:258
  42.0 4.5 %collective-permute-start.11 = (f32[3,3,64,128]{3,2,1,0:T(8,128)S(1)}, f32[3,3,64,128]{3,2,1,0:T(8,128)S(1)}, u32[]{:S(2)}, u32[]{:S(2)}) collective-permute-start(f32[3,3,64,128]{3,2,1,0:T(8,128)S(1)} %maximum_select_fusion.mine_ref), channel_id=1, source_target_pairs={{0,16},{16,0},{32,48},{48,32},{64,80},{80,64},{96,112},{112,96},{1... | collective-permute-start | bytes 884744 | tf_op jit(solution)/shard_map/ppermute | solution.py:267

commit v6 on v5

--- a/solution.py
+++ b/solution.py
@@ -35,36 +35,36 @@
     corner_ref[...] = packed[rows - SPILL:]
 
 
-def begin_kernel(field_ref, table_ref):
-    rows = field_ref.shape[1]
-    for g in range(field_ref.shape[0]):
+def begin_kernel(field_ref, table_ref, first_ref):
+    depth, rows, lanes = field_ref.shape
+    lane = lax.broadcasted_iota(jnp.int32, (rows, lanes), 1)
+    first = jnp.zeros((rows, lanes), jnp.float32)
+    for g in range(depth):
         own = field_ref[g]
         table_ref[0, g, pl.ds(SPILL, rows), :] = own
         table_ref[1, g, pl.ds(SPILL, rows), :] = pltpu.roll(own, 1, 1) - own
-
-
-def prepare(begun_ref, rows_ref, cols_ref, corner_ref, table_ref):
+        first = jnp.where(lane >= g * SPILL, pltpu.roll(own, g * SPILL + SPILL - 1, 1), first)
+    first_ref[...] = first
+
+
+def prepare(rows_ref, cols_ref, corner_ref, first_ref, table_ref, edge_ref):
     _, depth, tall, lanes = table_ref.shape
-    rows = tall - SPILL
     has_rows = lax.axis_index("tx") > 0
     has_cols = lax.axis_index("ty") > 0
-    first_lane = lax.broadcasted_iota(jnp.int32, (tall, lanes), 1) == 0
     beside = jnp.concatenate([jnp.where(has_rows, corner_ref[...], 0.0), cols_ref[...]], 0)
     beside = jnp.where(has_cols, beside, 0.0)
-    shifted = pltpu.roll(beside, 1, 1)
-
+    lane = lax.broadcasted_iota(jnp.int32, (SPILL, lanes), 1)
+    first = jnp.zeros((SPILL, lanes), jnp.float32)
     for g in range(depth):
-        turn = lanes - SPILL - g * SPILL
-        edge = pltpu.roll(beside, turn, 1)
-        before = pltpu.roll(shifted, turn, 1)
         above = jnp.where(has_rows, rows_ref[g], 0.0)
-        own = begun_ref[0, g, pl.ds(SPILL, rows), :]
-        step = jnp.concatenate([pltpu.roll(above, 1, 1) - above, begun_ref[1, g, pl.ds(SPILL, rows), :]], 0)
-        own = jnp.concatenate([above, own], 0)
-        table_ref[0, g] = own
-        table_ref[1, g] = jnp.where(first_lane, before - own, step)
-        table_ref[2, g] = edge
-        table_ref[3, g] = before - edge
+        table_ref[0, g, pl.ds(0, SPILL), :] = above
+        table_ref[1, g, pl.ds(0, SPILL), :] = pltpu.roll(above, 1, 1) - above
+        first = jnp.where(lane >= g * SPILL, pltpu.roll(above, g * SPILL + SPILL - 1, 1), first)
+    first = jnp.concatenate([first, first_ref[...]], 0)
+    lane = lax.broadcasted_iota(jnp.int32, (tall, lanes), 1)
+    edge = jnp.where(lane % SPILL == SPILL - 1, first, pltpu.roll(beside, lanes - 1, 1))
+    edge_ref[0] = edge
+    edge_ref[1] = beside - edge
 
 
 def spot():
@@ -74,10 +74,11 @@
     return core, z, lax.rem(rank, 2), lax.div(rank, 2)
 
 
-def render(whole_ref, parts_ref, table_ref, out_ref, base, mixed_refs):
+def render(whole_ref, parts_ref, table_ref, edge_ref, out_ref, base, strip_ref, mixed_refs):
     _, depth, tall, lanes = table_ref.shape
     rows = tall - SPILL
     lane = lax.broadcasted_iota(jnp.int32, (tall, lanes), 1)
+    group = lax.broadcasted_iota(jnp.int32, (SPILL, lanes), 1) // SPILL
 
     def view(k, carry):
         v = base + k
@@ -85,14 +86,19 @@
         absorb = parts_ref[v, 0, depth]
         through = jnp.ones((rows, lanes), jnp.float32)
         first = second = jnp.zeros((rows, lanes), jnp.float32)
+        weights = jnp.zeros((SPILL, lanes), jnp.float32)
+        for g in range(depth):
+            weights = jnp.where(group == g, parts_ref[v, 1, g], weights)
+        weights = jnp.concatenate([weights] * (tall // SPILL), 0)
+        strip_ref[...] = edge_ref[0] + weights * edge_ref[1]
 
         def columns(i):
             g = jnp.where(flipped, depth - 1 - i, i)
             offset, weight = whole_ref[v, 1, g], parts_ref[v, 1, g]
-            outside = lane >= lanes - offset
-            own = jnp.where(outside, table_ref[2, g], table_ref[0, g])
-            step = jnp.where(outside, table_ref[3, g], table_ref[1, g])
-            mixed_refs[i % len(mixed_refs)][...] = pltpu.roll(own + weight * step, offset, 1)
+            mixed = pltpu.roll(table_ref[0, g] + weight * table_ref[1, g], offset, 1)
+            strip = pltpu.roll(strip_ref[...], lax.rem(lanes + 1 - SPILL - g * SPILL + offset, lanes), 1)
+            mixed_refs[i % len(mixed_refs)][...] = mixed
+            pltpu.store(mixed_refs[i % len(mixed_refs)], strip, mask=lane <= offset)
 
         def tile_of(i):
             g = jnp.where(flipped, depth - 1 - i, i)
@@ -120,13 +126,17 @@
     lax.fori_loop(0, HALF, view, 0)
 
 
-def give_kernel(whole_ref, parts_ref, begun_ref, rows_ref, cols_ref, corner_ref, out_ref, table_ref, *mixed_refs):
-    prepare(begun_ref, rows_ref, cols_ref, corner_ref, table_ref)
-    render(whole_ref, parts_ref, table_ref, out_ref, (1 - spot()[0]) * HALF, mixed_refs)
-
-
-def keep_kernel(whole_ref, parts_ref, table_ref, out_ref, *mixed_refs):
-    render(whole_ref, parts_ref, table_ref, out_ref, spot()[0] * HALF, mixed_refs)
+def give_kernel(
+    whole_ref, parts_ref, begun_ref, first_ref, rows_ref, cols_ref, corner_ref,
+    out_ref, table_ref, edge_ref, strip_ref, *mixed_refs,
+):
+    prepare(rows_ref, cols_ref, corner_ref, first_ref, table_ref, edge_ref)
+    base = (1 - spot()[0]) * HALF
+    render(whole_ref, parts_ref, table_ref, edge_ref, out_ref, base, strip_ref, mixed_refs)
+
+
+def keep_kernel(whole_ref, parts_ref, table_ref, edge_ref, out_ref, strip_ref, *mixed_refs):
+    render(whole_ref, parts_ref, table_ref, edge_ref, out_ref, spot()[0] * HALF, strip_ref, mixed_refs)
 
 
 def paint_kernel(palette_ref, mine_ref, other_ref, image_ref, canvas_ref, sems):
@@ -199,11 +209,11 @@
     def array(*shape):
         return jax.ShapeDtypeStruct(shape, jnp.float32)
 
-    begun = pl.pallas_call(
+    begun, first = pl.pallas_call(
         begin_kernel,
-        out_shape=array(4, depth, rows + SPILL, lanes),
+        out_shape=(array(2, depth, rows + SPILL, lanes), array(rows, lanes)),
         in_specs=[vmem()],
-        out_specs=vmem(),
+        out_specs=(vmem(),) * 2,
         compiler_params=small,
         cost_estimate=pl.CostEstimate(flops=1000000, bytes_accessed=2000000, transcendentals=0),
     )(held)
@@ -216,25 +226,26 @@
 
     tables = (with_last(shear, order), with_last(fraction, absorb))
     part = array(HALF, 3, rows, lanes)
-    scratch = [pltpu.VMEM((rows + SPILL, lanes), jnp.float32)] * 4
-    give, table = pl.pallas_call(
+    rendering = pltpu.CompilerParams(vmem_limit_bytes=4 << 20)
+    scratch = [pltpu.VMEM((rows + SPILL, lanes), jnp.float32)] * 5
+    give, table, edge = pl.pallas_call(
         give_kernel,
-        out_shape=(part, array(4, depth, rows + SPILL, lanes)),
-        in_specs=[smem()] * 2 + [vmem()] * 4,
-        out_specs=(vmem(),) * 2,
+        out_shape=(part, array(2, depth, rows + SPILL, lanes), array(2, rows + SPILL, lanes)),
+        in_specs=[smem()] * 2 + [vmem()] * 5,
+        out_specs=(vmem(),) * 3,
         scratch_shapes=scratch,
         input_output_aliases={2: 1},
-        compiler_params=small,
-    )(*tables, begun, row_halo, col_halo, corner)
+        compiler_params=rendering,
+    )(*tables, begun, first, row_halo, col_halo, corner)
     keep = pl.pallas_call(
         keep_kernel,
         out_shape=part,
-        in_specs=[smem()] * 2 + [vmem()],
+        in_specs=[smem()] * 2 + [vmem()] * 2,
         out_specs=vmem(),
         scratch_shapes=scratch,
-        compiler_params=small,
+        compiler_params=rendering,
         cost_estimate=pl.CostEstimate(flops=10000000, bytes_accessed=5000000, transcendentals=0),
-    )(*tables, table)
+    )(*tables, table, edge)
 
     core, z, odd, half = spot()
     forward = lax.dynamic_slice_in_dim(tables[0][:, 0, depth], core * HALF, HALF) == 0

time: 48.2 us -> 47.8 us (level)
  no operation moved by 1% of the time
where the time goes in v6:
time: 47.8 us; the launch traced here: 47.6 us
  starting transfers between devices  23.9 us (50%)
  waiting for transfers between devices  13.8 us (29%)
  Pallas kernels  6.45 us (13%)
  other arithmetic  2.24 us (5%)
  local copies, waits for them, and re-layouts  1.15 us (2%)
    ppermute x3, waiting for transfers between devices, shards(): came.append(lax.ppermute(quarter(step), 'depth', within[step]))  5.7 us
    ppermute x3, starting transfers between devices, shards(): came.append(lax.ppermute(quarter(step), 'depth', within[step]))  4.81 us
    ppermute x1, starting transfers between devices, shards(): lax.ppermute(value, 'depth', along_z(lambda z: 7 - z))  4.58 us
    ppermute x1, waiting for transfers between devices, shards(): lax.ppermute(value, 'depth', along_z(lambda z: 7 - z))  3.92 us
    ppermute x3, starting transfers between devices, shards(): came.append(lax.ppermute(value, 'depth', within[step]))  3.62 us
    ppermute x1, starting transfers between devices, shards(): lax.ppermute(mine, 'depth', cores)  3.25 us
    ppermute x3, waiting for transfers between devices, shards(): came.append(lax.ppermute(value, 'depth', within[step]))  2.92 us
    pallas_call x1, Pallas kernels, shards(): pl.pallas_call(give_kernel, out_shape=(part, array(2, depth, rows + SPILL...  2.25 us
  transfers between devices with their start and end apart: 12, of which 6 were waited for; matrix products, arithmetic and copies ran while one was open for 4% of the time, Pallas kernels for 5%

profile of v6, /device:TPU:1, one launch (start us, length us, event | category | flops | bytes accessed | tf_op | source)
XLA Modules:
  0.0 47.6 jit_solution(6270184673833286490)
XLA Ops:
  0.0 1.0 %copy-done = f32[16,64,128]{2,1,0:T(8,128)S(1)} copy-done((f32[16,64,128]{2,1,0:T(8,128)S(1)}, f32[16,64,128]{2,1,0:T(8,128)}, u32[]{:S(2)}) %copy-start) | copy-done | bytes 524312
  1.0 0.2 shard_map.64
  1.3 2.2 %collective-permute-start = (f32[16,8,128]{2,1,0:T(8,128)S(1)}, f32[16,8,128]{2,1,0:T(8,128)S(1)}, u32[]{:S(2)}, u32[]{:S(2)}) collective-permute-start(f32[16,8,128]{2,1,0:T(8,128)S(1)} %get-tuple-element.17), channel_id=1, source_target_pairs={{0,4},{4,8},{8,12},{12,0},{1,5},{5,9},{9,13},{13,1},{2,6},{6,10},{... | collective-permute-start | bytes 196616 | tf_op jit(solution)/shard_map/ppermute | solution.py:205
  3.4 1.2 %collective-permute-start.1 = (f32[64,128]{1,0:T(8,128)S(1)}, f32[64,128]{1,0:T(8,128)S(1)}, u32[]{:S(2)}, u32[]{:S(2)}) collective-permute-start(f32[64,128]{1,0:T(8,128)S(1)} %get-tuple-element.18), channel_id=1, source_target_pairs={{0,1},{1,2},{2,3},{3,0},{4,5},{5,6},{6,7},{7,4},{8,9},{9,10},{10,1... | collective-permute-start | bytes 98312 | tf_op jit(solution)/shard_map/ppermute | solution.py:206
  4.7 2.2 %collective-permute-start.2 = (f32[8,128]{1,0:T(8,128)S(1)}, f32[8,128]{1,0:T(8,128)S(1)}, u32[]{:S(2)}, u32[]{:S(2)}) collective-permute-start(f32[8,128]{1,0:T(8,128)S(1)} %get-tuple-element.19), channel_id=1, source_target_pairs={{0,5},{1,6},{2,7},{4,9},{5,10},{6,11},{8,13},{9,14},{10,15},{12,4}... | collective-permute-start | bytes 12296 | tf_op jit(solution)/shard_map/ppermute | solution.py:207
  6.9 0.8 %pad_select_fusion.1.whole_ref = s32[6,2,17]{2,1,0:T(2,128)S(1)} fusion(s32[6,2,16]{2,1,0:T(2,128)} %bitcast.2, pred[17]{0:T(512)(128)(4,1)S(1)} %iota_compare_fusion, s32[6]{0:T(128)} %param.11), kind=kLoop, calls=%fused_computation.45 | loop fusion | flops 204 | bytes 1625 | tf_op jit(solution)/shard_map/jit(_where)/select_n | solution.py:225
  7.7 0.8 %pad_select_fusion.parts_ref = f32[6,2,17]{2,1,0:T(2,128)S(1)} fusion(f32[6,2,16]{2,1,0:T(2,128)} %bitcast.3, pred[17]{0:T(512)(128)(4,1)S(1)} %iota_compare_fusion, f32[6]{0:T(128)} %param.9), kind=kLoop, calls=%fused_computation.44 | loop fusion | flops 204 | bytes 1625 | tf_op jit(solution)/shard_map/jit(_where)/select_n | solution.py:225
  8.4 0.3 shard_map.65
  8.8 0.0 collective-permute-done.2.corner_ref
  8.8 2.3 %shard_map.66 = (f32[3,3,64,128]{3,2,1,0:T(8,128)S(1)}, f32[2,16,72,128]{3,2,1,0:T(8,128)S(1)}, f32[2,72,128]{2,1,0:T(8,128)S(1)}) custom-call(s32[6,2,17]{2,1,0:T(2,128)S(1)} %pad_select_fusion.1.whole_ref, f32[6,2,17]{2,1,0:T(2,128)S(1)} %pad_select_fusion.parts_ref, ...), custom_call_target="tpu_custom_call", output_to_operand_aliasing={{1}: (2, {})} | custom-call | tf_op jit(solution)/shard_map/pallas_call | solution.py:231
  11.1 2.0 %collective-permute-start.3 = (f32[3,3,64,128]{3,2,1,0:T(8,128)S(1)}, f32[3,3,64,128]{3,2,1,0:T(8,128)S(1)}, u32[]{:S(2)}, u32[]{:S(2)}) collective-permute-start(f32[3,3,64,128]{3,2,1,0:T(8,128)S(1)} %get-tuple-element.22), channel_id=1, source_target_pairs={{0,16},{16,0},{32,48},{48,32},{64,80},{80,64},{96,112},{112,96},{1... | collective-permute-start | bytes 884744 | tf_op jit(solution)/shard_map/ppermute | solution.py:253
  13.1 0.1 slice.90
  13.1 0.3 compare_reduce_fusion
  13.5 2.2 %shard_map.67 = f32[3,3,64,128]{3,2,1,0:T(8,128)S(1)} custom-call(s32[6,2,17]{2,1,0:T(2,128)S(1)} %pad_select_fusion.1.whole_ref, f32[6,2,17]{2,1,0:T(2,128)S(1)} %pad_select_fusion.parts_ref, f32[2,16,72,128]{3,2,1,0:T(8,128)S(1)} %get-tuple-element.20.table_ref, f32[2,72,128]{2,1,0:T(8,128)S(1)} %get-tuple-element.21.edge_ref), custom_call_target="tpu_custom_call" | custom-call | flops 10000000 | bytes 5000000 | tf_op jit(solution)/shard_map/pallas_call | solution.py:240
  15.6 0.1 fusion.1
  15.8 0.0 copy-start.1
  15.8 4.4 %collective-permute-start.6 = (f32[3,3,16,128]{3,2,1,0:T(8,128)S(1)}, f32[3,3,16,128]{3,2,1,0:T(8,128)S(1)}, u32[]{:S(2)}, u32[]{:S(2)}) collective-permute-start(f32[3,3,16,128]{3,2,1,0:T(8,128)S(1)} %get-tuple-element.33), channel_id=1, source_target_pairs={{0,96},{16,112},{32,64},{48,80},{64,32},{80,48},{96,0},{112,16},{1... | collective-permute-start | bytes 221192 | tf_op jit(solution)/shard_map/ppermute | solution.py:263
  20.2 0.4 collective-permute-start.4
  20.6 2.3 %collective-permute-done.6 = f32[3,3,16,128]{3,2,1,0:T(8,128)S(1)} collective-permute-done((f32[3,3,16,128]{3,2,1,0:T(8,128)S(1)}, f32[3,3,16,128]{3,2,1,0:T(8,128)S(1)}, u32[]{:S(2)}, u32[]{:S(2)}) %collective-permute-start.6) | collective-permute-done | bytes 73760 | tf_op jit(solution)/shard_map/ppermute | solution.py:263
  22.9 3.4 %collective-permute-done.5 = f32[3,3,16,128]{3,2,1,0:T(8,128)S(1)} collective-permute-done((f32[3,3,16,128]{3,2,1,0:T(8,128)S(1)}, f32[3,3,16,128]{3,2,1,0:T(8,128)S(1)}, u32[]{:S(2)}, u32[]{:S(2)}) %collective-permute-start.5) | collective-permute-done | bytes 73760 | tf_op jit(solution)/shard_map/ppermute | solution.py:263
  26.3 0.1 fusion.11
  26.5 4.6 %collective-permute-start.7 = (f32[3,3,16,128]{3,2,1,0:T(8,128)S(1)}, f32[3,3,16,128]{3,2,1,0:T(8,128)S(1)}, u32[]{:S(2)}, u32[]{:S(2)}) collective-permute-start(f32[3,3,16,128]{3,2,1,0:T(8,128)S(1)} %pad_maximum_fusion.1), channel_id=1, source_target_pairs={{0,224},{16,240},{32,192},{48,208},{64,160},{80,176},{96,128},{112... | collective-permute-start | bytes 221192 | tf_op jit(solution)/shard_map/ppermute | solution.py:266
  31.0 3.9 %collective-permute-done.7 = f32[3,3,16,128]{3,2,1,0:T(8,128)S(1)} collective-permute-done((f32[3,3,16,128]{3,2,1,0:T(8,128)S(1)}, f32[3,3,16,128]{3,2,1,0:T(8,128)S(1)}, u32[]{:S(2)}, u32[]{:S(2)}) %collective-permute-start.7) | collective-permute-done | bytes 73760 | tf_op jit(solution)/shard_map/ppermute | solution.py:266
  35.0 0.1 fusion.3
  35.1 0.1 collective-permute-start.10
  35.2 1.1 %collective-permute-start.9 = (f32[3,3,16,128]{3,2,1,0:T(8,128)S(1)}, f32[3,3,16,128]{3,2,1,0:T(8,128)S(1)}, u32[]{:S(2)}, u32[]{:S(2)}) collective-permute-start(f32[3,3,16,128]{3,2,1,0:T(8,128)S(1)} %pad_maximum_fusion.2), channel_id=1, source_target_pairs={{0,64},{16,80},{32,96},{48,112},{64,0},{80,16},{96,32},{112,48},{1... | collective-permute-start | bytes 221192 | tf_op jit(solution)/shard_map/ppermute | solution.py:269
  36.3 2.4 %collective-permute-start.8 = (f32[3,3,16,128]{3,2,1,0:T(8,128)S(1)}, f32[3,3,16,128]{3,2,1,0:T(8,128)S(1)}, u32[]{:S(2)}, u32[]{:S(2)}) collective-permute-start(f32[3,3,16,128]{3,2,1,0:T(8,128)S(1)} %pad_maximum_fusion.2), channel_id=1, source_target_pairs={{0,96},{16,112},{32,64},{48,80},{64,32},{80,48},{96,0},{112,16},{1... | collective-permute-start | bytes 221192 | tf_op jit(solution)/shard_map/ppermute | solution.py:269
  38.7 0.7 %collective-permute-done.9 = f32[3,3,16,128]{3,2,1,0:T(8,128)S(1)} collective-permute-done((f32[3,3,16,128]{3,2,1,0:T(8,128)S(1)}, f32[3,3,16,128]{3,2,1,0:T(8,128)S(1)}, u32[]{:S(2)}, u32[]{:S(2)}) %collective-permute-start.9) | collective-permute-done | bytes 73760 | tf_op jit(solution)/shard_map/ppermute | solution.py:269
  39.4 2.2 %collective-permute-done.8 = f32[3,3,16,128]{3,2,1,0:T(8,128)S(1)} collective-permute-done((f32[3,3,16,128]{3,2,1,0:T(8,128)S(1)}, f32[3,3,16,128]{3,2,1,0:T(8,128)S(1)}, u32[]{:S(2)}, u32[]{:S(2)}) %collective-permute-start.8) | collective-permute-done | bytes 73760 | tf_op jit(solution)/shard_map/ppermute | solution.py:269
  41.7 3.2 %collective-permute-start.11 = (f32[3,3,64,128]{3,2,1,0:T(8,128)S(1)}, f32[3,3,64,128]{3,2,1,0:T(8,128)S(1)}, u32[]{:S(2)}, u32[]{:S(2)}) collective-permute-start(f32[3,3,64,128]{3,2,1,0:T(8,128)S(1)} %maximum_select_fusion.mine_ref), channel_id=1, source_target_pairs={{0,16},{16,0},{32,48},{48,32},{64,80},{80,64},{96,112},{112,96},{1... | collective-permute-start | bytes 884744 | tf_op jit(solution)/shard_map/ppermute | solution.py:278
  44.9 1.2 %collective-permute-done.11.other_ref = f32[3,3,64,128]{3,2,1,0:T(8,128)S(1)} collective-permute-done((f32[3,3,64,128]{3,2,1,0:T(8,128)S(1)}, f32[3,3,64,128]{3,2,1,0:T(8,128)S(1)}, u32[]{:S(2)}, u32[]{:S(2)}) %collective-permute-start.11) | collective-permute-done | bytes 294944 | tf_op jit(solution)/shard_map/ppermute | solution.py:278
  46.1 1.5 %shard_map.68 = f32[6,4,64,128]{3,2,1,0:T(8,128)} custom-call(f32[3,3]{1,0:T(4,128)S(1)} %copy-done.1, f32[3,3,64,128]{3,2,1,0:T(8,128)S(1)} %maximum_select_fusion.mine_ref, f32[3,3,64,128]{3,2,1,0:T(8,128)S(1)} %collective-permute-done.11.other_ref), custom_call_target="tpu_custom_call" | custom-call | tf_op jit(solution)/shard_map/pallas_call | solution.py:271
  (17 shorter events, 0.1 us)
Async XLA Ops:
  0.0 1.0 %copy-start = (f32[16,64,128]{2,1,0:T(8,128)S(1)}, f32[16,64,128]{2,1,0:T(8,128)}, u32[]{:S(2)}) copy-start(f32[16,64,128]{2,1,0:T(8,128)} %field_ref.1) | copy-start | bytes 1572868
  1.3 7.5 %collective-permute-start = (f32[16,8,128]{2,1,0:T(8,128)S(1)}, f32[16,8,128]{2,1,0:T(8,128)S(1)}, u32[]{:S(2)}, u32[]{:S(2)}) collective-permute-start(f32[16,8,128]{2,1,0:T(8,128)S(1)} %get-tuple-element.17), channel_id=1, source_target_pairs={{0,4},{4,8},{8,12},{12,0},{1,5},{5,9},{9,13},{13,1},{2,6},{6,10},{... | collective-permute-start | bytes 196616 | tf_op jit(solution)/shard_map/ppermute | solution.py:205
  3.4 5.3 %collective-permute-start.1 = (f32[64,128]{1,0:T(8,128)S(1)}, f32[64,128]{1,0:T(8,128)S(1)}, u32[]{:S(2)}, u32[]{:S(2)}) collective-permute-start(f32[64,128]{1,0:T(8,128)S(1)} %get-tuple-element.18), channel_id=1, source_target_pairs={{0,1},{1,2},{2,3},{3,0},{4,5},{5,6},{6,7},{7,4},{8,9},{9,10},{10,1... | collective-permute-start | bytes 98312 | tf_op jit(solution)/shard_map/ppermute | solution.py:206
  4.7 4.1 %collective-permute-start.2 = (f32[8,128]{1,0:T(8,128)S(1)}, f32[8,128]{1,0:T(8,128)S(1)}, u32[]{:S(2)}, u32[]{:S(2)}) collective-permute-start(f32[8,128]{1,0:T(8,128)S(1)} %get-tuple-element.19), channel_id=1, source_target_pairs={{0,5},{1,6},{2,7},{4,9},{5,10},{6,11},{8,13},{9,14},{10,15},{12,4}... | collective-permute-start | bytes 12296 | tf_op jit(solution)/shard_map/ppermute | solution.py:207
  11.1 4.6 %collective-permute-start.3 = (f32[3,3,64,128]{3,2,1,0:T(8,128)S(1)}, f32[3,3,64,128]{3,2,1,0:T(8,128)S(1)}, u32[]{:S(2)}, u32[]{:S(2)}) collective-permute-start(f32[3,3,64,128]{3,2,1,0:T(8,128)S(1)} %get-tuple-element.22), channel_id=1, source_target_pairs={{0,16},{16,0},{32,48},{48,32},{64,80},{80,64},{96,112},{112,96},{1... | collective-permute-start | bytes 884744 | tf_op jit(solution)/shard_map/ppermute | solution.py:253
  15.8 30.3 %copy-start.1 = (f32[3,3]{1,0:T(4,128)S(1)}, f32[3,3]{1,0:T(4,128)}, u32[]{:S(2)}) copy-start(f32[3,3]{1,0:T(4,128)} %palette_ref.1) | copy-start | bytes 112
  15.8 7.1 %collective-permute-start.6 = (f32[3,3,16,128]{3,2,1,0:T(8,128)S(1)}, f32[3,3,16,128]{3,2,1,0:T(8,128)S(1)}, u32[]{:S(2)}, u32[]{:S(2)}) collective-permute-start(f32[3,3,16,128]{3,2,1,0:T(8,128)S(1)} %get-tuple-element.33), channel_id=1, source_target_pairs={{0,96},{16,112},{32,64},{48,80},{64,32},{80,48},{96,0},{112,16},{1... | collective-permute-start | bytes 221192 | tf_op jit(solution)/shard_map/ppermute | solution.py:263
  20.2 6.1 %collective-permute-start.5 = (f32[3,3,16,128]{3,2,1,0:T(8,128)S(1)}, f32[3,3,16,128]{3,2,1,0:T(8,128)S(1)}, u32[]{:S(2)}, u32[]{:S(2)}) collective-permute-start(f32[3,3,16,128]{3,2,1,0:T(8,128)S(1)} %get-tuple-element.34), channel_id=1, source_target_pairs={{0,64},{16,80},{32,96},{48,112},{64,0},{80,16},{96,32},{112,48},{1... | collective-permute-start | bytes 221192 | tf_op jit(solution)/shard_map/ppermute | solution.py:263
  20.2 6.1 %collective-permute-start.4 = (f32[3,3,16,128]{3,2,1,0:T(8,128)S(1)}, f32[3,3,16,128]{3,2,1,0:T(8,128)S(1)}, u32[]{:S(2)}, u32[]{:S(2)}) collective-permute-start(f32[3,3,16,128]{3,2,1,0:T(8,128)S(1)} %get-tuple-element.32), channel_id=1, source_target_pairs={{0,32},{16,48},{32,0},{48,16},{64,96},{80,112},{96,64},{112,80},{1... | collective-permute-start | bytes 221192 | tf_op jit(solution)/shard_map/ppermute | solution.py:263
  26.5 8.5 %collective-permute-start.7 = (f32[3,3,16,128]{3,2,1,0:T(8,128)S(1)}, f32[3,3,16,128]{3,2,1,0:T(8,128)S(1)}, u32[]{:S(2)}, u32[]{:S(2)}) collective-permute-start(f32[3,3,16,128]{3,2,1,0:T(8,128)S(1)} %pad_maximum_fusion.1), channel_id=1, source_target_pairs={{0,224},{16,240},{32,192},{48,208},{64,160},{80,176},{96,128},{112... | collective-permute-start | bytes 221192 | tf_op jit(solution)/shard_map/ppermute | solution.py:266
  35.1 3.6 %collective-permute-start.10 = (f32[3,3,16,128]{3,2,1,0:T(8,128)S(1)}, f32[3,3,16,128]{3,2,1,0:T(8,128)S(1)}, u32[]{:S(2)}, u32[]{:S(2)}) collective-permute-start(f32[3,3,16,128]{3,2,1,0:T(8,128)S(1)} %pad_maximum_fusion.2), channel_id=1, source_target_pairs={{0,32},{16,48},{32,0},{48,16},{64,96},{80,112},{96,64},{112,80},{1... | collective-permute-start | bytes 221192 | tf_op jit(solution)/shard_map/ppermute | solution.py:269
  35.2 4.3 %collective-permute-start.9 = (f32[3,3,16,128]{3,2,1,0:T(8,128)S(1)}, f32[3,3,16,128]{3,2,1,0:T(8,128)S(1)}, u32[]{:S(2)}, u32[]{:S(2)}) collective-permute-start(f32[3,3,16,128]{3,2,1,0:T(8,128)S(1)} %pad_maximum_fusion.2), channel_id=1, source_target_pairs={{0,64},{16,80},{32,96},{48,112},{64,0},{80,16},{96,32},{112,48},{1... | collective-permute-start | bytes 221192 | tf_op jit(solution)/shard_map/ppermute | solution.py:269
  36.3 5.3 %collective-permute-start.8 = (f32[3,3,16,128]{3,2,1,0:T(8,128)S(1)}, f32[3,3,16,128]{3,2,1,0:T(8,128)S(1)}, u32[]{:S(2)}, u32[]{:S(2)}) collective-permute-start(f32[3,3,16,128]{3,2,1,0:T(8,128)S(1)} %pad_maximum_fusion.2), channel_id=1, source_target_pairs={{0,96},{16,112},{32,64},{48,80},{64,32},{80,48},{96,0},{112,16},{1... | collective-permute-start | bytes 221192 | tf_op jit(solution)/shard_map/ppermute | solution.py:269
  41.7 4.5 %collective-permute-start.11 = (f32[3,3,64,128]{3,2,1,0:T(8,128)S(1)}, f32[3,3,64,128]{3,2,1,0:T(8,128)S(1)}, u32[]{:S(2)}, u32[]{:S(2)}) collective-permute-start(f32[3,3,64,128]{3,2,1,0:T(8,128)S(1)} %maximum_select_fusion.mine_ref), channel_id=1, source_target_pairs={{0,16},{16,0},{32,48},{48,32},{64,80},{80,64},{96,112},{112,96},{1... | collective-permute-start | bytes 884744 | tf_op jit(solution)/shard_map/ppermute | solution.py:278
